TPU v7x, 32 devices: a whole 2x2x4 slice. The times are simulated.
32 devices in a mesh: members: 2 (over x), lon: 8 (over z, y), lat: 2 (over core).
Axes of the slice: x: 2, y: 2, z: 4, core: 2. Of those that a mesh axis runs over, the one named last changes fastest.
Arguments:
- ocean_state: bfloat16 [200, 128, 1024], P(None, ('members', 'lat'), 'lon'), parts along dimension 1
- cotangent: bfloat16 [200, 128, 1024], P(None, ('members', 'lat'), 'lon'), parts along dimension 1
- kernel: float32 [200, 49], replicated, may hold values from -0.875 to 0.875
- norm_gain: float32 [200], replicated, may hold values from 0.1 to 1.9
- expand_weight: bfloat16 [200, 800], replicated, may hold values from -0.4375 to 0.4375
- reduce_weight: bfloat16 [800, 200], replicated, may hold values from -0.21875 to 0.21875
- layer_scale: float32 [200], replicated, may hold values from 0.5 to 1.5
- land_mask: int32 [64, 1024], P('lat', 'lon'), may hold values 0 or 1
Outputs:
- block_out: bfloat16 [200, 128, 1024], P(None, ('members', 'lat'), 'lon'), parts along dimension 1
- state_grad: bfloat16 [200, 128, 1024], P(None, ('members', 'lat'), 'lon'), parts along dimension 1
- kernel_grad: float32 [400, 49], P('members'), parts along dimension 0
- gain_grad: float32 [400], P('members'), parts along dimension 0
- expand_grad: float32 [400, 800], P('members'), parts along dimension 0
- reduce_grad: float32 [1600, 200], P('members'), parts along dimension 0
- scale_grad: float32 [400], P('members'), parts along dimension 0
There are 2 independent parts, one for each index of `members`. A program takes and returns all parts, laid end to end along the dimension named above; an argument that names none is the same for every part. Nothing has to cross between parts.
All inputs are finite; a program needn't handle non-finite values. No bound on the sum of `land_mask` on one device may be relied on, other than what follows from the above.
Results may differ from a plain program's by a relative error of at most 0.0065.
Values may be sent and summed in bfloat16 or wider, within the bound.
No kernel may reach another device: no remote copies, remote signals or barrier semaphores. Data moves between devices by JAX's collectives and lax.ppermute only.
A program may use at most 448 MiB of HBM per device.

v0:
```python
import jax
import jax.numpy as jnp
from jax import lax
from jax.sharding import PartitionSpec as P

KS = 7


def extended_2(cells, sides, width, closed):
    for axis, dim in sides:
        count = lax.axis_size(axis)
        ends = count if closed else count - 1
        head = lax.slice_in_dim(cells, 0, width, axis=dim)
        tail = lax.slice_in_dim(cells, cells.shape[dim] - width, cells.shape[dim], axis=dim)
        cells = jnp.concatenate(
            [
                lax.ppermute(tail, axis, [(i, (i + 1) % count) for i in range(ends)]),
                cells,
                lax.ppermute(head, axis, [((i + 1) % count, i) for i in range(ends)]),
            ],
            axis=dim,
        )
    return cells


def swapped(x, axis, apart):
    return lax.ppermute(x, axis, [(i, i ^ 1 << apart) for i in range(lax.axis_size(axis))])


def from_behind(block, axis, distance):
    devices = range(lax.axis_size(axis))
    route = [((i - distance) % len(devices), i) for i in devices]
    return lax.ppermute(block, axis, route)


def shifted(value, axis, steps):
    count = lax.axis_size(axis)
    initial, last = (max(0, -steps), min(count, count - steps))
    return lax.ppermute(value, axis, [(source, source + steps) for source in range(initial, last)])


def gelu(value):
    return jax.nn.gelu(value, approximate=True)


def on_device(
    ocean_state, cotangent, kernel, norm_gain, expand_weight, reduce_weight, layer_scale, land_mask
):
    channels, row_count, col_count = ocean_state.shape
    reach = KS // 2
    lon_devices = lax.axis_size("lon")
    bit_count = lon_devices.bit_length() - 1
    is_north = lax.axis_index("lat") == lax.axis_size("lat") - 1
    wide = extended_2(ocean_state, (("lon", 2),), reach, True)
    tall = extended_2(wide, (("lat", 1),), reach, False)
    partner_rows = wide[:, row_count - reach :][:, ::-1]
    for bit in range(bit_count):
        partner_rows = swapped(partner_rows, "lon", bit)
    across = partner_rows[:, :, ::-1]
    upper = jnp.where(is_north, across, tall[:, row_count + reach :])
    extended = jnp.concatenate([tall[:, : row_count + reach], upper], axis=1).astype(jnp.float32)
    convolved = jnp.zeros((channels, row_count, col_count), jnp.float32)
    for row_shift in range(KS):
        for col_shift in range(KS):
            tap_weight = kernel[:, row_shift * KS + col_shift][:, None, None]
            convolved = (
                convolved
                + tap_weight
                * extended[:, row_shift : row_shift + row_count, col_shift : col_shift + col_count]
            )
    average = jnp.mean(convolved, axis=0)
    centred = convolved - average
    variance = jnp.mean(centred * centred, axis=0)
    inverse = lax.rsqrt(variance + 1e-06)
    normalized = centred * inverse
    normed = (normalized * norm_gain[:, None, None]).astype(jnp.bfloat16)
    cells = row_count * col_count
    flattened = normed.reshape(channels, cells)
    hidden = jnp.einsum("cf,ct->ft", expand_weight, flattened, preferred_element_type=jnp.float32)
    activated = gelu(hidden).astype(jnp.bfloat16)
    mixed = jnp.einsum("fc,ft->ct", reduce_weight, activated, preferred_element_type=jnp.float32)
    wet_cells = land_mask.astype(jnp.float32).reshape(1, cells)
    statef = ocean_state.astype(jnp.float32).reshape(channels, cells)
    block_out = (
        (statef + wet_cells * layer_scale[:, None] * mixed)
        .astype(jnp.bfloat16)
        .reshape(channels, row_count, col_count)
    )
    branch_grad = cotangent.astype(jnp.float32).reshape(channels, cells) * wet_cells
    scale_part = jnp.sum(branch_grad * mixed, axis=1)
    mixed_grad = (layer_scale[:, None] * branch_grad).astype(jnp.bfloat16)
    reduce_part = jnp.einsum("ft,ct->fc", activated, mixed_grad, preferred_element_type=jnp.float32)
    act_grad = jnp.einsum(
        "fc,ct->ft", reduce_weight, mixed_grad, preferred_element_type=jnp.float32
    )
    pullback = jax.vjp(gelu, hidden)[1]
    hidden_grad = pullback(act_grad)[0].astype(jnp.bfloat16)
    expand_part = jnp.einsum(
        "ct,ft->cf", flattened, hidden_grad, preferred_element_type=jnp.float32
    )
    normed_grad = jnp.einsum(
        "cf,ft->ct", expand_weight, hidden_grad, preferred_element_type=jnp.float32
    ).reshape(channels, row_count, col_count)
    gain_part = jnp.sum(normed_grad * normalized, axis=(1, 2))
    unit_grad = normed_grad * norm_gain[:, None, None]
    conv_grad = (
        inverse
        * (
            unit_grad
            - jnp.mean(unit_grad, axis=0)
            - normalized * jnp.mean(unit_grad * normalized, axis=0)
        )
    ).astype(jnp.bfloat16)
    conv_wide = conv_grad.astype(jnp.float32)
    kernel_terms = []
    for row_shift in range(KS):
        for col_shift in range(KS):
            window = extended[
                :, row_shift : row_shift + row_count, col_shift : col_shift + col_count
            ]
            kernel_terms.append(jnp.sum(conv_wide * window, axis=(1, 2)))
    kernel_part = jnp.stack(kernel_terms, axis=1)
    kernel_grad, gain_grad, expand_grad, reduce_grad, scale_grad = lax.psum(
        (kernel_part, gain_part, expand_part, reduce_part, scale_part), ("lon", "lat")
    )
    padded_grad = jnp.zeros((channels, row_count + 2 * reach, col_count + 2 * reach), jnp.float32)
    for row_shift in range(KS):
        for col_shift in range(KS):
            tap_weight = kernel[:, row_shift * KS + col_shift][:, None, None]
            padded_grad = padded_grad + jnp.pad(
                tap_weight * conv_wide,
                ((0, 0), (row_shift, 2 * reach - row_shift), (col_shift, 2 * reach - col_shift)),
            )
    from_east = from_behind(padded_grad[:, :, :reach].astype(jnp.bfloat16), "lon", -1).astype(
        jnp.float32
    )
    from_west = from_behind(
        padded_grad[:, :, col_count + reach :].astype(jnp.bfloat16), "lon", 1
    ).astype(jnp.float32)
    column_core = padded_grad[:, :, reach : col_count + reach]
    column_core = column_core.at[:, :, :reach].add(from_west)
    column_core = column_core.at[:, :, col_count - reach :].add(from_east)
    from_above = shifted(column_core[:, :reach].astype(jnp.bfloat16), "lat", -1).astype(jnp.float32)
    from_below = shifted(column_core[:, row_count + reach :].astype(jnp.bfloat16), "lat", 1).astype(
        jnp.float32
    )
    inner = column_core[:, reach : row_count + reach]
    inner = inner.at[:, :reach].add(from_below)
    inner = inner.at[:, row_count - reach :].add(from_above)
    returned = jnp.where(is_north, column_core[:, row_count + reach :], 0.0)
    for bit in range(bit_count):
        returned = swapped(returned.astype(jnp.bfloat16), "lon", bit).astype(returned.dtype)
    mirrored = returned[:, ::-1, ::-1]
    inner = inner.at[:, row_count - reach :].add(jnp.where(is_north, mirrored, 0.0))
    state_grad = (cotangent.astype(jnp.float32) + inner).astype(jnp.bfloat16)
    return (block_out, state_grad, kernel_grad, gain_grad, expand_grad, reduce_grad, scale_grad)


def solution(mesh):
    return jax.shard_map(
        on_device,
        mesh=mesh,
        in_specs=(
            P(None, ("members", "lat"), "lon"),
            P(None, ("members", "lat"), "lon"),
            P(),
            P(),
            P(),
            P(),
            P(),
            P("lat", "lon"),
        ),
        out_specs=(
            P(None, ("members", "lat"), "lon"),
            P(None, ("members", "lat"), "lon"),
            P("members", None),
            P("members"),
            P("members", None),
            P("members", None),
            P("members"),
        ),
        check_vma=False,
    )
```

profile of v0, /device:TPU:1, one launch (start us, length us, event | category | flops | bytes accessed | tf_op | source)
XLA Modules:
  0.0 529.9 jit_solution(17611095558817879342)
XLA Ops:
  7.2 4.5 fusion.68
  14.5 5.2 collective-permute-start.1
  38.0 5.0 collective-permute-done.3
  43.7 4.5 collective-permute-start.6
  54.0 7.4 %collective-permute-done.5 = bf16[200,3,134]{0,2,1:T(8,128)(2,1)S(1)} collective-permute-done((bf16[200,3,134]{0,2,1:T(8,128)(2,1)S(1)}, bf16[200,3,134]{0,2,1:T(8,128)(2,1)S(1)}, u32[]{:S(2)}, u32[]{:S(2)}) %collective-permute-start.5) | collective-permute-done | bytes 160832 | tf_op jit(solution)/shard_map/ppermute | solution.py:27
  66.9 91.6 %fusion.66 = (f32[32,128]{1,0:T(8,128)S(1)}, f32[200,32,128]{0,2,1:T(8,128)}) fusion(f32[200,38,134]{0,2,1:T(8,128)} %maximum_convert_fusion, f32[200]{0:T(256)S(1)} %bitcast.216, f32[200]{0:T(256)S(1)} %bitcast.266, f32[200]{0:T(256)S(1)} %bitcast.242, f32[200]{0:T(256)S(1)} %bitcast.244, f32[200]{0:T(256)S(1)} %bitcast.246, f32[200]{0:T(256)S(1)} %bitcast.248, ...), kind=kLoop, calls=%fused_computation.202 | loop fusion | flops 80277504 | bytes 163895584 | tf_op jit(solution)/shard_map/reduce_sum | solution.py:71
  163.3 6.4 %fusion.10 = (bf16[800,4096]{1,0:T(8,128)(2,1)}, f32[4096,800]{0,1:T(8,128)S(1)}) fusion(bf16[200,4096]{0,1:T(8,128)(2,1)S(1)} %bitcast.167, bf16[200,800]{1,0:T(8,128)(2,1)S(1)} %copy-done), kind=kOutput, calls=%fused_computation.113 | convolution fusion | flops 1340211200 | bytes 21619200 | tf_op jit(solution)/shard_map/cf,ct->ft/dot_general | solution.py:79
  169.7 10.1 %fusion.6 = bf16[800,4096]{1,0:T(8,128)(2,1)S(1)} fusion(f32[4096,800]{0,1:T(8,128)S(1)} %get-tuple-element.245, bf16[800,200]{0,1:T(8,128)(2,1)S(1)} %copy-done.111, f32[200,4096]{1,0:T(8,128)S(1)} %copy-done.9, f32[200]{0:T(256)S(1)} %copy-done.113, f32[4096]{0:T(1024)S(1)} %convert_bitcast_fusion), kind=kOutput, calls=%fused_computation.106 | convolution fusion | flops 1378713600 | bytes 23274784 | tf_op jit(solution)/shard_map/fc,ct->ft/dot_general | solution.py:93
  183.6 5.2 copy.30
  188.8 6.5 %multiply_reduce_fusion = (f32[200]{0:T(256)}, f32[32,128]{1,0:T(8,128)S(1)}) fusion(f32[200,32,128]{0,2,1:T(8,128)} %get-tuple-element.134, f32[32,128]{1,0:T(8,128)S(1)} %add_rsqrt_fusion, f32[32,128]{1,0:T(8,128)S(1)} %broadcast_multiply_fusion.1, f32[200,4096]{0,1:T(8,128)} %copy.30, f32[200,32,128]{0,2,1:T(8,128)} %bitcast.164, f32[200]{0:T(256)S(1)} %copy-done.17), kind=kLoop, calls=%fused_computation.166 | loop fusion | flops 5730104 | bytes 9881152 | tf_op jit(solution)/shard_map/reduce_sum | solution.py:104
  196.3 11.5 %fusion.57 = (f32[200]{0:T(256)}, f32[200]{0:T(256)}, f32[200]{0:T(256)}, f32[200]{0:T(256)}, f32[200]{0:T(256)}, /*index=5*/f32[200]{0:T(256)}, f32[200]{0:T(25...) fusion(f32[200,38,134]{0,2,1:T(8,128)S(1)} %bitcast.163, ...), kind=kLoop, calls=%fused_computation.163 | loop fusion | flops 28669400 | bytes 50867136 | tf_op jit(solution)/shard_map/reduce_sum | solution.py:121
  207.7 13.8 %fusion.58 = (f32[200]{0:T(256)}, f32[200]{0:T(256)}, f32[200]{0:T(256)}, f32[200]{0:T(256)}, f32[200]{0:T(256)}, /*index=5*/f32[200]{0:T(256)}, f32[200]{0:T(25...) fusion(bf16[200,32,128]{0,2,1:T(8,128)(2,1)S(1)} %get-tuple-ele, ...), kind=kLoop, calls=%fused_computation.164 | loop fusion | flops 30306800 | bytes 60635200 | tf_op jit(solution)/shard_map/reduce_sum | solution.py:121
  221.6 13.0 %fusion.59 = (f32[200]{0:T(256)S(1)}, f32[200]{0:T(256)S(1)}, f32[200]{0:T(256)S(1)}, f32[200]{0:T(256)S(1)}, f32[200]{0:T(256)S(1)}, /*index=5*/f32[200]{0:T(25...) fusion(bf16[200,32,128]{0,2,1:T(8,128)(2,1)S(1)} %get-tuple-ele, ...), kind=kLoop, calls=%fused_computation.165 | loop fusion | flops 30306800 | bytes 60635200 | tf_op jit(solution)/shard_map/reduce_sum | solution.py:121
  234.5 17.5 %convert_multiply_fusion.62 = (f32[200,32,128]{0,2,1:T(8,128)}, f32[200,32,128]{0,2,1:T(8,128)}, f32[200,32,128]{0,2,1:T(8,128)}, f32[200,32,128]{0,2,1:T(8,128)...) fusion(bf16[200,32,128]{0,2,1:T(8,128)(2,1)S(1)} %get-tuple-ele, ...), kind=kLoop, calls=%fused_computation.62 | loop fusion | flops 11468800 | bytes 44247200 | tf_op jit(solution)/shard_map/mul | solution.py:131
  252.2 27.0 %convert_multiply_fusion.80 = (f32[200,32,128]{0,2,1:T(8,128)}, f32[200,32,128]{0,2,1:T(8,128)}, f32[200,32,128]{0,2,1:T(8,128)}, f32[200,32,128]{0,2,1:T(8,128)...) fusion(bf16[200,32,128]{0,2,1:T(8,128)(2,1)S(1)} %get-tuple-ele, ...), kind=kLoop, calls=%fused_computation.80 | loop fusion | flops 15564800 | bytes 60635200 | tf_op jit(solution)/shard_map/mul | solution.py:131
  279.4 26.8 %convert_multiply_fusion.97 = (f32[200,32,128]{0,2,1:T(8,128)}, f32[200,32,128]{0,2,1:T(8,128)}, f32[200,32,128]{0,2,1:T(8,128)}, f32[200,32,128]{0,2,1:T(8,128)...) fusion(bf16[200,32,128]{0,2,1:T(8,128)(2,1)S(1)} %get-tuple-ele, ...), kind=kLoop, calls=%fused_computation.97 | loop fusion | flops 15564800 | bytes 60635200 | tf_op jit(solution)/shard_map/mul | solution.py:131
  306.2 70.8 %fusion.65 = (bf16[200,38,134]{0,2,1:T(8,128)(2,1)}, f32[200,38,134]{0,2,1:T(8,128)S(1)}) fusion(f32[200,32,128]{0,2,1:T(8,128)} %get-tuple-element.145, f32[200,32,128]{0,2,1:T(8,128)} %get-tuple-element.192, f32[200,32,128]{0,2,1:T(8,128)} %get-tuple-element.191, f32[200,32,128]{0,2,1:T(8,128)} %get-tuple-element.190, ...), kind=kLoop, calls=%fused_computation.201 | loop fusion | flops 49901600 | bytes 166673600 | tf_op jit(solution)/shard_map/convert.3
  379.8 7.9 %multiply_reduce_fusion.3 = (f32[200]{0:T(256)S(1)}, bf16[25,8,32,128]{3,1,2,0:T(8,128)(2,1)}) fusion(f32[200,4096]{1,0:T(8,128)S(1)} %copy-done.10, f32[4096]{0:T(1024)S(1)} %copy-done.16, f32[200]{0:T(256)S(1)} %copy-done.114, f32[25,8,32,128]{3,2,1,0:T(8,128)S(1)} %copy-done.8, bf16[800,4096]{1,0:T(8,128)(2,1)} %get-tuple-element.244, ...), kind=kOutput, calls=%fused_computation.176 | convolution fusion | flops 1316454144 | bytes 15083584 | tf_op jit(solution)/shard_map/fc,ft->ct/dot_general | solution.py:81
  387.6 6.3 %fusion.64 = f32[800,200]{0,1:T(8,128)} fusion(bf16[800,4096]{1,0:T(8,128)(2,1)} %get-tuple-element.244, f32[200,4096]{1,0:T(8,128)S(1)} %copy-done.10, f32[200]{0:T(256)S(1)} %copy-done.114, f32[4096]{0:T(1024)S(1)} %copy-done.16), kind=kOutput, calls=%fused_computation.200 | convolution fusion | flops 1313177600 | bytes 10487584 | tf_op jit(solution)/shard_map/ft,ct->fc/dot_general | solution.py:92
  410.3 6.4 %fusion.72 = f32[200,800]{1,0:T(8,128)} fusion(bf16[200,4096]{0,1:T(8,128)(2,1)S(1)} %bitcast.168, bf16[800,4096]{1,0:T(8,128)(2,1)} %copy-done.115), kind=kOutput, calls=%fused_computation.208 | convolution fusion | flops 1310720000 | bytes 8832000 | tf_op jit(solution)/shard_map/ct,ft->cf/dot_general | solution.py:98
  420.5 56.2 %all-reduce.49 = (f32[200,49]{0,1:T(8,128)}, f32[200]{0:T(256)}, f32[200]{0:T(256)}) all-reduce(f32[200,49]{0,1:T(8,128)S(1)} %stack.199, f32[200]{0:T(256)S(1)} %copy-done.110, f32[200]{0:T(256)S(1)} %get-tuple-element.138), channel_id=1, replica_groups=mesh['members'=2,'lon'=8,'lat'=2] {'lon','lat'}, use_global_device_ids=true, to_apply=%region_53.54 | all-reduce | flops 10200 | bytes 81600 | tf_op jit(solution)/shard_map/psum | solution.py:123
  479.3 6.8 %collective-permute-start.10 = (bf16[200,3,128]{0,2,1:T(8,128)(2,1)S(1)}, bf16[200,3,128]{0,2,1:T(8,128)(2,1)S(1)}, u32[]{:S(2)}, u32[]{:S(2)}) collective-permute-start(bf16[200,3,128]{0,2,1:T(8,128)(2,1)S(1)} %get-tuple-element.136), channel_id=1, source_target_pairs={{1,0},{3,2},{5,4},{7,6},{9,8},{11,10},{13,12},{15,14},{17,16},{19,... | collective-permute-start | bytes 460808 | tf_op jit(solution)/shard_map/ppermute | solution.py:39
  494.6 13.6 %collective-permute-done.13 = bf16[200,3,128]{0,2,1:T(8,128)(2,1)S(1)} collective-permute-done((bf16[200,3,128]{0,2,1:T(8,128)(2,1)S(1)}, bf16[200,3,128]{0,2,1:T(8,128)(2,1)S(1)}, u32[]{:S(2)}, u32[]{:S(2)}) %collective-permute-start.13) | collective-permute-done | bytes 153632 | tf_op jit(solution)/shard_map/ppermute | solution.py:27
  510.2 4.3 add_convert_fusion
  (306 shorter events, 85.5 us)
Async XLA Ops:
  7.2 156.1 %copy-start = (bf16[200,800]{1,0:T(8,128)(2,1)S(1)}, bf16[200,800]{1,0:T(8,128)(2,1)}, u32[]{:S(2)}) copy-start(bf16[200,800]{1,0:T(8,128)(2,1)} %param.22) | copy-start | bytes 960004
  7.2 511.4 %all-reduce.53.cloned.1.call-start = ((), (), s32[]{:S(2)}) async-start(), calls=%async_computation | async-start | bytes 2867200 | tf_op jit(solution)/shard_map/psum | solution.py:123
  14.5 21.3 %collective-permute-start.1 = (bf16[200,32,3]{0,1,2:T(8,128)(2,1)S(1)}, bf16[200,32,3]{0,1,2:T(8,128)(2,1)S(1)}, u32[]{:S(2)}, u32[]{:S(2)}) collective-permute-start(bf16[200,32,3]{0,1,2:T(8,128)(2,1)S(1)} %copy.32), channel_id=1, source_target_pairs={{2,0},{4,2},{6,4},{8,6},{10,8},{12,10},{14,12},{0,14},{3,1},{5,3},... | collective-permute-start | bytes 115208 | tf_op jit(solution)/shard_map/ppermute | solution.py:19
  22.5 13.4 %collective-permute-start = (bf16[200,32,3]{0,1,2:T(8,128)(2,1)S(1)}, bf16[200,32,3]{0,1,2:T(8,128)(2,1)S(1)}, u32[]{:S(2)}, u32[]{:S(2)}) collective-permute-start(bf16[200,32,3]{0,1,2:T(8,128)(2,1)S(1)} %copy.31), channel_id=1, source_target_pairs={{0,2},{2,4},{4,6},{6,8},{8,10},{10,12},{12,14},{14,0},{1,3},{3,5},... | collective-permute-start | bytes 115208 | tf_op jit(solution)/shard_map/ppermute | solution.py:17
  22.6 147.2 %copy-start.15 = (f32[4096]{0:T(1024)}, f32[4096]{0:T(1024)S(1)}, u32[]{:S(2)}) copy-start(f32[4096]{0:T(1024)S(1)} %convert_bitcast_fusion) | copy-start | bytes 49156
  37.2 5.8 %collective-permute-start.3 = (bf16[200,3,134]{0,2,1:T(8,128)(2,1)S(1)}, bf16[200,3,134]{0,2,1:T(8,128)(2,1)S(1)}, u32[]{:S(2)}, u32[]{:S(2)}) collective-permute-start(bf16[200,3,134]{0,2,1:T(8,128)(2,1)S(1)} %rev.9), channel_id=1, source_target_pairs={{0,2},{2,0},{4,6},{6,4},{8,10},{10,8},{12,14},{14,12},{1,3},{3,1},... | collective-permute-start | bytes 482408 | tf_op jit(solution)/shard_map/ppermute | solution.py:27
  38.0 28.5 %copy-start.18 = (f32[200,1]{0,1:T(1,128)}, f32[200,1]{0,1:T(1,128)S(1)}, u32[]{:S(2)}) copy-start(f32[200,1]{0,1:T(1,128)S(1)} %get-tuple-element.195) | copy-start | bytes 2404
  43.0 5.2 collective-permute-start.4
  43.7 18.6 %collective-permute-start.6 = (bf16[200,3,134]{0,2,1:T(8,128)(2,1)S(1)}, bf16[200,3,134]{0,2,1:T(8,128)(2,1)}, u32[]{:S(2)}, u32[]{:S(2)}) collective-permute-start(bf16[200,3,134]{0,2,1:T(8,128)(2,1)S(1)} %get-tuple-element.142), channel_id=1, source_target_pairs={{1,0},{3,2},{5,4},{7,6},{9,8},{11,10},{13,12},{15,14},{17,16},{19,... | collective-permute-start | bytes 482408 | tf_op jit(solution)/shard_map/ppermute | solution.py:19
  48.2 13.2 %collective-permute-start.5 = (bf16[200,3,134]{0,2,1:T(8,128)(2,1)S(1)}, bf16[200,3,134]{0,2,1:T(8,128)(2,1)S(1)}, u32[]{:S(2)}, u32[]{:S(2)}) collective-permute-start(bf16[200,3,134]{0,2,1:T(8,128)(2,1)S(1)} %collective-permute-done.4), channel_id=1, source_target_pairs={{0,8},{2,10},{4,12},{6,14},{8,0},{10,2},{12,4},{14,6},{1,9},{3,11}... | collective-permute-start | bytes 482408 | tf_op jit(solution)/shard_map/ppermute | solution.py:27
  52.3 10.5 %collective-permute-start.2 = (bf16[200,3,134]{0,2,1:T(8,128)(2,1)S(1)}, bf16[200,3,134]{0,2,1:T(8,128)(2,1)}, u32[]{:S(2)}, u32[]{:S(2)}) collective-permute-start(bf16[200,3,134]{0,2,1:T(8,128)(2,1)S(1)} %get-tuple-element.143), channel_id=1, source_target_pairs={{0,1},{2,3},{4,5},{6,7},{8,9},{10,11},{12,13},{14,15},{16,17},{18,... | collective-permute-start | bytes 482408 | tf_op jit(solution)/shard_map/ppermute | solution.py:17
  252.0 27.2 %copy-start.21 = (f32[200,1]{0,1:T(1,128)S(1)}, f32[200,1]{0,1:T(1,128)}, u32[]{:S(2)}) copy-start(f32[200,1]{0,1:T(1,128)} %copy-done.20) | copy-start | bytes 2404
  306.2 73.6 %copy-start.8 = (f32[25,8,32,128]{3,2,1,0:T(8,128)S(1)}, f32[25,8,32,128]{3,2,1,0:T(8,128)}, u32[]{:S(2)}) copy-start(f32[25,8,32,128]{3,2,1,0:T(8,128)} %convert.11) | copy-start | bytes 9830404
  306.2 73.5 %copy-start.10 = (f32[200,4096]{1,0:T(8,128)S(1)}, f32[200,4096]{1,0:T(8,128)}, u32[]{:S(2)}) copy-start(f32[200,4096]{1,0:T(8,128)} %copy.29) | copy-start | bytes 9830404
  306.2 73.5 %copy-start.16 = (f32[4096]{0:T(1024)S(1)}, f32[4096]{0:T(1024)}, u32[]{:S(2)}) copy-start(f32[4096]{0:T(1024)} %copy-done.15) | copy-start | bytes 49156
  306.2 73.5 %copy-start.112 = (bf16[800,200]{0,1:T(8,128)(2,1)S(1)}, bf16[800,200]{0,1:T(8,128)(2,1)}, u32[]{:S(2)}) copy-start(bf16[800,200]{0,1:T(8,128)(2,1)} %param.23) | copy-start | bytes 960004
  306.2 73.5 %copy-start.114 = (f32[200]{0:T(256)S(1)}, f32[200]{0:T(256)}, u32[]{:S(2)}) copy-start(f32[200]{0:T(256)} %param.24) | copy-start | bytes 2404
  378.1 21.7 %collective-permute-start.7 = (bf16[200,38,3]{0,1,2:T(8,128)(2,1)S(1)}, bf16[200,38,3]{0,1,2:T(8,128)(2,1)S(1)}, u32[]{:S(2)}, u32[]{:S(2)}) collective-permute-start(bf16[200,38,3]{0,1,2:T(8,128)(2,1)S(1)} %copy.23), channel_id=1, source_target_pairs={{14,0},{0,2},{2,4},{4,6},{6,8},{8,10},{10,12},{12,14},{15,1},{1,3}... | collective-permute-start | bytes 136808 | tf_op jit(solution)/shard_map/ppermute | solution.py:33
  393.9 9.7 %collective-permute-start.8 = (bf16[200,38,3]{0,1,2:T(8,128)(2,1)S(1)}, bf16[200,38,3]{0,1,2:T(8,128)(2,1)S(1)}, u32[]{:S(2)}, u32[]{:S(2)}) collective-permute-start(bf16[200,38,3]{0,1,2:T(8,128)(2,1)S(1)} %copy.25), channel_id=1, source_target_pairs={{2,0},{4,2},{6,4},{8,6},{10,8},{12,10},{14,12},{0,14},{3,1},{5,3},... | collective-permute-start | bytes 136808 | tf_op jit(solution)/shard_map/ppermute | solution.py:33
  409.0 77.1 %collective-permute-start.11 = (bf16[200,3,128]{0,2,1:T(8,128)(2,1)S(1)}, bf16[200,3,128]{0,2,1:T(8,128)(2,1)S(1)}, u32[]{:S(2)}, u32[]{:S(2)}) collective-permute-start(bf16[200,3,128]{0,2,1:T(8,128)(2,1)S(1)} %get-tuple-element.135), channel_id=1, source_target_pairs={{0,2},{2,0},{4,6},{6,4},{8,10},{10,8},{12,14},{14,12},{1,3},{3,1},... | collective-permute-start | bytes 460808 | tf_op jit(solution)/shard_map/ppermute | solution.py:27
  409.0 77.1 %collective-permute-start.9 = (bf16[200,3,128]{0,2,1:T(8,128)(2,1)S(1)}, bf16[200,3,128]{0,2,1:T(8,128)(2,1)S(1)}, u32[]{:S(2)}, u32[]{:S(2)}) collective-permute-start(bf16[200,3,128]{0,2,1:T(8,128)(2,1)S(1)} %get-tuple-element.137), channel_id=1, source_target_pairs={{0,1},{2,3},{4,5},{6,7},{8,9},{10,11},{12,13},{14,15},{16,17},{18,... | collective-permute-start | bytes 460808 | tf_op jit(solution)/shard_map/ppermute | solution.py:39
  479.3 13.5 %collective-permute-start.10 = (bf16[200,3,128]{0,2,1:T(8,128)(2,1)S(1)}, bf16[200,3,128]{0,2,1:T(8,128)(2,1)S(1)}, u32[]{:S(2)}, u32[]{:S(2)}) collective-permute-start(bf16[200,3,128]{0,2,1:T(8,128)(2,1)S(1)} %get-tuple-element.136), channel_id=1, source_target_pairs={{1,0},{3,2},{5,4},{7,6},{9,8},{11,10},{13,12},{15,14},{17,16},{19,... | collective-permute-start | bytes 460808 | tf_op jit(solution)/shard_map/ppermute | solution.py:39
  486.1 6.7 %collective-permute-start.12 = (bf16[200,3,128]{0,2,1:T(8,128)(2,1)S(1)}, bf16[200,3,128]{0,2,1:T(8,128)(2,1)S(1)}, u32[]{:S(2)}, u32[]{:S(2)}) collective-permute-start(bf16[200,3,128]{0,2,1:T(8,128)(2,1)S(1)} %collective-permute-done.11), channel_id=1, source_target_pairs={{0,4},{2,6},{4,0},{6,2},{8,12},{10,14},{12,8},{14,10},{1,5},{3,7},... | collective-permute-start | bytes 460808 | tf_op jit(solution)/shard_map/ppermute | solution.py:27
  492.8 15.4 %collective-permute-start.13 = (bf16[200,3,128]{0,2,1:T(8,128)(2,1)S(1)}, bf16[200,3,128]{0,2,1:T(8,128)(2,1)S(1)}, u32[]{:S(2)}, u32[]{:S(2)}) collective-permute-start(bf16[200,3,128]{0,2,1:T(8,128)(2,1)S(1)} %collective-permute-done.12), channel_id=1, source_target_pairs={{0,8},{2,10},{4,12},{6,14},{8,0},{10,2},{12,4},{14,6},{1,9},{3,11}... | collective-permute-start | bytes 460808 | tf_op jit(solution)/shard_map/ppermute | solution.py:27
  (109 other events, 1042.5 us)
Sparse Core Ops, SparseCore 0:
  420.1 98.2 all-reduce.52
where the time goes:
time: 537 us; the launch traced here: 530 us
  other arithmetic  301 us (56%)
  local copies, waits for them, and re-layouts  59.5 us (11%)
  blocking collectives  56.2 us (10%)
  matrix products  40.7 us (8%)
  waiting for transfers between devices  28.1 us (5%)
  starting transfers between devices  27.8 us (5%)
  between operations  16.4 us (3%)
    reduce_sum x1, other arithmetic, on_device(): average = jnp.mean(convolved, axis=0)  91.6 us
    mul x3, other arithmetic, on_device(): tap_weight * conv_wide  71.3 us
    another operation x1, other arithmetic  70.8 us
    psum x1, blocking collectives, on_device(): lax.psum((kernel_part, gain_part, expand_part, reduce_part, scale_part),...  56.2 us
    reduce_sum x3, other arithmetic, on_device(): kernel_terms.append(jnp.sum(conv_wide * window, axis=(1, 2)))  38.2 us
    unnamed x245, local copies, waits for them, and re-layouts  28.8 us
    ppermute x6, waiting for transfers between devices, swapped(): lax.ppermute(x, axis, [(i, i ^ 1 << apart) for i in range(lax.axis_size(a...  28 us
  transfers between devices with their start and end apart: 15, of which 4 were waited for; matrix products, arithmetic and copies ran while one was open for 13% of the time, Pallas kernels for 0%

commit v1 on v0

v1 whole, which is shorter than its diff:
```python
import jax
import jax.numpy as jnp
from jax import lax
from jax.experimental import pallas as pl
from jax.experimental.pallas import tpu as pltpu
from jax.sharding import PartitionSpec as P

KS = 7
REACH = KS // 2
F32 = jnp.float32
BF16 = jnp.bfloat16
HALO = 8
VMEM_LIMIT = 58 << 20


def vmem():
    return pl.BlockSpec(memory_space=pltpu.VMEM)


def smem():
    return pl.BlockSpec(memory_space=pltpu.SMEM)


def call(body, outs, scratch=(), n_smem=0, n_in=0, cost=None):
    return pl.pallas_call(
        body,
        out_shape=outs,
        in_specs=[smem()] * n_smem + [vmem()] * (n_in - n_smem),
        out_specs=jax.tree.map(lambda _: vmem(), outs),
        scratch_shapes=list(scratch),
        compiler_params=pltpu.CompilerParams(vmem_limit_bytes=VMEM_LIMIT),
        cost_estimate=cost,
    )


def dot(a, b, ca, cb):
    return lax.dot_general(a, b, (((ca,), (cb,)), ((), ())), preferred_element_type=F32)


def shape(dims, dtype):
    return jax.ShapeDtypeStruct(dims, dtype)


def iota(dims, axis):
    return lax.broadcasted_iota(jnp.int32, dims, axis)


def as_f32(mask):
    return jnp.where(mask, 1.0, 0.0).astype(F32)


def tap_rows(rows):
    total = KS * (rows + HALO) + HALO
    q = iota((rows, total), 1)
    r = iota((rows, total), 0)
    t = (q - KS * rows) % HALO
    halo = jnp.where(t < REACH, rows + t, jnp.where(t < 2 * REACH, t - 2 * REACH, 4 * rows))
    halo = jnp.where(q < KS * (rows + HALO), halo, 4 * rows)
    return jnp.where(q < KS * rows, q % rows, halo) - r


def shift_stack(own, edge):
    lanes = own.shape[1]
    rows = own.shape[0] - HALO
    lane = iota(own.shape, 1)
    mains, halos = [], []
    for j in range(KS):
        d = j - REACH
        if d == 0:
            s = own
        elif d > 0:
            s = pltpu.roll(jnp.where(lane < d, edge, own), lanes - d, 1)
        else:
            s = pltpu.roll(jnp.where(lane >= lanes + d, edge, own), -d, 1)
        mains.append(s[:rows].astype(BF16))
        halos.append(s[rows:])
    halos.append(jnp.zeros_like(halos[0]))
    pairs = [
        jnp.concatenate([halos[i], halos[i + 1]], axis=0).astype(BF16)
        for i in range(0, KS + 1, 2)
    ]
    return jnp.concatenate(mains + pairs, axis=0)


def stage_halo(north, lat_ref, fold_ref, rb, rh):
    channels, lanes = lat_ref.shape[1], lat_ref.shape[2] // 2
    is_north = north != 0
    for t in range(REACH):
        near = lat_ref[t].astype(F32)
        far = fold_ref[t].astype(F32)
        up = jnp.where(is_north, far, near)
        low = jnp.where(is_north, near, jnp.zeros_like(near))
        rb[pl.ds(t * channels, channels), :] = up[:, :lanes]
        rh[pl.ds(t * channels, channels), :] = up[:, lanes:]
        rb[pl.ds((REACH + t) * channels, channels), :] = low[:, :lanes]
        rh[pl.ds((REACH + t) * channels, channels), :] = low[:, lanes:]
    for t in range(2 * REACH, HALO):
        rb[pl.ds(t * channels, channels), :] = jnp.zeros((channels, lanes), F32)
        rh[pl.ds(t * channels, channels), :] = jnp.zeros((channels, lanes), F32)


def channel_stack(c, channels, x_ref, h_ref, rb, rh):
    own = jnp.concatenate([x_ref[c].astype(F32), rb[pl.ds(c, HALO, stride=channels), :]], axis=0)
    edge = jnp.concatenate([h_ref[c].astype(F32), rh[pl.ds(c, HALO, stride=channels), :]], axis=0)
    return shift_stack(own, edge)


def pack_kernel(x_ref, lo_ref, hi_ref):
    lanes = x_ref.shape[1]
    k = iota((2 * HALO, lanes), 0)
    lane = iota((2 * HALO, lanes), 1)
    pick = ((k < REACH) & (lane == k)) | (
        (k >= HALO) & (k < HALO + REACH) & (lane == lanes - REACH + k - HALO)
    )
    sel = as_f32(pick).astype(BF16)
    edges = dot(sel, x_ref[...], 1, 1)
    lo_ref[...] = edges[:HALO].astype(BF16)
    hi_ref[...] = edges[HALO:].astype(BF16)


def unpack_kernel(north_ref, x_ref, east_ref, west_ref, h_ref, lat_ref, fold_ref, xs, hs):
    channels, rows, lanes = x_ref.shape
    k = iota((HALO, lanes), 0)
    lane = iota((HALO, lanes), 1)
    sel_e = as_f32((k < REACH) & (lane == k)).astype(BF16)
    sel_w = as_f32((k < REACH) & (lane == lanes - REACH + k)).astype(BF16)
    sel = jnp.concatenate([sel_e, sel_w], axis=0)
    ed = jnp.concatenate([east_ref[...], west_ref[...]], axis=0)
    hf = dot(ed, sel, 0, 0).reshape(channels, rows, lanes)
    h_ref[...] = hf.astype(BF16)
    g = HALO
    xs[0] = x_ref[:, :16, :].astype(F32)[:, :g].reshape(channels * g, lanes)
    xs[1] = x_ref[:, rows - 16 :, :].astype(F32)[:, 16 - g :].reshape(channels * g, lanes)
    hs[0] = hf[:, :g].reshape(channels * g, lanes)
    hs[1] = hf[:, rows - g :].reshape(channels * g, lanes)
    is_north = north_ref[0] != 0
    rev = as_f32(iota((lanes, lanes), 0) + iota((lanes, lanes), 1) == lanes - 1).astype(BF16)
    for t in range(REACH):
        for part, ref in ((0, xs), (1, hs)):
            bottom = ref.at[0][pl.ds(t, channels, stride=g), :]
            top = ref.at[1][pl.ds(g - REACH + t, channels, stride=g), :]
            span = slice(part * lanes, (part + 1) * lanes)
            lat_ref[t, :, span] = jnp.where(is_north, bottom, top).astype(BF16)
            fold_ref[REACH - 1 - t, :, span] = dot(top.astype(BF16), rev, 1, 0).astype(BF16)


def table_kernel(tab_ref, tab2_ref, a_ref, a2_ref):
    channels, rows, total = a_ref.shape
    gap = tap_rows(rows)

    def step(c, carry):
        one = jnp.zeros((rows, total), F32)
        two = jnp.zeros((rows, total), F32)
        for a in range(KS):
            hit = gap == a - REACH
            one = jnp.where(hit, tab_ref[c, a : a + 1, :], one)
            two = jnp.where(hit, tab2_ref[c, a : a + 1, :], two)
        a_ref[c] = one.astype(BF16)
        a2_ref[c] = two.astype(BF16)
        return carry

    lax.fori_loop(0, channels, step, 0)


def gelu_parts(hidden):
    k0 = 0.7978845608028654
    k1 = 0.044715 * k0
    sq = hidden * hidden
    th = jnp.tanh(hidden * (k0 + k1 * sq))
    half = 0.5 * th + 0.5
    act = hidden * half
    slope = half + act * (1.0 - th) * (k0 + 3.0 * k1 * sq)
    return act, slope


def main_kernel(
    north_ref, x_ref, h_ref, lat_ref, fold_ref, a_ref, cot_ref, mask_ref, gain_ref, scale_ref,
    wet_ref, we_ref, wr_ref, wrt_ref,
    out_ref, g_ref, exp_ref, red_ref, sums_ref,
    conv, cots, gs, ms, rb, rh, act_s, hg_s,
):
    channels, rows, lanes = x_ref.shape
    hiddens = we_ref.shape[1]
    stage_halo(north_ref[0], lat_ref, fold_ref, rb, rh)

    def conv_step(c, carry):
        stack = channel_stack(c, channels, x_ref, h_ref, rb, rh)
        conv[pl.ds(c, rows, stride=channels), :] = dot(a_ref[c], stack, 1, 0)
        cots[pl.ds(c, rows, stride=channels), :] = cot_ref[c].astype(F32) * mask_ref[...]
        return carry

    lax.fori_loop(0, channels, conv_step, 0, unroll=2)
    exp_ref[...] = jnp.zeros_like(exp_ref)
    red_ref[...] = jnp.zeros_like(red_ref)
    sums_ref[...] = jnp.zeros_like(sums_ref)

    def pair(ref, i):
        first = pl.multiple_of(2 * i * channels, 8)
        second = pl.multiple_of((2 * i + 1) * channels, 8)
        return jnp.concatenate(
            [ref[pl.ds(first, channels), :], ref[pl.ds(second, channels), :]], axis=1
        )

    def unpair(ref, i, value):
        ref[pl.ds(2 * i, channels, stride=rows), :] = value[:, :lanes]
        ref[pl.ds(2 * i + 1, channels, stride=rows), :] = value[:, lanes:]

    def cell_step(i, carry):
        gain = gain_ref[...]
        scale = scale_ref[...]
        value = pair(conv, i)
        centred = value - jnp.mean(value, axis=0, keepdims=True)
        inverse = lax.rsqrt(jnp.mean(centred * centred, axis=0, keepdims=True) + 1e-06)
        normalized = centred * inverse
        normed = (normalized * gain).astype(BF16)
        branch = pair(cots, i)
        mixed_grad = (scale * branch).astype(BF16)
        part = 160
        for f in range(0, hiddens, part):
            hidden = dot(wet_ref[f : f + part, :], normed, 1, 0)
            act_grad = dot(wr_ref[f : f + part, :], mixed_grad, 1, 0)
            act, slope = gelu_parts(hidden)
            act_s[f : f + part, :] = act.astype(BF16)
            hg_s[f : f + part, :] = (act_grad * slope).astype(BF16)
        mixed = dot(wrt_ref[...], act_s[...], 1, 0)
        red_ref[...] += dot(act_s[...], mixed_grad, 1, 1)
        normed_grad = dot(we_ref[...], hg_s[...], 1, 0)
        exp_ref[...] += dot(hg_s[...], normed, 1, 1)
        unpair(ms, i, scale * mixed)
        scaled = branch * mixed
        sums_ref[1] += scaled[:, :lanes] + scaled[:, lanes:]
        gained = normed_grad * normalized
        sums_ref[0] += gained[:, :lanes] + gained[:, lanes:]
        unit = normed_grad * gain
        m1 = jnp.mean(unit, axis=0, keepdims=True)
        m2 = jnp.mean(unit * normalized, axis=0, keepdims=True)
        unpair(gs, i, inverse * (unit - m1 - normalized * m2))
        return carry

    lax.fori_loop(0, rows // 2, cell_step, 0)

    def out_step(c, carry):
        at = pl.multiple_of(c * rows, rows)
        out_ref[c] = (x_ref[c].astype(F32) + mask_ref[...] * ms[pl.ds(at, rows), :]).astype(BF16)
        g_ref[c] = gs[pl.ds(at, rows), :].astype(BF16)
        return carry

    lax.fori_loop(0, channels, out_step, 0, unroll=4)


def tap_kernel(north_ref, x_ref, h_ref, lat_ref, fold_ref, g_ref, kg_ref, rb, rh, rowsum):
    channels, rows, lanes = x_ref.shape
    total = KS * (rows + HALO) + HALO
    stage_halo(north_ref[0], lat_ref, fold_ref, rb, rh)
    gap = tap_rows(rows)

    def step(c, carry):
        stack = channel_stack(c, channels, x_ref, h_ref, rb, rh)
        m = dot(g_ref[c], stack, 1, 1)
        for a in range(KS):
            rowsum[a, pl.ds(c, 1), :] = jnp.sum(
                jnp.where(gap == a - REACH, m, 0.0), axis=0, keepdims=True
            )
        return carry

    lax.fori_loop(0, channels, step, 0, unroll=2)
    q = iota((total, lanes), 0)
    block = jnp.where(q < KS * rows, q // rows, (q - KS * rows) // HALO)
    group = as_f32(block == iota((total, lanes), 1)).astype(BF16)
    for a in range(KS):
        v = rowsum[a]
        hi = v.astype(BF16)
        lo = (v - hi.astype(F32)).astype(BF16)
        kg_ref[a] = dot(hi, group, 1, 0) + dot(lo, group, 1, 0)


def adjoint_kernel(north_ref, g_ref, h_ref, lat_ref, fold_ref, a_ref, cot_ref, out_ref, rb, rh):
    channels, rows, lanes = g_ref.shape
    stage_halo(north_ref[0], lat_ref, fold_ref, rb, rh)

    def step(c, carry):
        stack = channel_stack(c, channels, g_ref, h_ref, rb, rh)
        out_ref[c] = (cot_ref[c].astype(F32) + dot(a_ref[c], stack, 1, 0)).astype(BF16)
        return carry

    lax.fori_loop(0, channels, step, 0, unroll=2)


def halo_exchange(field, north):
    channels, rows, lanes = field.shape
    n, m = lax.axis_size("lon"), lax.axis_size("lat")
    edge = shape((HALO, channels * rows), BF16)
    low, high = call(pack_kernel, (edge, edge), n_in=1)(field.reshape(channels * rows, lanes))
    from_east = lax.ppermute(low, "lon", [((i + 1) % n, i) for i in range(n)])
    from_west = lax.ppermute(high, "lon", [(i, (i + 1) % n) for i in range(n)])
    msg = shape((REACH, channels, 2 * lanes), BF16)
    lane_halo, lat_msg, fold_msg = call(
        unpack_kernel,
        (shape(field.shape, BF16), msg, msg),
        scratch=[pltpu.VMEM((2, channels * HALO, lanes), F32)] * 2,
        n_smem=1,
        n_in=4,
    )(north, field, from_east, from_west)
    lat_rows = lax.ppermute(lat_msg, "lat", [(0, 1), (1, 0)])
    fold_rows = lax.ppermute(
        fold_msg, ("lon", "lat"), [(i * m + m - 1, (n - 1 - i) * m + m - 1) for i in range(n)]
    )
    return lane_halo, lat_rows, fold_rows


def split_half(buf, bit):
    rows, lanes = buf.shape
    if (rows // 2) % 8 and lanes > 128:
        first, second = buf[:, : lanes // 2], buf[:, lanes // 2 :]
    else:
        first, second = buf[: rows // 2], buf[rows // 2 :]
    up = bit != 0
    return jnp.where(up, second, first), jnp.where(up, first, second)


def join_half(mine, other, bit, dims):
    up = bit != 0
    first, second = jnp.where(up, other, mine), jnp.where(up, mine, other)
    return jnp.concatenate([first, second], axis=1 if mine.shape[0] == dims[0] else 0)


def all_sum(buf):
    steps = [("lat", 0)] + [("lon", b) for b in range(lax.axis_size("lon").bit_length() - 1)]
    sizes = []
    for axis, b in steps:
        bit = (lax.axis_index(axis) >> b) & 1
        sizes.append(buf.shape)
        keep, send = split_half(buf, bit)
        pairs = [(i, i ^ (1 << b)) for i in range(lax.axis_size(axis))]
        buf = keep + lax.ppermute(send.astype(BF16), axis, pairs).astype(F32)
    buf = buf.astype(BF16)
    for (axis, b), dims in zip(steps[::-1], sizes[::-1]):
        bit = (lax.axis_index(axis) >> b) & 1
        pairs = [(i, i ^ (1 << b)) for i in range(lax.axis_size(axis))]
        buf = join_half(buf, lax.ppermute(buf, axis, pairs), bit, dims)
    return buf.astype(F32)


def stack_taps(taps, halo_taps, rows):
    main = jnp.repeat(taps, rows, axis=2)
    halo = jnp.concatenate([jnp.repeat(t[:, :, :, None], n, axis=3) for t, n in halo_taps], axis=3)
    halo = halo.reshape(taps.shape[0], KS, KS * HALO)
    both = jnp.concatenate([main, halo], axis=2)
    return jnp.pad(both, ((0, 0), (0, 1), (0, HALO)))


def on_device(
    ocean_state, cotangent, kernel, norm_gain, expand_weight, reduce_weight, layer_scale, land_mask
):
    channels, rows, lanes = ocean_state.shape
    hiddens = expand_weight.shape[1]
    total = KS * (rows + HALO) + HALO
    is_north = lax.axis_index("lat") == lax.axis_size("lat") - 1
    north = is_north.astype(jnp.int32).reshape(1)
    mask = land_mask.astype(F32)

    halo, lat_rows, fold_rows = halo_exchange(ocean_state, north)

    taps = kernel.reshape(channels, KS, KS)
    flipped = taps[:, ::-1, ::-1]
    beyond = jnp.where(is_north, taps, flipped)
    tab = stack_taps(taps, ((taps, HALO),), rows)
    tab2 = stack_taps(flipped, ((beyond, REACH), (flipped, HALO - REACH)), rows)
    table = shape((channels, rows, total), BF16)
    forward_table, adjoint_table = call(table_kernel, (table, table), n_in=2)(tab, tab2)

    rowbuf = pltpu.VMEM((HALO * channels, lanes), F32)
    cellbuf = pltpu.VMEM((channels * rows, lanes), F32)
    field = shape(ocean_state.shape, BF16)
    block_out, conv_grad, exp_part, red_part, sums = call(
        main_kernel,
        (
            field,
            field,
            shape((hiddens, channels), F32),
            shape((hiddens, channels), F32),
            shape((2, channels, lanes), F32),
        ),
        scratch=[cellbuf] * 4 + [rowbuf] * 2 + [pltpu.VMEM((hiddens, 2 * lanes), BF16)] * 2,
        n_smem=1,
        n_in=14,
    )(
        north, ocean_state, halo, lat_rows, fold_rows, forward_table, cotangent, mask,
        norm_gain.reshape(channels, 1), layer_scale.reshape(channels, 1),
        expand_weight.T, expand_weight, reduce_weight, reduce_weight.T,
    )

    g_halo, g_lat, g_fold = halo_exchange(conv_grad, north)

    kg = call(
        tap_kernel,
        shape((KS, channels, lanes), F32),
        scratch=[rowbuf] * 2 + [pltpu.VMEM((KS, channels, total), F32)],
        n_smem=1,
        n_in=6,
    )(north, ocean_state, halo, lat_rows, fold_rows, conv_grad)

    state_grad = call(
        adjoint_kernel, field, scratch=[rowbuf] * 2, n_smem=1, n_in=7
    )(north, conv_grad, g_halo, g_lat, g_fold, adjoint_table, cotangent)

    kernel_part = jnp.transpose(kg[:, :, :KS], (1, 0, 2)).reshape(channels, KS * KS)
    small = jnp.concatenate(
        [kernel_part, jnp.sum(sums[0], axis=1)[:, None], jnp.sum(sums[1], axis=1)[:, None]], axis=1
    )
    spare = 256 - channels
    small = jnp.pad(small, ((0, 2 * hiddens - channels), (0, spare - small.shape[1])))
    buf = jnp.concatenate([jnp.concatenate([exp_part, red_part], axis=0), small], axis=1)
    buf = all_sum(buf)
    expand_grad = buf[:hiddens, :channels].T
    reduce_grad = buf[hiddens:, :channels]
    tail = buf[:channels, channels:]
    kernel_grad = tail[:, : KS * KS]
    gain_grad = tail[:, KS * KS]
    scale_grad = tail[:, KS * KS + 1]
    return (block_out, state_grad, kernel_grad, gain_grad, expand_grad, reduce_grad, scale_grad)


def solution(mesh):
    tiles = P(None, ("members", "lat"), "lon")
    return jax.shard_map(
        on_device,
        mesh=mesh,
        in_specs=(tiles, tiles, P(), P(), P(), P(), P(), P("lat", "lon")),
        out_specs=(
            tiles, tiles, P("members", None), P("members"), P("members", None),
            P("members", None), P("members"),
        ),
        check_vma=False,
    )
```

time: 537 us -> 241 us (0.45); the launches traced: 530 us -> 240 us
  other arithmetic: 301 us -> 6.49 us
  Pallas kernels: 0 us -> 150 us
  blocking collectives: 56.2 us -> 0 us
  matrix products: 40.7 us -> 0 us
  local copies, waits for them, and re-layouts: 59.5 us -> 23.1 us
  between operations: 16.4 us -> 1.06 us
    pallas_call x0 -> x8, Pallas kernels: none -> 150 us  [the longest x1 55.4 us: on_device(): call(main_kernel, (field, field, shape((hiddens, channels), F32), shape((...]
    reduce_sum x6 -> x1, other arithmetic: 139 us -> 0.15 us  [on_device(): jnp.sum(sums[0], axis=1)[:, None]]
    mul x4 -> x0, other arithmetic: 71.3 us -> none  [the longest x3 71.3 us: on_device(): tap_weight * conv_wide]
    another operation x1 -> x0, other arithmetic: 70.8 us -> none
    psum x1 -> x0, blocking collectives: 56.2 us -> none  [on_device(): lax.psum((kernel_part, gain_part, expand_part, reduce_part, scale_part),...]
    dot_general x6 -> x0, matrix products: 40.7 us -> none  [the longest x1 10.1 us: on_device(): jnp.einsum('fc,ct->ft', reduce_weight, mixed_grad, preferred_element_type...]
    unnamed x245 -> x39, local copies, waits for them, and re-layouts: 28.8 us -> 10.7 us
    slice x9 -> x1, local copies, waits for them, and re-layouts: 13 us -> 0.11 us  [on_device(): reduce_grad = buf[hiddens:, :channels]]
  transfers between devices with their start and end apart: 15 -> 16, of which waited for: 4 -> 7; matrix products, arithmetic and copies ran while one was open for 13% -> 8% of each run, Pallas kernels for 0% -> 21%
where the time goes in v1:
time: 241 us; the launch traced here: 240 us
  Pallas kernels  150 us (62%)
  waiting for transfers between devices  32 us (13%)
  starting transfers between devices  28.1 us (12%)
  local copies, waits for them, and re-layouts  23.1 us (10%)
  other arithmetic  6.49 us (3%)
    pallas_call x1, Pallas kernels, on_device(): call(main_kernel, (field, field, shape((hiddens, channels), F32), shape((...  55.4 us
    pallas_call x1, Pallas kernels, on_device(): call(tap_kernel, shape((KS, channels, lanes), F32), scratch=[rowbuf] * 2...  36.5 us
    pallas_call x1, Pallas kernels, on_device(): call(adjoint_kernel, field, scratch=[rowbuf] * 2, n_smem=1, n_in=7)  28.9 us
    ppermute x4, waiting for transfers between devices, all_sum(): buf = keep + lax.ppermute(send.astype(BF16), axis, pairs).astype(F32)  15.9 us
    pallas_call x1, Pallas kernels, on_device(): call(table_kernel, (table, table), n_in=2)(tab, tab2)  15.7 us
    unnamed x39, local copies, waits for them, and re-layouts  10.7 us
    ppermute x2, starting transfers between devices, halo_exchange(): lax.ppermute(fold_msg, ('lon', 'lat'), [(i * m + m - 1, (n - 1 - i) * m +...  8.7 us
    ppermute x2, waiting for transfers between devices, halo_exchange(): lax.ppermute(fold_msg, ('lon', 'lat'), [(i * m + m - 1, (n - 1 - i) * m +...  8.2 us
  transfers between devices with their start and end apart: 16, of which 7 were waited for; matrix products, arithmetic and copies ran while one was open for 8% of the time, Pallas kernels for 21%

profile of v1, /device:TPU:1, one launch (start us, length us, event | category | flops | bytes accessed | tf_op | source)
XLA Modules:
  0.0 240.4 jit_solution(12845448305646856247)
XLA Ops:
  0.6 2.7 %shard_map.135 = (bf16[8,6400]{1,0:T(8,128)(2,1)}, bf16[8,6400]{1,0:T(8,128)(2,1)}) custom-call(bf16[6400,128]{1,0:T(8,128)(2,1)} %bitcast.23), custom_call_target="tpu_custom_call" | custom-call | tf_op jit(solution)/shard_map/pallas_call | solution.py:293
  3.3 5.1 %collective-permute-start = (bf16[8,6400]{1,0:T(8,128)(2,1)}, bf16[8,6400]{1,0:T(8,128)(2,1)S(1)}, u32[]{:S(2)}, u32[]{:S(2)}) collective-permute-start(bf16[8,6400]{1,0:T(8,128)(2,1)} %get-tuple-element.24), channel_id=1, source_target_pairs={{2,0},{4,2},{6,4},{8,6},{10,8},{12,10},{14,12},{0,14},{3,1},{5,3},... | collective-permute-start | bytes 307208 | tf_op jit(solution)/shard_map/ppermute | solution.py:294
  13.1 2.1 copy.25
  15.3 2.2 copy.26
  17.5 1.9 copy.29
  19.4 1.9 copy.32.wr_ref
  24.2 3.9 %shard_map.136 = (bf16[200,32,128]{2,1,0:T(8,128)(2,1)}, bf16[3,200,256]{2,1,0:T(8,128)(2,1)}, bf16[3,200,256]{2,1,0:T(8,128)(2,1)}) custom-call(s32[1]{0:T(128)} %bitcast.north_ref, bf16[200,32,128]{2,1,0:T(8,128)(2,1)} %x_ref.5, bf16[8,6400]{1,0:T(8,128)(2,1)} %copy-done.9, bf16[8,6400]{1,0:T(8,128)(2,1)} %copy-done.10), custom_call_target="tpu_custom_call" | custom-call | tf_op jit(solution)/shard_map/pallas_call | solution.py:297
  29.0 6.3 %collective-permute-start.3 = (bf16[3,200,256]{2,1,0:T(8,128)(2,1)}, bf16[3,200,256]{2,1,0:T(8,128)(2,1)S(1)}, u32[]{:S(2)}, u32[]{:S(2)}) collective-permute-start(bf16[3,200,256]{2,1,0:T(8,128)(2,1)} %get-tuple-element.28), channel_id=1, source_target_pairs={{1,15},{3,13},{5,11},{7,9},{9,7},{11,5},{13,3},{15,1},{17,31},{19,... | collective-permute-start | bytes 921608 | tf_op jit(solution)/shard_map/ppermute | solution.py:305
  35.4 3.5 %select_maximum_fusion = (f32[200,8,288]{2,1,0:T(8,128)}, f32[200,8,288]{2,1,0:T(8,128)}) fusion(f32[200,7,56]{2,1,0:T(8,128)S(1)} %copy-done, f32[200,7,224]{2,1,0:T(8,128)S(1)} %copy.27, f32[200,7,56]{2,1,0:T(8,128)S(1)} %copy-done.1, f32[200,7,224]{2,1,0:T(8,128)S(1)} %copy.25), kind=kLoop, calls=%fused_computation | loop fusion | flops 5990400 | bytes 6822400 | tf_op jit(solution)/shard_map/concatenate | solution.py:348
  38.8 15.7 %shard_map.137 = (bf16[200,32,288]{2,1,0:T(8,128)(2,1)}, bf16[200,32,288]{2,1,0:T(8,128)(2,1)}) custom-call(f32[200,8,288]{2,1,0:T(8,128)} %get-tuple-element.70.tab_ref, f32[200,8,288]{2,1,0:T(8,128)} %get-tuple-element.69.tab2_ref), custom_call_target="tpu_custom_call" | custom-call | tf_op jit(solution)/shard_map/pallas_call | solution.py:370
  55.4 55.4 %shard_map.138 = (bf16[200,32,128]{2,1,0:T(8,128)(2,1)}, bf16[200,32,128]{2,1,0:T(8,128)(2,1)}, f32[800,200]{1,0:T(8,128)}, f32[800,200]{1,0:T(8,128)}, f32[2,200,128]{2,1,0:T(8,128)}) custom-call(s32[1]{0:T(128)} %bitcast.north_ref, bf16[200,32,128]{2,1,0:T(8,128)(2,1)} %x_ref.5, bf16[200,32,128]{2,1,0:T(8,128)(2,1)} %get-tuple-element.26.h_ref, ...), custom_call_target="tpu_custom_call" | custom-call | tf_op jit(solution)/shard_map/pallas_call | solution.py:375
  110.9 36.5 %shard_map.142 = f32[7,200,128]{2,1,0:T(8,128)} custom-call(s32[1]{0:T(128)} %bitcast.north_ref, bf16[200,32,128]{2,1,0:T(8,128)(2,1)} %x_ref.5, bf16[200,32,128]{2,1,0:T(8,128)(2,1)} %get-tuple-element.26.h_ref, bf16[3,200,256]{2,1,0:T(8,128)(2,1)} %copy-done.2, bf16[3,200,256]{2,1,0:T(8,128)(2,1)} %copy-done.3, ...), custom_call_target="tpu_custom_call" | custom-call | tf_op jit(solution)/shard_map/pallas_call | solution.py:395
  152.4 6.5 %collective-permute-done.9 = bf16[400,256]{1,0:T(8,128)(2,1)S(1)} collective-permute-done((bf16[400,256]{1,0:T(8,128)(2,1)S(1)}, bf16[400,256]{1,0:T(8,128)(2,1)S(1)}, u32[]{:S(2)}, u32[]{:S(2)}) %collective-permute-start.9) | collective-permute-done | bytes 204832 | tf_op jit(solution)/shard_map/ppermute | solution.py:335
  159.1 3.5 %collective-permute-done.10 = bf16[200,256]{1,0:T(8,128)(2,1)S(1)} collective-permute-done((bf16[200,256]{1,0:T(8,128)(2,1)S(1)}, bf16[200,256]{1,0:T(8,128)(2,1)S(1)}, u32[]{:S(2)}, u32[]{:S(2)}) %collective-permute-start.10) | collective-permute-done | bytes 102432 | tf_op jit(solution)/shard_map/ppermute | solution.py:335
  162.7 4.1 %collective-permute-done.11 = bf16[200,128]{1,0:T(8,128)(2,1)S(1)} collective-permute-done((bf16[200,128]{1,0:T(8,128)(2,1)S(1)}, bf16[200,128]{1,0:T(8,128)(2,1)S(1)}, u32[]{:S(2)}, u32[]{:S(2)}) %collective-permute-start.11) | collective-permute-done | bytes 51232 | tf_op jit(solution)/shard_map/ppermute | solution.py:335
  167.0 3.9 %collective-permute-done.12 = bf16[200,128]{1,0:T(8,128)(2,1)S(1)} collective-permute-done((bf16[200,128]{1,0:T(8,128)(2,1)S(1)}, bf16[200,128]{1,0:T(8,128)(2,1)S(1)}, u32[]{:S(2)}, u32[]{:S(2)}) %collective-permute-start.12) | collective-permute-done | bytes 51232 | tf_op jit(solution)/shard_map/ppermute | solution.py:340
  171.0 4.0 %collective-permute-done.13 = bf16[200,256]{1,0:T(8,128)(2,1)S(1)} collective-permute-done((bf16[200,256]{1,0:T(8,128)(2,1)S(1)}, bf16[200,256]{1,0:T(8,128)(2,1)S(1)}, u32[]{:S(2)}, u32[]{:S(2)}) %collective-permute-start.13) | collective-permute-done | bytes 102432 | tf_op jit(solution)/shard_map/ppermute | solution.py:340
  175.8 2.7 %shard_map.139 = (bf16[8,6400]{1,0:T(8,128)(2,1)}, bf16[8,6400]{1,0:T(8,128)(2,1)}) custom-call(bf16[6400,128]{1,0:T(8,128)(2,1)} %bitcast.24), custom_call_target="tpu_custom_call" | custom-call | tf_op jit(solution)/shard_map/pallas_call | solution.py:293
  180.1 7.2 %collective-permute-start.15 = (bf16[800,256]{1,0:T(8,128)(2,1)S(1)}, bf16[800,256]{1,0:T(8,128)(2,1)S(1)}, u32[]{:S(2)}, u32[]{:S(2)}) collective-permute-start(bf16[800,256]{1,0:T(8,128)(2,1)S(1)} %pad_maximum_fusion.1), channel_id=1, source_target_pairs={{0,1},{1,0},{2,3},{3,2},{4,5},{5,4},{6,7},{7,6},{8,9},{9,8},{10,11... | collective-permute-start | bytes 1228808 | tf_op jit(solution)/shard_map/ppermute | solution.py:340
  188.6 3.8 %shard_map.140 = (bf16[200,32,128]{2,1,0:T(8,128)(2,1)}, bf16[3,200,256]{2,1,0:T(8,128)(2,1)}, bf16[3,200,256]{2,1,0:T(8,128)(2,1)}) custom-call(s32[1]{0:T(128)} %bitcast.north_ref, bf16[200,32,128]{2,1,0:T(8,128)(2,1)} %get-tuple-element.31.x_ref.g_ref, bf16[8,6400]{1,0:T(8,128)(2,1)} %copy-done.11, bf16[8,6400]{1,0:T(8,128)(2,1)} %copy-done.12), custom_call_target="tpu_custom_call" | custom-call | tf_op jit(solution)/shard_map/pallas_call | solution.py:297
  192.4 3.6 %collective-permute-start.6 = (bf16[3,200,256]{2,1,0:T(8,128)(2,1)}, bf16[3,200,256]{2,1,0:T(8,128)(2,1)S(1)}, u32[]{:S(2)}, u32[]{:S(2)}) collective-permute-start(bf16[3,200,256]{2,1,0:T(8,128)(2,1)} %get-tuple-element.35), channel_id=1, source_target_pairs={{0,1},{1,0},{2,3},{3,2},{4,5},{5,4},{6,7},{7,6},{8,9},{9,8},{10,11... | collective-permute-start | bytes 921608 | tf_op jit(solution)/shard_map/ppermute | solution.py:304
  195.9 2.4 collective-permute-start.7
  198.3 8.2 %collective-permute-done.7.fold_ref = bf16[3,200,256]{2,1,0:T(8,128)(2,1)S(1)} collective-permute-done((bf16[3,200,256]{2,1,0:T(8,128)(2,1)}, bf16[3,200,256]{2,1,0:T(8,128)(2,1)S(1)}, u32[]{:S(2)}, u32[]{:S(2)}) %collective-permute-start.7) | collective-permute-done | bytes 307232 | tf_op jit(solution)/shard_map/ppermute | solution.py:305
  207.3 28.9 %shard_map.141 = bf16[200,32,128]{2,1,0:T(8,128)(2,1)} custom-call(s32[1]{0:T(128)} %bitcast.north_ref, bf16[200,32,128]{2,1,0:T(8,128)(2,1)} %get-tuple-element.31.x_ref.g_ref, bf16[200,32,128]{2,1,0:T(8,128)(2,1)} %get-tuple-element.34.h_ref, bf16[3,200,256]{2,1,0:T(8,128)(2,1)} %copy-done.6, bf16[3,200,256]{2,1,0:T(8,128)(2,1)} %copy-done.7, ...), custom_call_target="tpu_custom_call" | custom-call | tf_op jit(solution)/shard_map/pallas_call | solution.py:403
  (100 shorter events, 23.3 us)
Async XLA Ops:
  0.6 7.8 %copy-start.13 = (f32[200,49]{0,1:T(8,128)S(1)}, f32[200,49]{0,1:T(8,128)}, u32[]{:S(2)}) copy-start(f32[200,49]{0,1:T(8,128)} %param.10) | copy-start | bytes 117604
  3.3 20.2 %collective-permute-start = (bf16[8,6400]{1,0:T(8,128)(2,1)}, bf16[8,6400]{1,0:T(8,128)(2,1)S(1)}, u32[]{:S(2)}, u32[]{:S(2)}) collective-permute-start(bf16[8,6400]{1,0:T(8,128)(2,1)} %get-tuple-element.24), channel_id=1, source_target_pairs={{2,0},{4,2},{6,4},{8,6},{10,8},{12,10},{14,12},{0,14},{3,1},{5,3},... | collective-permute-start | bytes 307208 | tf_op jit(solution)/shard_map/ppermute | solution.py:294
  8.4 15.1 %collective-permute-start.1 = (bf16[8,6400]{1,0:T(8,128)(2,1)}, bf16[8,6400]{1,0:T(8,128)(2,1)S(1)}, u32[]{:S(2)}, u32[]{:S(2)}) collective-permute-start(bf16[8,6400]{1,0:T(8,128)(2,1)} %get-tuple-element.25), channel_id=1, source_target_pairs={{0,2},{2,4},{4,6},{6,8},{8,10},{10,12},{12,14},{14,0},{1,3},{3,5},... | collective-permute-start | bytes 307208 | tf_op jit(solution)/shard_map/ppermute | solution.py:295
  15.3 6.1 %copy-start.15 = (f32[200]{0:T(256)S(1)}, f32[200]{0:T(256)}, u32[]{:S(2)}) copy-start(f32[200]{0:T(256)} %param.11) | copy-start | bytes 2404
  15.3 6.8 %copy-start.16 = (f32[200]{0:T(256)S(1)}, f32[200]{0:T(256)}, u32[]{:S(2)}) copy-start(f32[200]{0:T(256)} %param.14) | copy-start | bytes 2404
  15.3 7.6 %copy-start.14 = (s32[32,128]{1,0:T(8,128)S(1)}, s32[32,128]{1,0:T(8,128)}, u32[]{:S(2)}) copy-start(s32[32,128]{1,0:T(8,128)} %param.15) | copy-start | bytes 49156
  23.5 11.9 %copy-start = (f32[200,7,56]{2,1,0:T(8,128)S(1)}, f32[200,7,56]{2,1,0:T(8,128)}, u32[]{:S(2)}) copy-start(f32[200,7,56]{2,1,0:T(8,128)} %copy.28) | copy-start | bytes 940804
  23.5 11.9 %copy-start.1 = (f32[200,7,56]{2,1,0:T(8,128)S(1)}, f32[200,7,56]{2,1,0:T(8,128)}, u32[]{:S(2)}) copy-start(f32[200,7,56]{2,1,0:T(8,128)} %copy.26) | copy-start | bytes 940804
  28.1 26.5 %collective-permute-start.2 = (bf16[3,200,256]{2,1,0:T(8,128)(2,1)}, bf16[3,200,256]{2,1,0:T(8,128)(2,1)S(1)}, u32[]{:S(2)}, u32[]{:S(2)}) collective-permute-start(bf16[3,200,256]{2,1,0:T(8,128)(2,1)} %get-tuple-element.27), channel_id=1, source_target_pairs={{0,1},{1,0},{2,3},{3,2},{4,5},{5,4},{6,7},{7,6},{8,9},{9,8},{10,11... | collective-permute-start | bytes 921608 | tf_op jit(solution)/shard_map/ppermute | solution.py:304
  29.0 25.6 %collective-permute-start.3 = (bf16[3,200,256]{2,1,0:T(8,128)(2,1)}, bf16[3,200,256]{2,1,0:T(8,128)(2,1)S(1)}, u32[]{:S(2)}, u32[]{:S(2)}) collective-permute-start(bf16[3,200,256]{2,1,0:T(8,128)(2,1)} %get-tuple-element.28), channel_id=1, source_target_pairs={{1,15},{3,13},{5,11},{7,9},{9,7},{11,5},{13,3},{15,1},{17,31},{19,... | collective-permute-start | bytes 921608 | tf_op jit(solution)/shard_map/ppermute | solution.py:305
  147.4 1.7 copy-start.8
  150.3 1.8 collective-permute-start.8
  152.3 6.6 %collective-permute-start.9 = (bf16[400,256]{1,0:T(8,128)(2,1)S(1)}, bf16[400,256]{1,0:T(8,128)(2,1)S(1)}, u32[]{:S(2)}, u32[]{:S(2)}) collective-permute-start(bf16[400,256]{1,0:T(8,128)(2,1)S(1)} %select_convert_fusion.1), channel_id=1, source_target_pairs={{0,2},{2,0},{4,6},{6,4},{8,10},{10,8},{12,14},{14,12},{1,3},{3,1},... | collective-permute-start | bytes 614408 | tf_op jit(solution)/shard_map/ppermute | solution.py:335
  159.0 3.6 %collective-permute-start.10 = (bf16[200,256]{1,0:T(8,128)(2,1)S(1)}, bf16[200,256]{1,0:T(8,128)(2,1)S(1)}, u32[]{:S(2)}, u32[]{:S(2)}) collective-permute-start(bf16[200,256]{1,0:T(8,128)(2,1)S(1)} %select_convert_fusion.2), channel_id=1, source_target_pairs={{0,4},{2,6},{4,0},{6,2},{8,12},{10,14},{12,8},{14,10},{1,5},{3,7},... | collective-permute-start | bytes 307208 | tf_op jit(solution)/shard_map/ppermute | solution.py:335
  162.7 4.2 %collective-permute-start.11 = (bf16[200,128]{1,0:T(8,128)(2,1)S(1)}, bf16[200,128]{1,0:T(8,128)(2,1)S(1)}, u32[]{:S(2)}, u32[]{:S(2)}) collective-permute-start(bf16[200,128]{1,0:T(8,128)(2,1)S(1)} %select_convert_fusion.3), channel_id=1, source_target_pairs={{0,8},{2,10},{4,12},{6,14},{8,0},{10,2},{12,4},{14,6},{1,9},{3,11}... | collective-permute-start | bytes 153608 | tf_op jit(solution)/shard_map/ppermute | solution.py:335
  166.9 4.0 %collective-permute-start.12 = (bf16[200,128]{1,0:T(8,128)(2,1)S(1)}, bf16[200,128]{1,0:T(8,128)(2,1)S(1)}, u32[]{:S(2)}, u32[]{:S(2)}) collective-permute-start(bf16[200,128]{1,0:T(8,128)(2,1)S(1)} %add_convert_fusion), channel_id=1, source_target_pairs={{0,8},{2,10},{4,12},{6,14},{8,0},{10,2},{12,4},{14,6},{1,9},{3,11}... | collective-permute-start | bytes 153608 | tf_op jit(solution)/shard_map/ppermute | solution.py:340
  170.9 4.1 %collective-permute-start.13 = (bf16[200,256]{1,0:T(8,128)(2,1)S(1)}, bf16[200,256]{1,0:T(8,128)(2,1)S(1)}, u32[]{:S(2)}, u32[]{:S(2)}) collective-permute-start(bf16[200,256]{1,0:T(8,128)(2,1)S(1)} %pad_maximum_fusion.3), channel_id=1, source_target_pairs={{0,4},{2,6},{4,0},{6,2},{8,12},{10,14},{12,8},{14,10},{1,5},{3,7},... | collective-permute-start | bytes 307208 | tf_op jit(solution)/shard_map/ppermute | solution.py:340
  175.1 4.9 %collective-permute-start.14 = (bf16[400,256]{1,0:T(8,128)(2,1)S(1)}, bf16[400,256]{1,0:T(8,128)(2,1)S(1)}, u32[]{:S(2)}, u32[]{:S(2)}) collective-permute-start(bf16[400,256]{1,0:T(8,128)(2,1)S(1)} %pad_maximum_fusion.2), channel_id=1, source_target_pairs={{0,2},{2,0},{4,6},{6,4},{8,10},{10,8},{12,14},{14,12},{1,3},{3,1},... | collective-permute-start | bytes 614408 | tf_op jit(solution)/shard_map/ppermute | solution.py:340
  178.5 8.8 %collective-permute-start.4 = (bf16[8,6400]{1,0:T(8,128)(2,1)}, bf16[8,6400]{1,0:T(8,128)(2,1)S(1)}, u32[]{:S(2)}, u32[]{:S(2)}) collective-permute-start(bf16[8,6400]{1,0:T(8,128)(2,1)} %get-tuple-element.32), channel_id=1, source_target_pairs={{2,0},{4,2},{6,4},{8,6},{10,8},{12,10},{14,12},{0,14},{3,1},{5,3},... | collective-permute-start | bytes 307208 | tf_op jit(solution)/shard_map/ppermute | solution.py:294
  178.5 8.8 %collective-permute-start.5 = (bf16[8,6400]{1,0:T(8,128)(2,1)}, bf16[8,6400]{1,0:T(8,128)(2,1)S(1)}, u32[]{:S(2)}, u32[]{:S(2)}) collective-permute-start(bf16[8,6400]{1,0:T(8,128)(2,1)} %get-tuple-element.33), channel_id=1, source_target_pairs={{0,2},{2,4},{4,6},{6,8},{8,10},{10,12},{12,14},{14,0},{1,3},{3,5},... | collective-permute-start | bytes 307208 | tf_op jit(solution)/shard_map/ppermute | solution.py:295
  180.1 56.0 %collective-permute-start.15 = (bf16[800,256]{1,0:T(8,128)(2,1)S(1)}, bf16[800,256]{1,0:T(8,128)(2,1)S(1)}, u32[]{:S(2)}, u32[]{:S(2)}) collective-permute-start(bf16[800,256]{1,0:T(8,128)(2,1)S(1)} %pad_maximum_fusion.1), channel_id=1, source_target_pairs={{0,1},{1,0},{2,3},{3,2},{4,5},{5,4},{6,7},{7,6},{8,9},{9,8},{10,11... | collective-permute-start | bytes 1228808 | tf_op jit(solution)/shard_map/ppermute | solution.py:340
  192.4 5.9 %collective-permute-start.6 = (bf16[3,200,256]{2,1,0:T(8,128)(2,1)}, bf16[3,200,256]{2,1,0:T(8,128)(2,1)S(1)}, u32[]{:S(2)}, u32[]{:S(2)}) collective-permute-start(bf16[3,200,256]{2,1,0:T(8,128)(2,1)} %get-tuple-element.35), channel_id=1, source_target_pairs={{0,1},{1,0},{2,3},{3,2},{4,5},{5,4},{6,7},{7,6},{8,9},{9,8},{10,11... | collective-permute-start | bytes 921608 | tf_op jit(solution)/shard_map/ppermute | solution.py:304
  195.9 10.6 %collective-permute-start.7 = (bf16[3,200,256]{2,1,0:T(8,128)(2,1)}, bf16[3,200,256]{2,1,0:T(8,128)(2,1)S(1)}, u32[]{:S(2)}, u32[]{:S(2)}) collective-permute-start(bf16[3,200,256]{2,1,0:T(8,128)(2,1)} %get-tuple-element.36), channel_id=1, source_target_pairs={{1,15},{3,13},{5,11},{7,9},{9,7},{11,5},{13,3},{15,1},{17,31},{19,... | collective-permute-start | bytes 921608 | tf_op jit(solution)/shard_map/ppermute | solution.py:305
  198.3 8.2 %copy-start.6 = (bf16[3,200,256]{2,1,0:T(8,128)(2,1)}, bf16[3,200,256]{2,1,0:T(8,128)(2,1)S(1)}, u32[]{:S(2)}) copy-start(bf16[3,200,256]{2,1,0:T(8,128)(2,1)S(1)} %collective-permute-done.6.lat_ref) | copy-start | bytes 921604
  (9 other events, 7.4 us)

commit v2 on v1

v2 whole, which is shorter than its diff:
```python
import functools

import jax
import jax.numpy as jnp
from jax import lax
from jax.experimental import pallas as pl
from jax.experimental.pallas import tpu as pltpu
from jax.sharding import PartitionSpec as P

KS = 7
REACH = KS // 2
F32 = jnp.float32
BF16 = jnp.bfloat16
HALO = 8
VMEM_LIMIT = 58 << 20
CHUNKS = 5


def vmem():
    return pl.BlockSpec(memory_space=pltpu.VMEM)


def smem():
    return pl.BlockSpec(memory_space=pltpu.SMEM)


def call(body, outs, scratch=(), n_smem=0, n_in=0, cost=None):
    return pl.pallas_call(
        body,
        out_shape=outs,
        in_specs=[smem()] * n_smem + [vmem()] * (n_in - n_smem),
        out_specs=jax.tree.map(lambda _: vmem(), outs),
        scratch_shapes=list(scratch),
        compiler_params=pltpu.CompilerParams(vmem_limit_bytes=VMEM_LIMIT),
        cost_estimate=cost,
    )


def grid_call(body, grid, outs, in_specs, out_specs, scratch, cost, aliases=None):
    return pl.pallas_call(
        body,
        grid=(grid,),
        out_shape=outs,
        in_specs=in_specs,
        out_specs=out_specs,
        scratch_shapes=list(scratch),
        input_output_aliases=aliases or {},
        compiler_params=pltpu.CompilerParams(
            vmem_limit_bytes=VMEM_LIMIT, dimension_semantics=("arbitrary",)
        ),
        cost_estimate=cost,
    )


def dot(a, b, ca, cb):
    return lax.dot_general(a, b, (((ca,), (cb,)), ((), ())), preferred_element_type=F32)


def shape(dims, dtype):
    return jax.ShapeDtypeStruct(dims, dtype)


def iota(dims, axis):
    return lax.broadcasted_iota(jnp.int32, dims, axis)


def as_f32(mask):
    return jnp.where(mask, 1.0, 0.0).astype(F32)


def stack_base(rows):
    return (KS + 1) * rows


def tap_places(rows):
    width = stack_base(rows) + 256
    q = iota((KS * KS, width), 1)
    base = stack_base(rows)
    w = q % 128 + REACH
    w = jnp.where(w >= 128, w - 128, w)
    row_j = q // 128 * (128 // rows) + w // rows
    row_a = w % rows
    t = q % HALO
    halo_j = (q - base) % 128 // HALO
    upper = q >= base + 128
    halo_a = jnp.where(upper, t + REACH + 1, t - REACH)
    j = jnp.where(q < base, row_j, halo_j)
    a = jnp.where(q < base, row_a, halo_a)
    halo_ok = (upper & (t < REACH)) | ((q < base + 128) & (t >= REACH) & (t < 2 * REACH))
    ok = (j < KS) & (a < KS) & (a >= 0) & ((q < base) | halo_ok)
    return jnp.where(ok, a * KS + j, -1), upper


def split(value):
    high = value.astype(BF16)
    return high, (value - high.astype(F32)).astype(BF16)


def tap_rows(taps, rows, adjoint=None):
    place, upper = tap_places(rows)
    if adjoint is not None:
        keep = (upper & (adjoint != 0)) | (place < 0)
        place = jnp.where(keep, place, KS * KS - 1 - place)
    pick = as_f32(place == iota(place.shape, 0)).astype(BF16)
    high, low = split(taps)
    return dot(high, pick, 1, 0) + dot(low, pick, 1, 0)


def valid_rows(rows):
    q = iota((rows, stack_base(rows)), 1)
    gap = q % rows - iota((rows, stack_base(rows)), 0)
    return (gap >= -REACH) & (gap <= REACH)


def valid_halo():
    r = iota((8, 128), 0)
    q = iota((8, 128), 1)
    t = q % HALO
    inside = q < KS * HALO
    low = (r < REACH) & (t >= REACH) & (t < 2 * REACH) & inside
    up = (r >= 8 - REACH) & (t < REACH) & inside
    return low, up


def tap_matrix(row, rows):
    base = stack_base(rows)
    parts = [
        pltpu.roll(jnp.broadcast_to(row[:, v : v + 128], (rows, 128)), 0, 1, stride=1, stride_axis=0)
        for v in range(0, base, 128)
    ]
    own = jnp.where(valid_rows(rows), jnp.concatenate(parts, axis=1), 0.0)
    low_ok, up_ok = valid_halo()
    low = jnp.broadcast_to(row[:, base : base + 128], (8, 128))
    up = jnp.broadcast_to(row[:, base + 128 :], (8, 128))
    low = jnp.where(low_ok, pltpu.roll(low, 0, 1, stride=1, stride_axis=0), 0.0)
    up = jnp.where(up_ok, pltpu.roll(up, 128 - 7, 1, stride=1, stride_axis=0), 0.0)
    halo = jnp.concatenate([low, jnp.zeros((rows - 16, 128), F32), up], axis=0)
    return jnp.concatenate([own, halo], axis=1)


def tap_sums(m, rows):
    base = stack_base(rows)

    def aligned(v, shift):
        v = pltpu.roll(v, shift % 128, 1, stride=1, stride_axis=0)
        return jnp.sum(v, axis=0, keepdims=True)

    q = iota((rows, base), 1)
    gap = q % rows + iota((rows, base), 0) - (rows - 1)
    own = jnp.where((gap >= -REACH) & (gap <= REACH), m[:, :base], 0.0)
    parts = [aligned(own[:, v : v + 128], 1 - rows) for v in range(0, base, 128)]
    r = iota((8, 128), 0)
    q = iota((8, 128), 1)
    t = q % HALO
    inside = q < KS * HALO
    low_ok = (r >= 8 - REACH) & (t >= REACH) & (t < 2 * REACH) & inside
    up_ok = (r < REACH) & (t < REACH) & inside
    low = jnp.where(low_ok, m[rows - 8 :, base:], 0.0)
    up = jnp.where(up_ok, m[:8, base:], 0.0)
    return jnp.concatenate(parts + [aligned(low, -7), aligned(up, 0)], axis=1)


def shift_stack(own, edge):
    lanes = own.shape[1]
    rows = own.shape[0] - HALO
    lane = iota(own.shape, 1)
    mains, halos = [], []
    for j in range(KS):
        d = j - REACH
        if d == 0:
            s = own
        elif d > 0:
            s = pltpu.roll(jnp.where(lane < d, edge, own), lanes - d, 1)
        else:
            s = pltpu.roll(jnp.where(lane >= lanes + d, edge, own), -d, 1)
        mains.append(s[:rows].astype(BF16))
        halos.append(s[rows:])
    halos.append(jnp.zeros_like(halos[0]))
    pairs = [
        jnp.concatenate([halos[i], halos[i + 1]], axis=0).astype(BF16)
        for i in range(0, KS + 1, 2)
    ]
    gap = jnp.zeros((rows, lanes), BF16)
    rest = jnp.zeros((128 - (KS + 1) * HALO, lanes), BF16)
    return jnp.concatenate(mains + [gap] + pairs + [rest], axis=0)


def stage_halo(north, lat_ref, fold_ref, rb, rh):
    channels, lanes = lat_ref.shape[1], lat_ref.shape[2] // 2
    is_north = north != 0
    for t in range(REACH):
        near = lat_ref[t].astype(F32)
        far = fold_ref[t].astype(F32)
        up = jnp.where(is_north, far, near)
        low = jnp.where(is_north, near, jnp.zeros_like(near))
        rb[pl.ds(t * channels, channels), :] = up[:, :lanes]
        rh[pl.ds(t * channels, channels), :] = up[:, lanes:]
        rb[pl.ds((REACH + t) * channels, channels), :] = low[:, :lanes]
        rh[pl.ds((REACH + t) * channels, channels), :] = low[:, lanes:]
    for t in range(2 * REACH, HALO):
        rb[pl.ds(t * channels, channels), :] = jnp.zeros((channels, lanes), F32)
        rh[pl.ds(t * channels, channels), :] = jnp.zeros((channels, lanes), F32)


def channel_stack(c, first, x_ref, h_ref, rb, rh):
    at = pl.ds(first + c, HALO, stride=rb.shape[0] // HALO)
    own = jnp.concatenate([x_ref[c].astype(F32), rb[at, :]], axis=0)
    edge = jnp.concatenate([h_ref[c].astype(F32), rh[at, :]], axis=0)
    return shift_stack(own, edge)


def lane_edges(cells):
    lanes = cells.shape[1]
    k = iota((2 * HALO, lanes), 0)
    lane = iota((2 * HALO, lanes), 1)
    pick = ((k < REACH) & (lane == k)) | (
        (k >= HALO) & (k < HALO + REACH) & (lane == lanes - REACH + k - HALO)
    )
    return dot(as_f32(pick).astype(BF16), cells, 1, 1)


def pack_kernel(x_ref, lo_ref, hi_ref):
    edges = lane_edges(x_ref[...])
    lo_ref[...] = edges[:HALO].astype(BF16)
    hi_ref[...] = edges[HALO:].astype(BF16)


def unpack_kernel(north_ref, x_ref, east_ref, west_ref, h_ref, lat_ref, fold_ref, xs, hs):
    channels, rows, lanes = x_ref.shape
    k = iota((HALO, lanes), 0)
    lane = iota((HALO, lanes), 1)
    sel_e = as_f32((k < REACH) & (lane == k)).astype(BF16)
    sel_w = as_f32((k < REACH) & (lane == lanes - REACH + k)).astype(BF16)
    sel = jnp.concatenate([sel_e, sel_w], axis=0)
    ed = jnp.concatenate([east_ref[...], west_ref[...]], axis=0)
    hf = dot(ed, sel, 0, 0).reshape(channels, rows, lanes)
    h_ref[...] = hf.astype(BF16)
    g = HALO
    xs[0] = x_ref[:, :16, :].astype(F32)[:, :g].reshape(channels * g, lanes)
    xs[1] = x_ref[:, rows - 16 :, :].astype(F32)[:, 16 - g :].reshape(channels * g, lanes)
    hs[0] = hf[:, :g].reshape(channels * g, lanes)
    hs[1] = hf[:, rows - g :].reshape(channels * g, lanes)
    is_north = north_ref[0] != 0
    rev = as_f32(iota((lanes, lanes), 0) + iota((lanes, lanes), 1) == lanes - 1).astype(BF16)
    for t in range(REACH):
        for part, ref in ((0, xs), (1, hs)):
            bottom = ref.at[0][pl.ds(t, channels, stride=g), :]
            top = ref.at[1][pl.ds(g - REACH + t, channels, stride=g), :]
            span = slice(part * lanes, (part + 1) * lanes)
            lat_ref[t, :, span] = jnp.where(is_north, bottom, top).astype(BF16)
            fold_ref[REACH - 1 - t, :, span] = dot(top.astype(BF16), rev, 1, 0).astype(BF16)


def gelu_parts(hidden):
    k0 = 0.7978845608028654
    k1 = 0.044715 * k0
    sq = hidden * hidden
    th = jnp.tanh(hidden * (k0 + k1 * sq))
    half = 0.5 * th + 0.5
    act = hidden * half
    slope = half + act * (1.0 - th) * (k0 + 3.0 * k1 * sq)
    return act, slope


def main_kernel(
    north_ref, gain_ref, scale_ref, x_ref, h_ref, lat_ref, fold_ref, taps_ref, cot_ref, mask_ref,
    wet_ref, we_ref, wr_ref, wrt_ref,
    out_ref, g_ref, back_ref, low_ref, high_ref, keep_ref, send_ref, sums_ref,
    conv, cots, gs, gr, ms, rb, rh, act_s, hg_s, exp_ref, red_ref, rows_s, gain_s, scale_s,
):
    chunk, rows, lanes = x_ref.shape
    hiddens, channels = wet_ref.shape
    step = pl.program_id(0)

    @pl.when(step == 0)
    def _():
        stage_halo(north_ref[0], lat_ref, fold_ref, rb, rh)
        rows_s[...] = tap_rows(taps_ref[...], rows)

    @pl.when(step < CHUNKS)
    def _():
        first = step * chunk

        def conv_step(k, carry):
            c = first + k
            stack = channel_stack(k, first, x_ref, h_ref, rb, rh)
            high, low = split(tap_matrix(rows_s[pl.ds(c, 1), :], rows))
            both = dot(jnp.concatenate([high, low], axis=0), stack, 1, 0)
            conv[pl.ds(c, rows, stride=channels), :] = both[:rows] + both[rows:]
            wet = mask_ref[...].astype(F32)
            cots[pl.ds(c, rows, stride=channels), :] = cot_ref[k].astype(F32) * wet
            gain_s[pl.ds(c, 1), :] = jnp.full((1, lanes), gain_ref[c])
            scale_s[pl.ds(c, 1), :] = jnp.full((1, lanes), scale_ref[c])
            return carry

        lax.fori_loop(0, chunk, conv_step, 0, unroll=20)

    @pl.when(step == CHUNKS)
    def _():
        cell_work(
            north_ref, wet_ref, we_ref, wr_ref, wrt_ref, keep_ref, send_ref, sums_ref,
            conv, cots, gs, gr, ms, act_s, hg_s, exp_ref, red_ref, gain_s, scale_s, rows,
        )

    @pl.when(step > CHUNKS)
    def _():
        first = (step - CHUNKS - 1) * chunk

        def out_step(k, carry):
            at = pl.multiple_of((first + k) * rows, rows)
            wet = mask_ref[...].astype(F32)
            out_ref[k] = (x_ref[k].astype(F32) + wet * ms[pl.ds(at, rows), :]).astype(BF16)
            g_ref[k] = gs[pl.ds(at, rows), :].astype(BF16)
            back_ref[k] = gr[pl.ds(at, rows), :].astype(BF16)
            return carry

        lax.fori_loop(0, chunk, out_step, 0, unroll=4)
        edges = lane_edges(g_ref[...].reshape(chunk * rows, lanes))
        low_ref[...] = edges[:HALO].astype(BF16)
        high_ref[...] = edges[HALO:].astype(BF16)


def cell_work(
    north_ref, wet_ref, we_ref, wr_ref, wrt_ref, keep_ref, send_ref, sums_ref,
    conv, cots, gs, gr, ms, act_s, hg_s, exp_ref, red_ref, gain_s, scale_s, rows,
):
    hiddens, channels = wet_ref.shape
    lanes = conv.shape[1]
    exp_ref[...] = jnp.zeros_like(exp_ref)
    red_ref[...] = jnp.zeros_like(red_ref)
    sums_ref[...] = jnp.zeros_like(sums_ref)

    def pair(ref, i):
        first = pl.multiple_of(2 * i * channels, 8)
        second = pl.multiple_of((2 * i + 1) * channels, 8)
        return jnp.concatenate(
            [ref[pl.ds(first, channels), :], ref[pl.ds(second, channels), :]], axis=1
        )

    def unpair(ref, i, value):
        ref[pl.ds(2 * i, channels, stride=rows), :] = value[:, :lanes]
        ref[pl.ds(2 * i + 1, channels, stride=rows), :] = value[:, lanes:]

    def cell_step(i, carry):
        gain = jnp.concatenate([gain_s[...]] * 2, axis=1)
        scale = jnp.concatenate([scale_s[...]] * 2, axis=1)
        value = pair(conv, i)
        centred = value - jnp.mean(value, axis=0, keepdims=True)
        inverse = lax.rsqrt(jnp.mean(centred * centred, axis=0, keepdims=True) + 1e-06)
        normalized = centred * inverse
        normed = (normalized * gain).astype(BF16)
        branch = pair(cots, i)
        mixed_grad = (scale * branch).astype(BF16)
        part = 160
        for f in range(0, hiddens, part):
            hidden = dot(wet_ref[f : f + part, :], normed, 1, 0)
            act_grad = dot(wr_ref[f : f + part, :], mixed_grad, 1, 0)
            act, slope = gelu_parts(hidden)
            act_s[f : f + part, :] = act.astype(BF16)
            hg_s[f : f + part, :] = (act_grad * slope).astype(BF16)
        mixed = dot(wrt_ref[...], act_s[...], 1, 0)
        red_ref[...] += dot(act_s[...], mixed_grad, 1, 1)
        normed_grad = dot(we_ref[...], hg_s[...], 1, 0)
        exp_ref[...] += dot(hg_s[...], normed, 1, 1)
        unpair(ms, i, scale * mixed)
        scaled = branch * mixed
        sums_ref[1] += scaled[:, :lanes] + scaled[:, lanes:]
        gained = normed_grad * normalized
        sums_ref[0] += gained[:, :lanes] + gained[:, lanes:]
        unit = normed_grad * gain
        m1 = jnp.mean(unit, axis=0, keepdims=True)
        m2 = jnp.mean(unit * normalized, axis=0, keepdims=True)
        grad = inverse * (unit - m1 - normalized * m2)
        unpair(gs, i, grad)
        gr[pl.ds(rows - 1 - 2 * i, channels, stride=rows), :] = grad[:, :lanes]
        gr[pl.ds(rows - 2 - 2 * i, channels, stride=rows), :] = grad[:, lanes:]
        return carry

    lax.fori_loop(0, rows // 2, cell_step, 0)

    is_north = north_ref[0] != 0
    expand, reduce = exp_ref[...], red_ref[...]
    blank = jnp.zeros((hiddens, 2 * lanes - channels), F32)
    keep_ref[...] = jnp.concatenate([jnp.where(is_north, reduce, expand), blank], axis=1)
    send = jnp.concatenate([jnp.where(is_north, expand, reduce), blank], axis=1)
    send_ref[...] = send.astype(BF16)


def tap_kernel(start, north_ref, x_ref, h_ref, lat_ref, fold_ref, back_ref, sums_ref, small_ref, rb, rh, rows_s):
    chunk, rows, lanes = x_ref.shape
    first = (pl.program_id(0) + start) * chunk

    @pl.when(pl.program_id(0) == 0)
    def _():
        stage_halo(north_ref[0], lat_ref, fold_ref, rb, rh)

    def step(k, carry):
        stack = channel_stack(k, first, x_ref, h_ref, rb, rh)
        rows_s[pl.ds(k, 1), :] = tap_sums(dot(back_ref[k], stack, 1, 1), rows)
        return carry

    lax.fori_loop(0, chunk, step, 0, unroll=20)
    place, _ = tap_places(rows)
    pick = as_f32(place == iota(place.shape, 0))
    pick = jnp.concatenate([pick, jnp.zeros((lanes - KS * KS, pick.shape[1]), F32)], axis=0)
    pick = pick.astype(BF16)
    high, low = split(rows_s[...])
    lane = iota((chunk, lanes), 1)
    small = dot(high, pick, 1, 1) + dot(low, pick, 1, 1)
    for i in range(2):
        total = jnp.sum(sums_ref[i], axis=1, keepdims=True)
        small = jnp.where(lane == KS * KS + i, total, small)
    small_ref[...] = small


def adjoint_kernel(start, north_ref, g_ref, h_ref, lat_ref, fold_ref, taps_ref, cot_ref, *refs):
    out_ref, rb, rh, rows_s = refs[-4:]
    chunk, rows, lanes = g_ref.shape
    first = (pl.program_id(0) + start) * chunk

    @pl.when(pl.program_id(0) == 0)
    def _():
        stage_halo(north_ref[0], lat_ref, fold_ref, rb, rh)
        rows_s[...] = tap_rows(taps_ref[...], rows, north_ref[0])

    def step(k, carry):
        stack = channel_stack(k, first, g_ref, h_ref, rb, rh)
        matrix = tap_matrix(rows_s[pl.ds(first + k, 1), :], rows).astype(BF16)
        out_ref[k] = (cot_ref[k].astype(F32) + dot(matrix, stack, 1, 0)).astype(BF16)
        return carry

    lax.fori_loop(0, chunk, step, 0, unroll=20)


def lon_edges(low, high):
    n = lax.axis_size("lon")
    east = lax.ppermute(low, "lon", [((i + 1) % n, i) for i in range(n)])
    west = lax.ppermute(high, "lon", [(i, (i + 1) % n) for i in range(n)])
    return east, west


def halo_rows(field, east, west, north):
    channels, rows, lanes = field.shape
    n, m = lax.axis_size("lon"), lax.axis_size("lat")
    msg = shape((REACH, channels, 2 * lanes), BF16)
    lane_halo, lat_msg, fold_msg = call(
        unpack_kernel,
        (shape(field.shape, BF16), msg, msg),
        scratch=[pltpu.VMEM((2, channels * HALO, lanes), F32)] * 2,
        n_smem=1,
        n_in=4,
        cost=cost(3),
    )(north, field, east, west)
    fold_rows = lax.ppermute(
        fold_msg, ("lon", "lat"), [(i * m + m - 1, (n - 1 - i) * m + m - 1) for i in range(n)]
    )
    lat_rows = lax.ppermute(lat_msg, "lat", [(0, 1), (1, 0)])
    return lane_halo, lat_rows, fold_rows


def cost(micros):
    return pl.CostEstimate(flops=int(micros * 1e9), bytes_accessed=int(micros * 3e6), transcendentals=0)


def split_half(buf, bit):
    rows, lanes = buf.shape
    if (rows // 2) % 8 and lanes > 128:
        first, second = buf[:, : lanes // 2], buf[:, lanes // 2 :]
    else:
        first, second = buf[: rows // 2], buf[rows // 2 :]
    up = bit != 0
    return jnp.where(up, second, first), jnp.where(up, first, second)


def join_half(mine, other, bit, dims):
    up = bit != 0
    first, second = jnp.where(up, other, mine), jnp.where(up, mine, other)
    return jnp.concatenate([first, second], axis=1 if mine.shape[0] == dims[0] else 0)


def partner(value, axis, b):
    return lax.ppermute(value, axis, [(i, i ^ (1 << b)) for i in range(lax.axis_size(axis))])


def lon_bits():
    return range(lax.axis_size("lon").bit_length() - 1)


def both_sum(value, axis, b):
    mine = value.astype(BF16)
    return mine.astype(F32) + partner(mine, axis, b).astype(F32)


def together(*values):
    return lax.optimization_barrier(values)


def on_device(
    ocean_state, cotangent, kernel, norm_gain, expand_weight, reduce_weight, layer_scale, land_mask
):
    channels, rows, lanes = ocean_state.shape
    hiddens = expand_weight.shape[1]
    width = stack_base(rows) + 256
    is_north = lax.axis_index("lat") == lax.axis_size("lat") - 1
    north = is_north.astype(jnp.int32).reshape(1)
    edge = shape((HALO, channels * rows), BF16)
    field = shape(ocean_state.shape, BF16)
    rowbuf = pltpu.VMEM((HALO * channels, lanes), F32)
    cellbuf = pltpu.VMEM((channels * rows, lanes), F32)
    tapbuf = pltpu.VMEM((channels, width), F32)
    hidbuf = pltpu.VMEM((hiddens, 2 * lanes), BF16)
    gradbuf = pltpu.VMEM((hiddens, channels), F32)
    lanebuf = pltpu.VMEM((channels, lanes), F32)

    low, high = call(pack_kernel, (edge, edge), n_in=1, cost=cost(2))(
        ocean_state.reshape(channels * rows, lanes)
    )
    east, west = lon_edges(low, high)
    halo, lat_rows, fold_rows = halo_rows(ocean_state, east, west, north)

    chunk = channels // CHUNKS
    whole = vmem()

    def block(index):
        return pl.BlockSpec((chunk, rows, lanes), lambda i: (index(i), 0, 0))

    def into(i):
        return jnp.minimum(i, CHUNKS - 1)

    def back_out(i):
        return jnp.maximum(i - CHUNKS - 1, 0)

    def both_ways(i):
        return jnp.where(i <= CHUNKS, into(i), back_out(i))

    edge_block = pl.BlockSpec((HALO, chunk * rows), lambda i: (0, back_out(i)))
    block_out, conv_grad, back_grad, g_low, g_high, keep, send, sums = grid_call(
        main_kernel,
        2 * CHUNKS + 1,
        (
            field,
            field,
            field,
            edge,
            edge,
            shape((hiddens, 2 * lanes), F32),
            shape((hiddens, 2 * lanes), BF16),
            shape((2, channels, lanes), F32),
        ),
        [smem()] * 3 + [block(both_ways), block(into), whole, whole, whole, block(into)] + [whole] * 5,
        [block(back_out)] * 3 + [edge_block] * 2 + [whole] * 3,
        [cellbuf] * 5 + [rowbuf] * 2 + [hidbuf] * 2 + [gradbuf] * 2 + [tapbuf] + [lanebuf] * 2,
        cost(40),
    )(
        north, norm_gain, layer_scale, ocean_state, halo, lat_rows, fold_rows, kernel, cotangent,
        land_mask, expand_weight.T, expand_weight, reduce_weight, reduce_weight.T,
    )

    def taps_part(start, count, field, back):
        here = block(lambda i: i + start)
        return grid_call(
            functools.partial(tap_kernel, start),
            count,
            shape((count * chunk, lanes), F32),
            [smem(), here, here, whole, whole, here]
            + [pl.BlockSpec((2, chunk, lanes), lambda i: (0, i + start, 0))],
            pl.BlockSpec((chunk, lanes), lambda i: (i, 0)),
            [rowbuf] * 2 + [pltpu.VMEM((chunk, width), F32)],
            cost(3 * count),
        )(north, field, halo, lat_rows, fold_rows, back, sums)

    def adjoint_part(start, count, grad, lane_halo, previous):
        here = block(lambda i: i + start)
        extra = () if previous is None else (previous,)
        return grid_call(
            functools.partial(adjoint_kernel, start),
            count,
            shape(ocean_state.shape, BF16),
            [smem(), here, here, whole, whole, whole, here]
            + [pl.BlockSpec(memory_space=pl.ANY)] * len(extra),
            here,
            [rowbuf] * 2 + [tapbuf],
            cost(2 * count),
            {7: 0} if extra else None,
        )(north, grad, lane_halo, g_lat, g_fold, kernel, cotangent, *extra)

    bits = list(lon_bits())
    first_part = (CHUNKS + 1) // 2

    def side(b):
        return (lax.axis_index("lon") >> b) & 1

    g_east, g_west = lon_edges(g_low, g_high)
    buf = keep + partner(send, "lat", 0).astype(F32)
    sizes, parts = [], []
    back = back_grad
    for b in bits:
        sizes.append(buf.shape)
        stay, go = split_half(buf, side(b))
        got = partner(go.astype(BF16), "lon", b)
        if len(parts) < 2:
            start = len(parts) * first_part
            count = CHUNKS - first_part if parts else first_part
            parts.append(taps_part(start, count, ocean_state, back))
            got, back = together(got, parts[-1], back)[::2]
        buf = stay + got.astype(F32)
    small = jnp.concatenate(parts, axis=0)
    g_halo, g_lat, g_fold = halo_rows(conv_grad, g_east, g_west, north)
    buf = buf.astype(BF16)
    state_grad = None
    done = 0
    grad = conv_grad
    for n, b in enumerate(bits[::-1]):
        got = partner(buf, "lon", b)
        small = both_sum(small, "lon", b)
        if n > 0 and done < CHUNKS:
            count = min(2, CHUNKS - done)
            state_grad = adjoint_part(done, count, grad, g_halo, state_grad)
            done += count
            got, state_grad, grad = together(got, state_grad, grad)
        buf = join_half(buf, got, side(b), sizes[len(bits) - 1 - n])
    if done < CHUNKS:
        state_grad = adjoint_part(done, CHUNKS - done, grad, g_halo, state_grad)
    other = partner(buf, "lat", 0)
    small = both_sum(small, "lat", 0)
    expand = jnp.where(is_north, other, buf)[:, :channels].astype(F32)
    reduce = jnp.where(is_north, buf, other)[:, :channels].astype(F32)
    kernel_grad = small[:, : KS * KS]
    gain_grad = small[:, KS * KS]
    scale_grad = small[:, KS * KS + 1]
    return (block_out, state_grad, kernel_grad, gain_grad, expand.T, reduce, scale_grad)


def solution(mesh):
    tiles = P(None, ("members", "lat"), "lon")
    return jax.shard_map(
        on_device,
        mesh=mesh,
        in_specs=(tiles, tiles, P(), P(), P(), P(), P(), P("lat", "lon")),
        out_specs=(
            tiles, tiles, P("members", None), P("members"), P("members", None),
            P("members", None), P("members"),
        ),
        check_vma=False,
    )
```

time: 241 us -> 148 us (0.61)
  Pallas kernels: 150 us -> 84.5 us
  local copies, waits for them, and re-layouts: 23.1 us -> 9.23 us
  waiting for transfers between devices: 32 us -> 22.1 us
  other arithmetic: 6.49 us -> 2.34 us
    pallas_call x8 -> x9, Pallas kernels: 150 us -> 84.5 us  [the longest x1 44.1 us: on_device(): grid_call(main_kernel, 2 * CHUNKS + 1, (field, field, field, edge, edge,...]
    ppermute x16 -> x20, waiting for transfers between devices: 32 us -> 22.1 us  [the longest x2 11.3 us: halo_rows(): lax.ppermute(fold_msg, ('lon', 'lat'), [(i * m + m - 1, (n - 1 - i) * m +...]
    reshape x10 -> x0, local copies, waits for them, and re-layouts: 6.07 us -> none  [the longest x2 3.15 us: stack_taps(): main = jnp.repeat(taps, rows, axis=2)]
    concatenate x3 -> x1, other arithmetic: 3.88 us -> 0.01 us  [on_device(): small = jnp.concatenate(parts, axis=0)]
    another operation x2 -> x0, local copies, waits for them, and re-layouts: 2.97 us -> none  [stack_taps(): halo = halo.reshape(taps.shape[0], KS, KS * HALO)]
    unnamed x39 -> x30, local copies, waits for them, and re-layouts: 10.7 us -> 8.43 us
    ppermute x16 -> x20, starting transfers between devices: 28.1 us -> 28.5 us  [the longest x12 12 us: partner(): lax.ppermute(value, axis, [(i, i ^ 1 << b) for i in range(lax.axis_size(a...]
  transfers between devices with their start and end apart: 16 -> 20, of which waited for: 7 -> 8; matrix products, arithmetic and copies ran while one was open for 8% -> 4% of each run, Pallas kernels for 21% -> 23%
where the time goes in v2:
time: 148 us; the launch traced here: 147 us
  Pallas kernels  84.5 us (57%)
  starting transfers between devices  28.5 us (19%)
  waiting for transfers between devices  22.1 us (15%)
  local copies, waits for them, and re-layouts  9.23 us (6%)
  other arithmetic  2.34 us (2%)
    pallas_call x1, Pallas kernels, on_device(): grid_call(main_kernel, 2 * CHUNKS + 1, (field, field, field, edge, edge,...  44.1 us
    pallas_call x2, Pallas kernels, taps_part(): grid_call(functools.partial(tap_kernel, start), count, shape((count * chu...  15.7 us
    pallas_call x3, Pallas kernels, adjoint_part(): grid_call(functools.partial(adjoint_kernel, start), count, shape(ocean_st...  14.1 us
    ppermute x12, starting transfers between devices, partner(): lax.ppermute(value, axis, [(i, i ^ 1 << b) for i in range(lax.axis_size(a...  12 us
    ppermute x2, waiting for transfers between devices, halo_rows(): lax.ppermute(fold_msg, ('lon', 'lat'), [(i * m + m - 1, (n - 1 - i) * m +...  11.3 us
    unnamed x30, local copies, waits for them, and re-layouts  8.43 us
    pallas_call x2, Pallas kernels, halo_rows(): call(unpack_kernel, (shape(field.shape, BF16), msg, msg), scratch=[pltpu....  7.79 us
    ppermute x2, starting transfers between devices, halo_rows(): lax.ppermute(fold_msg, ('lon', 'lat'), [(i * m + m - 1, (n - 1 - i) * m +...  6.79 us
  transfers between devices with their start and end apart: 20, of which 8 were waited for; matrix products, arithmetic and copies ran while one was open for 4% of the time, Pallas kernels for 23%

profile of v2, /device:TPU:1, one launch (start us, length us, event | category | flops | bytes accessed | tf_op | source)
XLA Modules:
  0.0 147.5 jit_solution(12287138478047901038)
XLA Ops:
  0.6 2.7 %shard_map.135 = (bf16[8,6400]{1,0:T(8,128)(2,1)}, bf16[8,6400]{1,0:T(8,128)(2,1)}) custom-call(bf16[6400,128]{1,0:T(8,128)(2,1)} %bitcast.10), custom_call_target="tpu_custom_call" | custom-call | flops 2000000000 | bytes 6000000 | tf_op jit(solution)/shard_map/pallas_call | solution.py:515
  3.3 5.1 %collective-permute-start = (bf16[8,6400]{1,0:T(8,128)(2,1)}, bf16[8,6400]{1,0:T(8,128)(2,1)S(1)}, u32[]{:S(2)}, u32[]{:S(2)}) collective-permute-start(bf16[8,6400]{1,0:T(8,128)(2,1)} %get-tuple-element.32), channel_id=1, source_target_pairs={{2,0},{4,2},{6,4},{8,6},{10,8},{12,10},{14,12},{0,14},{3,1},{5,3},... | collective-permute-start | bytes 307208 | tf_op jit(solution)/shard_map/ppermute | solution.py:437
  8.4 2.0 %collective-permute-done.east_ref = bf16[8,6400]{1,0:T(8,128)(2,1)S(1)} collective-permute-done((bf16[8,6400]{1,0:T(8,128)(2,1)}, bf16[8,6400]{1,0:T(8,128)(2,1)S(1)}, u32[]{:S(2)}, u32[]{:S(2)}) %collective-permute-start) | collective-permute-done | bytes 102432 | tf_op jit(solution)/shard_map/ppermute | solution.py:437
  10.4 4.4 %collective-permute-done.1.west_ref = bf16[8,6400]{1,0:T(8,128)(2,1)S(1)} collective-permute-done((bf16[8,6400]{1,0:T(8,128)(2,1)}, bf16[8,6400]{1,0:T(8,128)(2,1)S(1)}, u32[]{:S(2)}, u32[]{:S(2)}) %collective-permute-start.1) | collective-permute-done | bytes 102432 | tf_op jit(solution)/shard_map/ppermute | solution.py:438
  15.5 3.9 %shard_map.136 = (bf16[200,32,128]{2,1,0:T(8,128)(2,1)}, bf16[3,200,256]{2,1,0:T(8,128)(2,1)}, bf16[3,200,256]{2,1,0:T(8,128)(2,1)}) custom-call(s32[1]{0:T(128)} %bitcast.north_ref, bf16[200,32,128]{2,1,0:T(8,128)(2,1)} %x_ref.7, bf16[8,6400]{1,0:T(8,128)(2,1)} %copy-done.8, bf16[8,6400]{1,0:T(8,128)(2,1)} %copy-done.9), custom_call_target="tpu_custom_call" | custom-call | flops 3000000000 | bytes 9000000 | tf_op jit(solution)/shard_map/pallas_call | solution.py:446
  19.4 2.1 %collective-permute-start.2 = (bf16[3,200,256]{2,1,0:T(8,128)(2,1)}, bf16[3,200,256]{2,1,0:T(8,128)(2,1)S(1)}, u32[]{:S(2)}, u32[]{:S(2)}) collective-permute-start(bf16[3,200,256]{2,1,0:T(8,128)(2,1)} %get-tuple-element.35), channel_id=1, source_target_pairs={{0,1},{1,0},{2,3},{3,2},{4,5},{5,4},{6,7},{7,6},{8,9},{9,8},{10,11... | collective-permute-start | bytes 921608 | tf_op jit(solution)/shard_map/ppermute | solution.py:457
  21.5 1.9 %collective-permute-start.3 = (bf16[3,200,256]{2,1,0:T(8,128)(2,1)}, bf16[3,200,256]{2,1,0:T(8,128)(2,1)S(1)}, u32[]{:S(2)}, u32[]{:S(2)}) collective-permute-start(bf16[3,200,256]{2,1,0:T(8,128)(2,1)} %get-tuple-element.36), channel_id=1, source_target_pairs={{1,15},{3,13},{5,11},{7,9},{9,7},{11,5},{13,3},{15,1},{17,31},{19,... | collective-permute-start | bytes 921608 | tf_op jit(solution)/shard_map/ppermute | solution.py:454
  26.0 5.9 %collective-permute-done.3.fold_ref = bf16[3,200,256]{2,1,0:T(8,128)(2,1)S(1)} collective-permute-done((bf16[3,200,256]{2,1,0:T(8,128)(2,1)}, bf16[3,200,256]{2,1,0:T(8,128)(2,1)S(1)}, u32[]{:S(2)}, u32[]{:S(2)}) %collective-permute-start.3) | collective-permute-done | bytes 307232 | tf_op jit(solution)/shard_map/ppermute | solution.py:454
  32.7 44.1 %shard_map.137 = (bf16[200,32,128]{2,1,0:T(8,128)(2,1)}, bf16[200,32,128]{2,1,0:T(8,128)(2,1)}, bf16[200,32,128]{2,1,0:T(8,128)(2,1)}, bf16[8,6400]{1,0:T(8,128)...) custom-call(s32[1]{0:T(128)} %bitcast.north_ref, ...), custom_call_target="tpu_custom_call" | custom-call | flops 40000000000 | bytes 120000000 | tf_op jit(solution)/shard_map/pallas_call | solution.py:537
  77.1 1.4 collective-permute-start.11
  78.4 9.0 %shard_map.138 = f32[120,128]{1,0:T(8,128)} custom-call(s32[1]{0:T(128)} %bitcast.north_ref, bf16[200,32,128]{2,1,0:T(8,128)(2,1)} %x_ref.7, bf16[200,32,128]{2,1,0:T(8,128)(2,1)} %get-tuple-element.34.h_ref, bf16[3,200,256]{2,1,0:T(8,128)(2,1)} %copy-done.6, bf16[3,200,256]{2,1,0:T(8,128)(2,1)} %copy-done.7, ...), custom_call_target="tpu_custom_call" | custom-call | flops 8999999488 | bytes 27000000 | tf_op jit(solution)/shard_map/pallas_call | solution.py:561
  89.0 3.9 %shard_map.140 = (bf16[200,32,128]{2,1,0:T(8,128)(2,1)}, bf16[3,200,256]{2,1,0:T(8,128)(2,1)}, bf16[3,200,256]{2,1,0:T(8,128)(2,1)}) custom-call(s32[1]{0:T(128)} %bitcast.north_ref, bf16[200,32,128]{2,1,0:T(8,128)(2,1)} %get-tuple-element.54.x_ref.g_ref, bf16[8,6400]{1,0:T(8,128)(2,1)} %copy-done.10, bf16[8,6400]{1,0:T(8,128)(2,1)} %copy-done.11), custom_call_target="tpu_custom_call" | custom-call | flops 3000000000 | bytes 9000000 | tf_op jit(solution)/shard_map/pallas_call | solution.py:446
  93.9 4.9 %collective-permute-start.13 = (bf16[3,200,256]{2,1,0:T(8,128)(2,1)}, bf16[3,200,256]{2,1,0:T(8,128)(2,1)S(1)}, u32[]{:S(2)}, u32[]{:S(2)}) collective-permute-start(bf16[3,200,256]{2,1,0:T(8,128)(2,1)} %get-tuple-element.50), channel_id=1, source_target_pairs={{1,15},{3,13},{5,11},{7,9},{9,7},{11,5},{13,3},{15,1},{17,31},{19,... | collective-permute-start | bytes 921608 | tf_op jit(solution)/shard_map/ppermute | solution.py:454
  99.1 5.4 %collective-permute-done.13.fold_ref = bf16[3,200,256]{2,1,0:T(8,128)(2,1)S(1)} collective-permute-done((bf16[3,200,256]{2,1,0:T(8,128)(2,1)}, bf16[3,200,256]{2,1,0:T(8,128)(2,1)S(1)}, u32[]{:S(2)}, u32[]{:S(2)}) %collective-permute-start.13) | collective-permute-done | bytes 307232 | tf_op jit(solution)/shard_map/ppermute | solution.py:454
  105.2 5.2 %shard_map.141.refs_0_ = bf16[200,32,128]{2,1,0:T(8,128)(2,1)} custom-call(s32[1]{0:T(128)} %bitcast.north_ref, bf16[200,32,128]{2,1,0:T(8,128)(2,1)} %get-tuple-element.54.x_ref.g_ref, bf16[200,32,128]{2,1,0:T(8,128)(2,1)} %get-tuple-element.48.h_ref, bf16[3,200,256]{2,1,0:T(8,128)(2,1)} %copy-done.3, bf16[3,200,256]{2,1,0:T(8,128)(2,1)} %copy-done.4, ...), custom_call_target="tpu_custom_call" | custom-call | flops 4000000000 | bytes 12000000 | tf_op jit(solution)/shard_map/pallas_call | solution.py:575
  110.5 6.7 %shard_map.139 = f32[80,128]{1,0:T(8,128)} custom-call(s32[1]{0:T(128)} %bitcast.north_ref, bf16[200,32,128]{2,1,0:T(8,128)(2,1)} %x_ref.7, bf16[200,32,128]{2,1,0:T(8,128)(2,1)} %get-tuple-element.34.h_ref, bf16[3,200,256]{2,1,0:T(8,128)(2,1)} %copy-done.6, bf16[3,200,256]{2,1,0:T(8,128)(2,1)} %copy-done.7, ...), custom_call_target="tpu_custom_call" | custom-call | flops 6000000000 | bytes 18000000 | tf_op jit(solution)/shard_map/pallas_call | solution.py:561
  118.6 2.0 %collective-permute-start.7 = (bf16[200,128]{1,0:T(8,128)(2,1)S(1)}, bf16[200,128]{1,0:T(8,128)(2,1)S(1)}, u32[]{:S(2)}, u32[]{:S(2)}) collective-permute-start(bf16[200,128]{1,0:T(8,128)(2,1)S(1)} %select_convert_fusion.3), channel_id=1, source_target_pairs={{0,8},{2,10},{4,12},{6,14},{8,0},{10,2},{12,4},{14,6},{1,9},{3,11}... | collective-permute-start | bytes 153608 | tf_op jit(solution)/shard_map/ppermute | solution.py:482
  120.6 1.4 collective-permute-done.15
  122.0 2.0 %collective-permute-start.16 = (bf16[200,128]{1,0:T(8,128)(2,1)S(1)}, bf16[200,128]{1,0:T(8,128)(2,1)S(1)}, u32[]{:S(2)}, u32[]{:S(2)}) collective-permute-start(bf16[200,128]{1,0:T(8,128)(2,1)S(1)} %add_convert_fusion.2), channel_id=1, source_target_pairs={{0,4},{2,6},{4,0},{6,2},{8,12},{10,14},{12,8},{14,10},{1,5},{3,7},... | collective-permute-start | bytes 153608 | tf_op jit(solution)/shard_map/ppermute | solution.py:482
  125.5 2.9 %collective-permute-start.17 = (bf16[200,128]{1,0:T(8,128)(2,1)S(1)}, bf16[200,128]{1,0:T(8,128)(2,1)S(1)}, u32[]{:S(2)}, u32[]{:S(2)}) collective-permute-start(bf16[200,128]{1,0:T(8,128)(2,1)S(1)} %add_convert_fusion.1), channel_id=1, source_target_pairs={{0,2},{2,0},{4,6},{6,4},{8,10},{10,8},{12,14},{14,12},{1,3},{3,1},... | collective-permute-start | bytes 153608 | tf_op jit(solution)/shard_map/ppermute | solution.py:482
  130.1 2.0 %collective-permute-done.9 = bf16[200,256]{1,0:T(8,128)(2,1)S(1)} collective-permute-done((bf16[200,256]{1,0:T(8,128)(2,1)S(1)}, bf16[200,256]{1,0:T(8,128)(2,1)S(1)}, u32[]{:S(2)}, u32[]{:S(2)}) %collective-permute-start.9) | collective-permute-done | bytes 102432 | tf_op jit(solution)/shard_map/ppermute | solution.py:482
  132.1 2.2 %collective-permute-start.14 = (bf16[400,256]{1,0:T(8,128)(2,1)S(1)}, bf16[400,256]{1,0:T(8,128)(2,1)S(1)}, u32[]{:S(2)}, u32[]{:S(2)}) collective-permute-start(bf16[400,256]{1,0:T(8,128)(2,1)S(1)} %pad_maximum_fusion.1), channel_id=1, source_target_pairs={{0,2},{2,0},{4,6},{6,4},{8,10},{10,8},{12,14},{14,12},{1,3},{3,1},... | collective-permute-start | bytes 614408 | tf_op jit(solution)/shard_map/ppermute | solution.py:482
  134.3 5.2 %shard_map.142.refs_0_ = bf16[200,32,128]{2,1,0:T(8,128)(2,1)} custom-call(s32[1]{0:T(128)} %bitcast.north_ref, bf16[200,32,128]{2,1,0:T(8,128)(2,1)} %get-tuple-element.54.x_ref.g_ref, bf16[200,32,128]{2,1,0:T(8,128)(2,1)} %get-tuple-element.48.h_ref, bf16[3,200,256]{2,1,0:T(8,128)(2,1)} %copy-done.3, ...), custom_call_target="tpu_custom_call", output_to_operand_aliasing={{}: (7, {})} | custom-call | flops 4000000000 | bytes 12000000 | tf_op jit(solution)/shard_map/pallas_call | solution.py:575
  141.3 3.8 %shard_map.143 = bf16[200,32,128]{2,1,0:T(8,128)(2,1)} custom-call(s32[1]{0:T(128)} %bitcast.north_ref, bf16[200,32,128]{2,1,0:T(8,128)(2,1)} %get-tuple-element.54.x_ref.g_ref, bf16[200,32,128]{2,1,0:T(8,128)(2,1)} %get-tuple-element.48.h_ref, bf16[3,200,256]{2,1,0:T(8,128)(2,1)} %copy-done.3, ...), custom_call_target="tpu_custom_call", output_to_operand_aliasing={{}: (7, {})} | custom-call | flops 2000000000 | bytes 6000000 | tf_op jit(solution)/shard_map/pallas_call | solution.py:575
  (77 shorter events, 16.6 us)
Async XLA Ops:
  3.3 7.1 %collective-permute-start = (bf16[8,6400]{1,0:T(8,128)(2,1)}, bf16[8,6400]{1,0:T(8,128)(2,1)S(1)}, u32[]{:S(2)}, u32[]{:S(2)}) collective-permute-start(bf16[8,6400]{1,0:T(8,128)(2,1)} %get-tuple-element.32), channel_id=1, source_target_pairs={{2,0},{4,2},{6,4},{8,6},{10,8},{12,10},{14,12},{0,14},{3,1},{5,3},... | collective-permute-start | bytes 307208 | tf_op jit(solution)/shard_map/ppermute | solution.py:437
  8.4 6.4 %collective-permute-start.1 = (bf16[8,6400]{1,0:T(8,128)(2,1)}, bf16[8,6400]{1,0:T(8,128)(2,1)S(1)}, u32[]{:S(2)}, u32[]{:S(2)}) collective-permute-start(bf16[8,6400]{1,0:T(8,128)(2,1)} %get-tuple-element.33), channel_id=1, source_target_pairs={{0,2},{2,4},{4,6},{6,8},{8,10},{10,12},{12,14},{14,0},{1,3},{3,5},... | collective-permute-start | bytes 307208 | tf_op jit(solution)/shard_map/ppermute | solution.py:438
  15.5 7.9 %copy-start.5 = (f32[200,49]{0,1:T(8,128)S(1)}, f32[200,49]{0,1:T(8,128)}, u32[]{:S(2)}) copy-start(f32[200,49]{0,1:T(8,128)} %param.10) | copy-start | bytes 117604
  15.5 8.7 %copy-start.1 = (bf16[200,800]{1,0:T(8,128)(2,1)S(1)}, bf16[200,800]{1,0:T(8,128)(2,1)}, u32[]{:S(2)}) copy-start(bf16[200,800]{1,0:T(8,128)(2,1)} %we_ref.1) | copy-start | bytes 960004
  15.5 9.6 %copy-start.2 = (bf16[800,200]{0,1:T(8,128)(2,1)S(1)}, bf16[800,200]{0,1:T(8,128)(2,1)}, u32[]{:S(2)}) copy-start(bf16[800,200]{0,1:T(8,128)(2,1)} %param.13) | copy-start | bytes 960004
  19.4 6.7 %collective-permute-start.2 = (bf16[3,200,256]{2,1,0:T(8,128)(2,1)}, bf16[3,200,256]{2,1,0:T(8,128)(2,1)S(1)}, u32[]{:S(2)}, u32[]{:S(2)}) collective-permute-start(bf16[3,200,256]{2,1,0:T(8,128)(2,1)} %get-tuple-element.35), channel_id=1, source_target_pairs={{0,1},{1,0},{2,3},{3,2},{4,5},{5,4},{6,7},{7,6},{8,9},{9,8},{10,11... | collective-permute-start | bytes 921608 | tf_op jit(solution)/shard_map/ppermute | solution.py:457
  21.5 10.5 %collective-permute-start.3 = (bf16[3,200,256]{2,1,0:T(8,128)(2,1)}, bf16[3,200,256]{2,1,0:T(8,128)(2,1)S(1)}, u32[]{:S(2)}, u32[]{:S(2)}) collective-permute-start(bf16[3,200,256]{2,1,0:T(8,128)(2,1)} %get-tuple-element.36), channel_id=1, source_target_pairs={{1,15},{3,13},{5,11},{7,9},{9,7},{11,5},{13,3},{15,1},{17,31},{19,... | collective-permute-start | bytes 921608 | tf_op jit(solution)/shard_map/ppermute | solution.py:454
  76.8 22.0 %collective-permute-start.4 = (bf16[800,256]{1,0:T(8,128)(2,1)}, bf16[800,256]{1,0:T(8,128)(2,1)S(1)}, u32[]{:S(2)}, u32[]{:S(2)}) collective-permute-start(bf16[800,256]{1,0:T(8,128)(2,1)} %get-tuple-element.39), channel_id=1, source_target_pairs={{0,1},{1,0},{2,3},{3,2},{4,5},{5,4},{6,7},{7,6},{8,9},{9,8},{10,11... | collective-permute-start | bytes 1228808 | tf_op jit(solution)/shard_map/ppermute | solution.py:482
  76.9 11.4 %collective-permute-start.10 = (bf16[8,6400]{1,0:T(8,128)(2,1)}, bf16[8,6400]{1,0:T(8,128)(2,1)S(1)}, u32[]{:S(2)}, u32[]{:S(2)}) collective-permute-start(bf16[8,6400]{1,0:T(8,128)(2,1)} %get-tuple-element.46), channel_id=1, source_target_pairs={{2,0},{4,2},{6,4},{8,6},{10,8},{12,10},{14,12},{0,14},{3,1},{5,3},... | collective-permute-start | bytes 307208 | tf_op jit(solution)/shard_map/ppermute | solution.py:437
  77.1 11.2 %collective-permute-start.11 = (bf16[8,6400]{1,0:T(8,128)(2,1)}, bf16[8,6400]{1,0:T(8,128)(2,1)S(1)}, u32[]{:S(2)}, u32[]{:S(2)}) collective-permute-start(bf16[8,6400]{1,0:T(8,128)(2,1)} %get-tuple-element.47), channel_id=1, source_target_pairs={{0,2},{2,4},{4,6},{6,8},{8,10},{10,12},{12,14},{14,0},{1,3},{3,5},... | collective-permute-start | bytes 307208 | tf_op jit(solution)/shard_map/ppermute | solution.py:438
  89.0 9.8 %copy-start = (f32[800,256]{1,0:T(8,128)S(1)}, f32[800,256]{1,0:T(8,128)}, u32[]{:S(2)}) copy-start(f32[800,256]{1,0:T(8,128)} %get-tuple-element.38) | copy-start | bytes 2457604
  92.9 6.2 %collective-permute-start.12 = (bf16[3,200,256]{2,1,0:T(8,128)(2,1)}, bf16[3,200,256]{2,1,0:T(8,128)(2,1)S(1)}, u32[]{:S(2)}, u32[]{:S(2)}) collective-permute-start(bf16[3,200,256]{2,1,0:T(8,128)(2,1)} %get-tuple-element.49), channel_id=1, source_target_pairs={{0,1},{1,0},{2,3},{3,2},{4,5},{5,4},{6,7},{7,6},{8,9},{9,8},{10,11... | collective-permute-start | bytes 921608 | tf_op jit(solution)/shard_map/ppermute | solution.py:457
  93.9 10.6 %collective-permute-start.13 = (bf16[3,200,256]{2,1,0:T(8,128)(2,1)}, bf16[3,200,256]{2,1,0:T(8,128)(2,1)S(1)}, u32[]{:S(2)}, u32[]{:S(2)}) collective-permute-start(bf16[3,200,256]{2,1,0:T(8,128)(2,1)} %get-tuple-element.50), channel_id=1, source_target_pairs={{1,15},{3,13},{5,11},{7,9},{9,7},{11,5},{13,3},{15,1},{17,31},{19,... | collective-permute-start | bytes 921608 | tf_op jit(solution)/shard_map/ppermute | solution.py:454
  99.0 11.4 %collective-permute-start.5 = (bf16[400,256]{1,0:T(8,128)(2,1)S(1)}, bf16[400,256]{1,0:T(8,128)(2,1)S(1)}, u32[]{:S(2)}, u32[]{:S(2)}) collective-permute-start(bf16[400,256]{1,0:T(8,128)(2,1)S(1)} %select_convert_fusion.1), channel_id=1, source_target_pairs={{0,2},{2,0},{4,6},{6,4},{8,10},{10,8},{12,14},{14,12},{1,3},{3,1},... | collective-permute-start | bytes 614408 | tf_op jit(solution)/shard_map/ppermute | solution.py:482
  110.5 8.1 %collective-permute-start.6 = (bf16[200,256]{1,0:T(8,128)(2,1)S(1)}, bf16[200,256]{1,0:T(8,128)(2,1)S(1)}, u32[]{:S(2)}, u32[]{:S(2)}) collective-permute-start(bf16[200,256]{1,0:T(8,128)(2,1)S(1)} %select_convert_fusion.2), channel_id=1, source_target_pairs={{0,4},{2,6},{4,0},{6,2},{8,12},{10,14},{12,8},{14,10},{1,5},{3,7},... | collective-permute-start | bytes 307208 | tf_op jit(solution)/shard_map/ppermute | solution.py:482
  118.1 3.9 %collective-permute-start.15 = (bf16[200,128]{1,0:T(8,128)(2,1)S(1)}, bf16[200,128]{1,0:T(8,128)(2,1)S(1)}, u32[]{:S(2)}, u32[]{:S(2)}) collective-permute-start(bf16[200,128]{1,0:T(8,128)(2,1)S(1)} %pad_maximum_fusion.3), channel_id=1, source_target_pairs={{0,8},{2,10},{4,12},{6,14},{8,0},{10,2},{12,4},{14,6},{1,9},{3,11}... | collective-permute-start | bytes 153608 | tf_op jit(solution)/shard_map/ppermute | solution.py:482
  118.6 5.4 %collective-permute-start.7 = (bf16[200,128]{1,0:T(8,128)(2,1)S(1)}, bf16[200,128]{1,0:T(8,128)(2,1)S(1)}, u32[]{:S(2)}, u32[]{:S(2)}) collective-permute-start(bf16[200,128]{1,0:T(8,128)(2,1)S(1)} %select_convert_fusion.3), channel_id=1, source_target_pairs={{0,8},{2,10},{4,12},{6,14},{8,0},{10,2},{12,4},{14,6},{1,9},{3,11}... | collective-permute-start | bytes 153608 | tf_op jit(solution)/shard_map/ppermute | solution.py:482
  122.0 3.5 %collective-permute-start.16 = (bf16[200,128]{1,0:T(8,128)(2,1)S(1)}, bf16[200,128]{1,0:T(8,128)(2,1)S(1)}, u32[]{:S(2)}, u32[]{:S(2)}) collective-permute-start(bf16[200,128]{1,0:T(8,128)(2,1)S(1)} %add_convert_fusion.2), channel_id=1, source_target_pairs={{0,4},{2,6},{4,0},{6,2},{8,12},{10,14},{12,8},{14,10},{1,5},{3,7},... | collective-permute-start | bytes 153608 | tf_op jit(solution)/shard_map/ppermute | solution.py:482
  124.0 4.4 %collective-permute-start.8 = (bf16[200,128]{1,0:T(8,128)(2,1)S(1)}, bf16[200,128]{1,0:T(8,128)(2,1)S(1)}, u32[]{:S(2)}, u32[]{:S(2)}) collective-permute-start(bf16[200,128]{1,0:T(8,128)(2,1)S(1)} %add_convert_fusion.3), channel_id=1, source_target_pairs={{0,8},{2,10},{4,12},{6,14},{8,0},{10,2},{12,4},{14,6},{1,9},{3,11}... | collective-permute-start | bytes 153608 | tf_op jit(solution)/shard_map/ppermute | solution.py:482
  125.5 4.5 %collective-permute-start.17 = (bf16[200,128]{1,0:T(8,128)(2,1)S(1)}, bf16[200,128]{1,0:T(8,128)(2,1)S(1)}, u32[]{:S(2)}, u32[]{:S(2)}) collective-permute-start(bf16[200,128]{1,0:T(8,128)(2,1)S(1)} %add_convert_fusion.1), channel_id=1, source_target_pairs={{0,2},{2,0},{4,6},{6,4},{8,10},{10,8},{12,14},{14,12},{1,3},{3,1},... | collective-permute-start | bytes 153608 | tf_op jit(solution)/shard_map/ppermute | solution.py:482
  128.5 3.6 %collective-permute-start.9 = (bf16[200,256]{1,0:T(8,128)(2,1)S(1)}, bf16[200,256]{1,0:T(8,128)(2,1)S(1)}, u32[]{:S(2)}, u32[]{:S(2)}) collective-permute-start(bf16[200,256]{1,0:T(8,128)(2,1)S(1)} %pad_maximum_fusion.2), channel_id=1, source_target_pairs={{0,4},{2,6},{4,0},{6,2},{8,12},{10,14},{12,8},{14,10},{1,5},{3,7},... | collective-permute-start | bytes 307208 | tf_op jit(solution)/shard_map/ppermute | solution.py:482
  130.0 9.7 %collective-permute-start.18 = (bf16[200,128]{1,0:T(8,128)(2,1)S(1)}, bf16[200,128]{1,0:T(8,128)(2,1)S(1)}, u32[]{:S(2)}, u32[]{:S(2)}) collective-permute-start(bf16[200,128]{1,0:T(8,128)(2,1)S(1)} %add_convert_fusion), channel_id=1, source_target_pairs={{0,1},{1,0},{2,3},{3,2},{4,5},{5,4},{6,7},{7,6},{8,9},{9,8},{10,11... | collective-permute-start | bytes 153608 | tf_op jit(solution)/shard_map/ppermute | solution.py:482
  132.1 7.4 %collective-permute-start.14 = (bf16[400,256]{1,0:T(8,128)(2,1)S(1)}, bf16[400,256]{1,0:T(8,128)(2,1)S(1)}, u32[]{:S(2)}, u32[]{:S(2)}) collective-permute-start(bf16[400,256]{1,0:T(8,128)(2,1)S(1)} %pad_maximum_fusion.1), channel_id=1, source_target_pairs={{0,2},{2,0},{4,6},{6,4},{8,10},{10,8},{12,14},{14,12},{1,3},{3,1},... | collective-permute-start | bytes 614408 | tf_op jit(solution)/shard_map/ppermute | solution.py:482
  139.6 5.4 %collective-permute-start.19 = (bf16[800,256]{1,0:T(8,128)(2,1)S(1)}, bf16[800,256]{1,0:T(8,128)(2,1)S(1)}, u32[]{:S(2)}, u32[]{:S(2)}) collective-permute-start(bf16[800,256]{1,0:T(8,128)(2,1)S(1)} %pad_maximum_fusion), channel_id=1, source_target_pairs={{0,1},{1,0},{2,3},{3,2},{4,5},{5,4},{6,7},{7,6},{8,9},{9,8},{10,11... | collective-permute-start | bytes 1228808 | tf_op jit(solution)/shard_map/ppermute | solution.py:482
  (8 other events, 19.2 us)

commit v3 on v2

--- a/solution.py
+++ b/solution.py
@@ -14,6 +14,9 @@
 HALO = 8
 VMEM_LIMIT = 58 << 20
 CHUNKS = 5
+WIDE = 8
+SMALL = 64
+PITCH = 40
 
 
 def vmem():
@@ -307,14 +310,14 @@
         first = (step - CHUNKS - 1) * chunk
 
         def out_step(k, carry):
-            at = pl.multiple_of((first + k) * rows, rows)
+            at = pl.multiple_of((first + k) * PITCH, 8)
             wet = mask_ref[...].astype(F32)
             out_ref[k] = (x_ref[k].astype(F32) + wet * ms[pl.ds(at, rows), :]).astype(BF16)
             g_ref[k] = gs[pl.ds(at, rows), :].astype(BF16)
             back_ref[k] = gr[pl.ds(at, rows), :].astype(BF16)
             return carry
 
-        lax.fori_loop(0, chunk, out_step, 0, unroll=4)
+        lax.fori_loop(0, chunk, out_step, 0, unroll=10)
         edges = lane_edges(g_ref[...].reshape(chunk * rows, lanes))
         low_ref[...] = edges[:HALO].astype(BF16)
         high_ref[...] = edges[HALO:].astype(BF16)
@@ -330,26 +333,29 @@
     red_ref[...] = jnp.zeros_like(red_ref)
     sums_ref[...] = jnp.zeros_like(sums_ref)
 
-    def pair(ref, i):
-        first = pl.multiple_of(2 * i * channels, 8)
-        second = pl.multiple_of((2 * i + 1) * channels, 8)
-        return jnp.concatenate(
-            [ref[pl.ds(first, channels), :], ref[pl.ds(second, channels), :]], axis=1
-        )
-
-    def unpair(ref, i, value):
-        ref[pl.ds(2 * i, channels, stride=rows), :] = value[:, :lanes]
-        ref[pl.ds(2 * i + 1, channels, stride=rows), :] = value[:, lanes:]
+    def cat(values):
+        return jnp.concatenate(values, axis=1)
+
+    def group(ref, i):
+        at = [pl.multiple_of((WIDE * i + k) * channels, 8) for k in range(WIDE)]
+        return cat([ref[pl.ds(a, channels), :] for a in at])
+
+    def ungroup(ref, i, value):
+        for k in range(WIDE):
+            ref[pl.ds(WIDE * i + k, channels, stride=PITCH), :] = value[:, k * lanes : (k + 1) * lanes]
+
+    def fold(value):
+        return sum(value[:, k * lanes : (k + 1) * lanes] for k in range(WIDE))
 
     def cell_step(i, carry):
-        gain = jnp.concatenate([gain_s[...]] * 2, axis=1)
-        scale = jnp.concatenate([scale_s[...]] * 2, axis=1)
-        value = pair(conv, i)
+        gain = cat([gain_s[...]] * WIDE)
+        scale = cat([scale_s[...]] * WIDE)
+        value = group(conv, i)
         centred = value - jnp.mean(value, axis=0, keepdims=True)
         inverse = lax.rsqrt(jnp.mean(centred * centred, axis=0, keepdims=True) + 1e-06)
         normalized = centred * inverse
         normed = (normalized * gain).astype(BF16)
-        branch = pair(cots, i)
+        branch = group(cots, i)
         mixed_grad = (scale * branch).astype(BF16)
         part = 160
         for f in range(0, hiddens, part):
@@ -362,28 +368,28 @@
         red_ref[...] += dot(act_s[...], mixed_grad, 1, 1)
         normed_grad = dot(we_ref[...], hg_s[...], 1, 0)
         exp_ref[...] += dot(hg_s[...], normed, 1, 1)
-        unpair(ms, i, scale * mixed)
-        scaled = branch * mixed
-        sums_ref[1] += scaled[:, :lanes] + scaled[:, lanes:]
-        gained = normed_grad * normalized
-        sums_ref[0] += gained[:, :lanes] + gained[:, lanes:]
+        ungroup(ms, i, scale * mixed)
+        sums_ref[1] += fold(branch * mixed)
+        sums_ref[0] += fold(normed_grad * normalized)
         unit = normed_grad * gain
         m1 = jnp.mean(unit, axis=0, keepdims=True)
         m2 = jnp.mean(unit * normalized, axis=0, keepdims=True)
         grad = inverse * (unit - m1 - normalized * m2)
-        unpair(gs, i, grad)
-        gr[pl.ds(rows - 1 - 2 * i, channels, stride=rows), :] = grad[:, :lanes]
-        gr[pl.ds(rows - 2 - 2 * i, channels, stride=rows), :] = grad[:, lanes:]
+        ungroup(gs, i, grad)
+        for k in range(WIDE):
+            at = pl.ds(rows - 1 - WIDE * i - k, channels, stride=PITCH)
+            gr[at, :] = grad[:, k * lanes : (k + 1) * lanes]
         return carry
 
-    lax.fori_loop(0, rows // 2, cell_step, 0)
-
+    lax.fori_loop(0, rows // WIDE, cell_step, 0)
     is_north = north_ref[0] != 0
     expand, reduce = exp_ref[...], red_ref[...]
+    mine = jnp.where(is_north, reduce, expand)
+    theirs = jnp.where(is_north, expand, reduce)
     blank = jnp.zeros((hiddens, 2 * lanes - channels), F32)
-    keep_ref[...] = jnp.concatenate([jnp.where(is_north, reduce, expand), blank], axis=1)
-    send = jnp.concatenate([jnp.where(is_north, expand, reduce), blank], axis=1)
-    send_ref[...] = send.astype(BF16)
+    for ref, value in ((keep_ref, mine), (send_ref, theirs)):
+        ref[:hiddens, :] = value[:, :lanes].astype(ref.dtype)
+        ref[hiddens:, :] = cat([value[:, lanes:], blank]).astype(ref.dtype)
 
 
 def tap_kernel(start, north_ref, x_ref, h_ref, lat_ref, fold_ref, back_ref, sums_ref, small_ref, rb, rh, rows_s):
@@ -402,15 +408,15 @@
     lax.fori_loop(0, chunk, step, 0, unroll=20)
     place, _ = tap_places(rows)
     pick = as_f32(place == iota(place.shape, 0))
-    pick = jnp.concatenate([pick, jnp.zeros((lanes - KS * KS, pick.shape[1]), F32)], axis=0)
-    pick = pick.astype(BF16)
+    blank = jnp.zeros((SMALL - KS * KS, pick.shape[1]), F32)
+    pick = jnp.concatenate([pick, blank], axis=0).astype(BF16)
     high, low = split(rows_s[...])
-    lane = iota((chunk, lanes), 1)
-    small = dot(high, pick, 1, 1) + dot(low, pick, 1, 1)
+    taps = dot(high, pick, 1, 1) + dot(low, pick, 1, 1)
+    lane = iota((chunk, SMALL), 1)
     for i in range(2):
         total = jnp.sum(sums_ref[i], axis=1, keepdims=True)
-        small = jnp.where(lane == KS * KS + i, total, small)
-    small_ref[...] = small
+        taps = jnp.where(lane == KS * KS + i, total, taps)
+    small_ref[...] = taps
 
 
 def adjoint_kernel(start, north_ref, g_ref, h_ref, lat_ref, fold_ref, taps_ref, cot_ref, *refs):
@@ -462,20 +468,16 @@
     return pl.CostEstimate(flops=int(micros * 1e9), bytes_accessed=int(micros * 3e6), transcendentals=0)
 
 
-def split_half(buf, bit):
-    rows, lanes = buf.shape
-    if (rows // 2) % 8 and lanes > 128:
-        first, second = buf[:, : lanes // 2], buf[:, lanes // 2 :]
-    else:
-        first, second = buf[: rows // 2], buf[rows // 2 :]
+def halves(buf, bit):
+    half = buf.shape[0] // 2
+    first, second = buf[:half], buf[half:]
     up = bit != 0
     return jnp.where(up, second, first), jnp.where(up, first, second)
 
 
-def join_half(mine, other, bit, dims):
+def joined(mine, other, bit):
     up = bit != 0
-    first, second = jnp.where(up, other, mine), jnp.where(up, mine, other)
-    return jnp.concatenate([first, second], axis=1 if mine.shape[0] == dims[0] else 0)
+    return jnp.concatenate([jnp.where(up, other, mine), jnp.where(up, mine, other)], axis=0)
 
 
 def partner(value, axis, b):
@@ -484,11 +486,6 @@
 
 def lon_bits():
     return range(lax.axis_size("lon").bit_length() - 1)
-
-
-def both_sum(value, axis, b):
-    mine = value.astype(BF16)
-    return mine.astype(F32) + partner(mine, axis, b).astype(F32)
 
 
 def together(*values):
@@ -507,8 +504,9 @@
     field = shape(ocean_state.shape, BF16)
     rowbuf = pltpu.VMEM((HALO * channels, lanes), F32)
     cellbuf = pltpu.VMEM((channels * rows, lanes), F32)
+    pitchbuf = pltpu.VMEM((channels * PITCH, lanes), F32)
     tapbuf = pltpu.VMEM((channels, width), F32)
-    hidbuf = pltpu.VMEM((hiddens, 2 * lanes), BF16)
+    hidbuf = pltpu.VMEM((hiddens, WIDE * lanes), BF16)
     gradbuf = pltpu.VMEM((hiddens, channels), F32)
     lanebuf = pltpu.VMEM((channels, lanes), F32)
 
@@ -543,31 +541,18 @@
             field,
             edge,
             edge,
-            shape((hiddens, 2 * lanes), F32),
-            shape((hiddens, 2 * lanes), BF16),
+            shape((2 * hiddens, lanes), F32),
+            shape((2 * hiddens, lanes), BF16),
             shape((2, channels, lanes), F32),
         ),
-        [smem()] * 3 + [block(both_ways), block(into), whole, whole, whole, block(into)] + [whole] * 5,
+        [smem()] * 3 + [block(both_ways), block(into)] + [whole] * 3 + [block(into)] + [whole] * 5,
         [block(back_out)] * 3 + [edge_block] * 2 + [whole] * 3,
-        [cellbuf] * 5 + [rowbuf] * 2 + [hidbuf] * 2 + [gradbuf] * 2 + [tapbuf] + [lanebuf] * 2,
+        [cellbuf] * 2 + [pitchbuf] * 3 + [rowbuf] * 2 + [hidbuf] * 2 + [gradbuf] * 2 + [tapbuf] + [lanebuf] * 2,
         cost(40),
     )(
-        north, norm_gain, layer_scale, ocean_state, halo, lat_rows, fold_rows, kernel, cotangent,
-        land_mask, expand_weight.T, expand_weight, reduce_weight, reduce_weight.T,
+        north, norm_gain, layer_scale, ocean_state, halo, lat_rows, fold_rows, kernel, cotangent, land_mask,
+         expand_weight.T, expand_weight, reduce_weight, reduce_weight.T,
     )
-
-    def taps_part(start, count, field, back):
-        here = block(lambda i: i + start)
-        return grid_call(
-            functools.partial(tap_kernel, start),
-            count,
-            shape((count * chunk, lanes), F32),
-            [smem(), here, here, whole, whole, here]
-            + [pl.BlockSpec((2, chunk, lanes), lambda i: (0, i + start, 0))],
-            pl.BlockSpec((chunk, lanes), lambda i: (i, 0)),
-            [rowbuf] * 2 + [pltpu.VMEM((chunk, width), F32)],
-            cost(3 * count),
-        )(north, field, halo, lat_rows, fold_rows, back, sums)
 
     def adjoint_part(start, count, grad, lane_halo, previous):
         here = block(lambda i: i + start)
@@ -575,8 +560,8 @@
         return grid_call(
             functools.partial(adjoint_kernel, start),
             count,
-            shape(ocean_state.shape, BF16),
-            [smem(), here, here, whole, whole, whole, here]
+            field,
+            [smem(), here, here] + [whole] * 3 + [here]
             + [pl.BlockSpec(memory_space=pl.ANY)] * len(extra),
             here,
             [rowbuf] * 2 + [tapbuf],
@@ -584,47 +569,72 @@
             {7: 0} if extra else None,
         )(north, grad, lane_halo, g_lat, g_fold, kernel, cotangent, *extra)
 
+    g_east, g_west = lon_edges(g_low, g_high)
+    def taps_part(start, count, back):
+        here = block(lambda i: i + start)
+        return grid_call(
+            functools.partial(tap_kernel, start),
+            count,
+            shape((count * chunk, SMALL), F32),
+            [smem(), here, here] + [whole] * 2
+            + [here, pl.BlockSpec((2, chunk, lanes), lambda i: (0, i + start, 0))],
+            pl.BlockSpec((chunk, SMALL), lambda i: (i, 0)),
+            [rowbuf] * 2 + [pltpu.VMEM((chunk, width), F32)],
+            cost(3 * count),
+        )(north, ocean_state, halo, lat_rows, fold_rows, back, sums)
+
+    buf = keep + partner(send, "lat", 0).astype(F32)
     bits = list(lon_bits())
-    first_part = (CHUNKS + 1) // 2
-
-    def side(b):
-        return (lax.axis_index("lon") >> b) & 1
-
-    g_east, g_west = lon_edges(g_low, g_high)
-    buf = keep + partner(send, "lat", 0).astype(F32)
-    sizes, parts = [], []
-    back = back_grad
-    for b in bits:
-        sizes.append(buf.shape)
-        stay, go = split_half(buf, side(b))
-        got = partner(go.astype(BF16), "lon", b)
-        if len(parts) < 2:
-            start = len(parts) * first_part
-            count = CHUNKS - first_part if parts else first_part
-            parts.append(taps_part(start, count, ocean_state, back))
-            got, back = together(got, parts[-1], back)[::2]
-        buf = stay + got.astype(F32)
-    small = jnp.concatenate(parts, axis=0)
-    g_halo, g_lat, g_fold = halo_rows(conv_grad, g_east, g_west, north)
-    buf = buf.astype(BF16)
-    state_grad = None
-    done = 0
-    grad = conv_grad
-    for n, b in enumerate(bits[::-1]):
-        got = partner(buf, "lon", b)
-        small = both_sum(small, "lon", b)
-        if n > 0 and done < CHUNKS:
+    parts, taps_done, back = [], 0, back_grad
+    g_halo, state_grad, done, grad = None, None, 0, conv_grad
+    steps = [(b, True) for b in bits] + [(b, False) for b in bits[::-1]]
+    for b, halving in steps:
+        bit = (lax.axis_index("lon") >> b) & 1
+        if halving:
+            stay, go = halves(buf, bit)
+            go = go.astype(BF16)
+        else:
+            if done == 0:
+                small = jnp.concatenate(parts, axis=0)
+                half = channels // 2
+                small = jnp.concatenate([small[:half], small[half:]], axis=1)
+                small = jnp.pad(small, ((0, -half % 8), (0, 0)))
+                small = small + partner(small, "lat", 0)
+            stay, own = buf.astype(BF16), small.astype(BF16)
+            go = jnp.concatenate([stay, own], axis=0)
+        go, grad, back = together(go, grad, back)
+        got = partner(go, "lon", b)
+        if taps_done and g_halo is None:
+            g_halo, g_lat, g_fold = halo_rows(grad, g_east, g_west, north)
+            got, g_halo, back = together(got, g_halo, back)
+        elif taps_done < CHUNKS:
+            count = min(CHUNKS - taps_done, (CHUNKS + 1) // 2)
+            parts.append(taps_part(taps_done, count, back))
+            taps_done += count
+            got, parts[-1] = together(got, parts[-1])
+        elif done < CHUNKS and not halving:
             count = min(2, CHUNKS - done)
             state_grad = adjoint_part(done, count, grad, g_halo, state_grad)
             done += count
-            got, state_grad, grad = together(got, state_grad, grad)
-        buf = join_half(buf, got, side(b), sizes[len(bits) - 1 - n])
+            got, state_grad = together(got, state_grad)
+        if halving:
+            buf = stay + got.astype(F32)
+        else:
+            rows_here = stay.shape[0]
+            buf = joined(stay, got[:rows_here], bit)
+            small = own.astype(F32) + got[rows_here:].astype(F32)
     if done < CHUNKS:
         state_grad = adjoint_part(done, CHUNKS - done, grad, g_halo, state_grad)
     other = partner(buf, "lat", 0)
-    small = both_sum(small, "lat", 0)
-    expand = jnp.where(is_north, other, buf)[:, :channels].astype(F32)
-    reduce = jnp.where(is_north, buf, other)[:, :channels].astype(F32)
+
+    def unfolded(value):
+        top, rest = value[:hiddens], value[hiddens:, : channels - lanes]
+        return jnp.concatenate([top, rest], axis=1).astype(F32)
+
+    expand = unfolded(jnp.where(is_north, other, buf))
+    reduce = unfolded(jnp.where(is_north, buf, other))
+    half = channels // 2
+    small = jnp.concatenate([small[:half, :SMALL], small[:half, SMALL:]], axis=0)
     kernel_grad = small[:, : KS * KS]
     gain_grad = small[:, KS * KS]
     scale_grad = small[:, KS * KS + 1]

time: 148 us -> 130 us (0.88)
  Pallas kernels: 84.5 us -> 74.6 us
  starting transfers between devices: 28.5 us -> 23.2 us
  waiting for transfers between devices: 22.1 us -> 17.3 us
    pallas_call x1, Pallas kernels: 44.1 us -> 34.3 us  [on_device(): grid_call(main_kernel, 2 * CHUNKS + 1, (field, field, field, edge, edge,...]
    ppermute x2, waiting for transfers between devices: 11.3 us -> 5.94 us  [halo_rows(): lax.ppermute(fold_msg, ('lon', 'lat'), [(i * m + m - 1, (n - 1 - i) * m +...]
    ppermute x12 -> x9, starting transfers between devices: 12 us -> 7.08 us  [partner(): lax.ppermute(value, axis, [(i, i ^ 1 << b) for i in range(lax.axis_size(a...]
    another operation x2 -> x0, other arithmetic: 1.61 us -> none
    ppermute x12 -> x9, waiting for transfers between devices: 4.3 us -> 4.94 us  [partner(): lax.ppermute(value, axis, [(i, i ^ 1 << b) for i in range(lax.axis_size(a...]
  transfers between devices with their start and end apart: 20 -> 17, of which waited for: 8 -> 7; matrix products, arithmetic and copies ran while one was open for 4% -> 5% of each run, Pallas kernels for 23% -> 26%
where the time goes in v3:
time: 130 us
  Pallas kernels  74.6 us (57%)
  starting transfers between devices  23.2 us (18%)
  waiting for transfers between devices  17.3 us (13%)
  local copies, waits for them, and re-layouts  9.83 us (8%)
  other arithmetic  3.62 us (3%)
    pallas_call x1, Pallas kernels, on_device(): grid_call(main_kernel, 2 * CHUNKS + 1, (field, field, field, edge, edge,...  34.3 us
    pallas_call x2, Pallas kernels, taps_part(): grid_call(functools.partial(tap_kernel, start), count, shape((count * chu...  15.7 us
    pallas_call x3, Pallas kernels, adjoint_part(): grid_call(functools.partial(adjoint_kernel, start), count, field, [smem()...  14.1 us
    unnamed x30, local copies, waits for them, and re-layouts  9.69 us
    pallas_call x2, Pallas kernels, halo_rows(): call(unpack_kernel, (shape(field.shape, BF16), msg, msg), scratch=[pltpu....  7.74 us
    ppermute x9, starting transfers between devices, partner(): lax.ppermute(value, axis, [(i, i ^ 1 << b) for i in range(lax.axis_size(a...  7.08 us
    ppermute x2, starting transfers between devices, halo_rows(): lax.ppermute(fold_msg, ('lon', 'lat'), [(i * m + m - 1, (n - 1 - i) * m +...  6.24 us
    ppermute x2, waiting for transfers between devices, halo_rows(): lax.ppermute(fold_msg, ('lon', 'lat'), [(i * m + m - 1, (n - 1 - i) * m +...  5.94 us
  transfers between devices with their start and end apart: 17, of which 7 were waited for; matrix products, arithmetic and copies ran while one was open for 5% of the time, Pallas kernels for 26%

profile of v3, /device:TPU:1, one launch (start us, length us, event | category | flops | bytes accessed | tf_op | source)
XLA Modules:
  0.0 129.6 jit_solution(5088158368338723276)
XLA Ops:
  0.6 2.7 %shard_map.135 = (bf16[8,6400]{1,0:T(8,128)(2,1)}, bf16[8,6400]{1,0:T(8,128)(2,1)}) custom-call(bf16[6400,128]{1,0:T(8,128)(2,1)} %bitcast.8), custom_call_target="tpu_custom_call" | custom-call | flops 2000000000 | bytes 6000000 | tf_op jit(solution)/shard_map/pallas_call | solution.py:513
  3.3 5.1 %collective-permute-start = (bf16[8,6400]{1,0:T(8,128)(2,1)}, bf16[8,6400]{1,0:T(8,128)(2,1)S(1)}, u32[]{:S(2)}, u32[]{:S(2)}) collective-permute-start(bf16[8,6400]{1,0:T(8,128)(2,1)} %get-tuple-element.51), channel_id=1, source_target_pairs={{2,0},{4,2},{6,4},{8,6},{10,8},{12,10},{14,12},{0,14},{3,1},{5,3},... | collective-permute-start | bytes 307208 | tf_op jit(solution)/shard_map/ppermute | solution.py:443
  8.4 2.0 %collective-permute-done.east_ref = bf16[8,6400]{1,0:T(8,128)(2,1)S(1)} collective-permute-done((bf16[8,6400]{1,0:T(8,128)(2,1)}, bf16[8,6400]{1,0:T(8,128)(2,1)S(1)}, u32[]{:S(2)}, u32[]{:S(2)}) %collective-permute-start) | collective-permute-done | bytes 102432 | tf_op jit(solution)/shard_map/ppermute | solution.py:443
  10.4 4.4 %collective-permute-done.1.west_ref = bf16[8,6400]{1,0:T(8,128)(2,1)S(1)} collective-permute-done((bf16[8,6400]{1,0:T(8,128)(2,1)}, bf16[8,6400]{1,0:T(8,128)(2,1)S(1)}, u32[]{:S(2)}, u32[]{:S(2)}) %collective-permute-start.1) | collective-permute-done | bytes 102432 | tf_op jit(solution)/shard_map/ppermute | solution.py:444
  15.5 3.9 %shard_map.136 = (bf16[200,32,128]{2,1,0:T(8,128)(2,1)}, bf16[3,200,256]{2,1,0:T(8,128)(2,1)}, bf16[3,200,256]{2,1,0:T(8,128)(2,1)}) custom-call(s32[1]{0:T(128)} %bitcast.north_ref, bf16[200,32,128]{2,1,0:T(8,128)(2,1)} %x_ref.7, bf16[8,6400]{1,0:T(8,128)(2,1)} %copy-done.10, bf16[8,6400]{1,0:T(8,128)(2,1)} %copy-done.11), custom_call_target="tpu_custom_call" | custom-call | flops 3000000000 | bytes 9000000 | tf_op jit(solution)/shard_map/pallas_call | solution.py:452
  19.4 2.1 %collective-permute-start.2 = (bf16[3,200,256]{2,1,0:T(8,128)(2,1)}, bf16[3,200,256]{2,1,0:T(8,128)(2,1)S(1)}, u32[]{:S(2)}, u32[]{:S(2)}) collective-permute-start(bf16[3,200,256]{2,1,0:T(8,128)(2,1)} %get-tuple-element.54), channel_id=1, source_target_pairs={{0,1},{1,0},{2,3},{3,2},{4,5},{5,4},{6,7},{7,6},{8,9},{9,8},{10,11... | collective-permute-start | bytes 921608 | tf_op jit(solution)/shard_map/ppermute | solution.py:463
  21.5 1.9 %collective-permute-start.3 = (bf16[3,200,256]{2,1,0:T(8,128)(2,1)}, bf16[3,200,256]{2,1,0:T(8,128)(2,1)S(1)}, u32[]{:S(2)}, u32[]{:S(2)}) collective-permute-start(bf16[3,200,256]{2,1,0:T(8,128)(2,1)} %get-tuple-element.55), channel_id=1, source_target_pairs={{1,15},{3,13},{5,11},{7,9},{9,7},{11,5},{13,3},{15,1},{17,31},{19,... | collective-permute-start | bytes 921608 | tf_op jit(solution)/shard_map/ppermute | solution.py:460
  26.0 5.9 %collective-permute-done.3.fold_ref = bf16[3,200,256]{2,1,0:T(8,128)(2,1)S(1)} collective-permute-done((bf16[3,200,256]{2,1,0:T(8,128)(2,1)}, bf16[3,200,256]{2,1,0:T(8,128)(2,1)S(1)}, u32[]{:S(2)}, u32[]{:S(2)}) %collective-permute-start.3) | collective-permute-done | bytes 307232 | tf_op jit(solution)/shard_map/ppermute | solution.py:460
  32.7 34.3 %shard_map.137 = (bf16[200,32,128]{2,1,0:T(8,128)(2,1)}, bf16[200,32,128]{2,1,0:T(8,128)(2,1)}, bf16[200,32,128]{2,1,0:T(8,128)(2,1)}, bf16[8,6400]{1,0:T(8,128)...) custom-call(s32[1]{0:T(128)} %bitcast.north_ref, ...), custom_call_target="tpu_custom_call" | custom-call | flops 40000000000 | bytes 120000000 | tf_op jit(solution)/shard_map/pallas_call | solution.py:535
  67.3 1.3 %collective-permute-start.8 = (bf16[8,6400]{1,0:T(8,128)(2,1)}, bf16[8,6400]{1,0:T(8,128)(2,1)S(1)}, u32[]{:S(2)}, u32[]{:S(2)}) collective-permute-start(bf16[8,6400]{1,0:T(8,128)(2,1)} %get-tuple-element.69), channel_id=1, source_target_pairs={{0,2},{2,4},{4,6},{6,8},{8,10},{10,12},{12,14},{14,0},{1,3},{3,5},... | collective-permute-start | bytes 307208 | tf_op jit(solution)/shard_map/ppermute | solution.py:444
  69.1 1.2 convert_add_fusion
  70.4 9.0 %shard_map.138 = f32[120,64]{1,0:T(8,128)} custom-call(s32[1]{0:T(128)} %bitcast.north_ref, bf16[200,32,128]{2,1,0:T(8,128)(2,1)} %x_ref.7, bf16[200,32,128]{2,1,0:T(8,128)(2,1)} %get-tuple-element.53.h_ref, bf16[3,200,256]{2,1,0:T(8,128)(2,1)} %copy-done.6, bf16[3,200,256]{2,1,0:T(8,128)(2,1)} %copy-done.7, ...), custom_call_target="tpu_custom_call" | custom-call | flops 8999999488 | bytes 27000000 | tf_op jit(solution)/shard_map/pallas_call | solution.py:575
  80.9 3.8 %shard_map.139 = (bf16[200,32,128]{2,1,0:T(8,128)(2,1)}, bf16[3,200,256]{2,1,0:T(8,128)(2,1)}, bf16[3,200,256]{2,1,0:T(8,128)(2,1)}) custom-call(s32[1]{0:T(128)} %bitcast.north_ref, bf16[200,32,128]{2,1,0:T(8,128)(2,1)} %get-tuple-element.91.x_ref.g_ref, bf16[8,6400]{1,0:T(8,128)(2,1)} %copy-done.8, bf16[8,6400]{1,0:T(8,128)(2,1)} %copy-done.9), custom_call_target="tpu_custom_call" | custom-call | flops 3000000000 | bytes 9000000 | tf_op jit(solution)/shard_map/pallas_call | solution.py:452
  85.9 4.3 %collective-permute-start.13 = (bf16[3,200,256]{2,1,0:T(8,128)(2,1)}, bf16[3,200,256]{2,1,0:T(8,128)(2,1)S(1)}, u32[]{:S(2)}, u32[]{:S(2)}) collective-permute-start(bf16[3,200,256]{2,1,0:T(8,128)(2,1)} %get-tuple-element.84), channel_id=1, source_target_pairs={{1,15},{3,13},{5,11},{7,9},{9,7},{11,5},{13,3},{15,1},{17,31},{19,... | collective-permute-start | bytes 921608 | tf_op jit(solution)/shard_map/ppermute | solution.py:460
  90.3 1.6 %collective-permute-start.9 = (bf16[200,128]{1,0:T(8,128)(2,1)S(1)}, bf16[200,128]{1,0:T(8,128)(2,1)S(1)}, u32[]{:S(2)}, u32[]{:S(2)}) collective-permute-start(bf16[200,128]{1,0:T(8,128)(2,1)S(1)} %select_convert_fusion.2), channel_id=1, source_target_pairs={{0,8},{2,10},{4,12},{6,14},{8,0},{10,2},{12,4},{14,6},{1,9},{3,11}... | collective-permute-start | bytes 153608 | tf_op jit(solution)/shard_map/ppermute | solution.py:484
  91.9 6.7 %shard_map.140 = f32[80,64]{1,0:T(8,128)} custom-call(s32[1]{0:T(128)} %bitcast.north_ref, bf16[200,32,128]{2,1,0:T(8,128)(2,1)} %x_ref.7, bf16[200,32,128]{2,1,0:T(8,128)(2,1)} %get-tuple-element.53.h_ref, bf16[3,200,256]{2,1,0:T(8,128)(2,1)} %copy-done.6, bf16[3,200,256]{2,1,0:T(8,128)(2,1)} %copy-done.7, ...), custom_call_target="tpu_custom_call" | custom-call | flops 6000000000 | bytes 18000000 | tf_op jit(solution)/shard_map/pallas_call | solution.py:575
  98.6 1.8 %collective-permute-done.9 = bf16[200,128]{1,0:T(8,128)(2,1)S(1)} collective-permute-done((bf16[200,128]{1,0:T(8,128)(2,1)S(1)}, bf16[200,128]{1,0:T(8,128)(2,1)S(1)}, u32[]{:S(2)}, u32[]{:S(2)}) %collective-permute-start.9) | collective-permute-done | bytes 51232 | tf_op jit(solution)/shard_map/ppermute | solution.py:484
  104.1 5.2 %shard_map.141.refs_0_ = bf16[200,32,128]{2,1,0:T(8,128)(2,1)} custom-call(s32[1]{0:T(128)} %bitcast.north_ref, bf16[200,32,128]{2,1,0:T(8,128)(2,1)} %get-tuple-element.91.x_ref.g_ref, bf16[200,32,128]{2,1,0:T(8,128)(2,1)} %get-tuple-element.82.h_ref, bf16[3,200,256]{2,1,0:T(8,128)(2,1)} %copy-done.2, bf16[3,200,256]{2,1,0:T(8,128)(2,1)} %copy-done.3, ...), custom_call_target="tpu_custom_call" | custom-call | flops 4000000000 | bytes 12000000 | tf_op jit(solution)/shard_map/pallas_call | solution.py:560
  109.4 2.3 %collective-permute-start.14 = (bf16[504,128]{1,0:T(8,128)(2,1)S(1)}, bf16[504,128]{1,0:T(8,128)(2,1)S(1)}, u32[]{:S(2)}, u32[]{:S(2)}) collective-permute-start(bf16[504,128]{1,0:T(8,128)(2,1)S(1)} %pad_maximum_fusion.3), channel_id=1, source_target_pairs={{0,4},{2,6},{4,0},{6,2},{8,12},{10,14},{12,8},{14,10},{1,5},{3,7},... | collective-permute-start | bytes 387080 | tf_op jit(solution)/shard_map/ppermute | solution.py:484
  111.6 5.2 %shard_map.142.refs_0_ = bf16[200,32,128]{2,1,0:T(8,128)(2,1)} custom-call(s32[1]{0:T(128)} %bitcast.north_ref, bf16[200,32,128]{2,1,0:T(8,128)(2,1)} %get-tuple-element.91.x_ref.g_ref, bf16[200,32,128]{2,1,0:T(8,128)(2,1)} %get-tuple-element.82.h_ref, bf16[3,200,256]{2,1,0:T(8,128)(2,1)} %copy-done.2, ...), custom_call_target="tpu_custom_call", output_to_operand_aliasing={{}: (7, {})} | custom-call | flops 4000000000 | bytes 12000000 | tf_op jit(solution)/shard_map/pallas_call | solution.py:560
  116.9 1.2 collective-permute-start.15
  118.1 3.8 %shard_map.143 = bf16[200,32,128]{2,1,0:T(8,128)(2,1)} custom-call(s32[1]{0:T(128)} %bitcast.north_ref, bf16[200,32,128]{2,1,0:T(8,128)(2,1)} %get-tuple-element.91.x_ref.g_ref, bf16[200,32,128]{2,1,0:T(8,128)(2,1)} %get-tuple-element.82.h_ref, bf16[3,200,256]{2,1,0:T(8,128)(2,1)} %copy-done.2, ...), custom_call_target="tpu_custom_call", output_to_operand_aliasing={{}: (7, {})} | custom-call | flops 2000000000 | bytes 6000000 | tf_op jit(solution)/shard_map/pallas_call | solution.py:560
  121.9 1.5 %collective-permute-done.15 = bf16[904,128]{1,0:T(8,128)(2,1)S(1)} collective-permute-done((bf16[904,128]{1,0:T(8,128)(2,1)S(1)}, bf16[904,128]{1,0:T(8,128)(2,1)S(1)}, u32[]{:S(2)}, u32[]{:S(2)}) %collective-permute-start.15) | collective-permute-done | bytes 231456 | tf_op jit(solution)/shard_map/ppermute | solution.py:484
  123.6 1.7 %collective-permute-start.16 = (bf16[1600,128]{1,0:T(8,128)(2,1)S(1)}, bf16[1600,128]{1,0:T(8,128)(2,1)S(1)}, u32[]{:S(2)}, u32[]{:S(2)}) collective-permute-start(bf16[1600,128]{1,0:T(8,128)(2,1)S(1)} %pad_maximum_fusion), channel_id=1, source_target_pairs={{0,1},{1,0},{2,3},{3,2},{4,5},{5,4},{6,7},{7,6},{8,9},{9,8},{10,11... | collective-permute-start | bytes 1228808 | tf_op jit(solution)/shard_map/ppermute | solution.py:484
  (80 shorter events, 15.6 us)
Async XLA Ops:
  3.3 7.1 %collective-permute-start = (bf16[8,6400]{1,0:T(8,128)(2,1)}, bf16[8,6400]{1,0:T(8,128)(2,1)S(1)}, u32[]{:S(2)}, u32[]{:S(2)}) collective-permute-start(bf16[8,6400]{1,0:T(8,128)(2,1)} %get-tuple-element.51), channel_id=1, source_target_pairs={{2,0},{4,2},{6,4},{8,6},{10,8},{12,10},{14,12},{0,14},{3,1},{5,3},... | collective-permute-start | bytes 307208 | tf_op jit(solution)/shard_map/ppermute | solution.py:443
  8.4 6.4 %collective-permute-start.1 = (bf16[8,6400]{1,0:T(8,128)(2,1)}, bf16[8,6400]{1,0:T(8,128)(2,1)S(1)}, u32[]{:S(2)}, u32[]{:S(2)}) collective-permute-start(bf16[8,6400]{1,0:T(8,128)(2,1)} %get-tuple-element.52), channel_id=1, source_target_pairs={{0,2},{2,4},{4,6},{6,8},{8,10},{10,12},{12,14},{14,0},{1,3},{3,5},... | collective-permute-start | bytes 307208 | tf_op jit(solution)/shard_map/ppermute | solution.py:444
  10.4 4.4 %copy-start.10 = (bf16[8,6400]{1,0:T(8,128)(2,1)}, bf16[8,6400]{1,0:T(8,128)(2,1)S(1)}, u32[]{:S(2)}) copy-start(bf16[8,6400]{1,0:T(8,128)(2,1)S(1)} %collective-permute-done.east_ref) | copy-start | bytes 307204
  15.5 7.9 %copy-start.5 = (f32[200,49]{0,1:T(8,128)S(1)}, f32[200,49]{0,1:T(8,128)}, u32[]{:S(2)}) copy-start(f32[200,49]{0,1:T(8,128)} %param.10) | copy-start | bytes 117604
  15.5 8.7 %copy-start = (bf16[200,800]{1,0:T(8,128)(2,1)S(1)}, bf16[200,800]{1,0:T(8,128)(2,1)}, u32[]{:S(2)}) copy-start(bf16[200,800]{1,0:T(8,128)(2,1)} %we_ref.1) | copy-start | bytes 960004
  15.5 9.6 %copy-start.1 = (bf16[800,200]{0,1:T(8,128)(2,1)S(1)}, bf16[800,200]{0,1:T(8,128)(2,1)}, u32[]{:S(2)}) copy-start(bf16[800,200]{0,1:T(8,128)(2,1)} %param.13) | copy-start | bytes 960004
  19.4 6.7 %collective-permute-start.2 = (bf16[3,200,256]{2,1,0:T(8,128)(2,1)}, bf16[3,200,256]{2,1,0:T(8,128)(2,1)S(1)}, u32[]{:S(2)}, u32[]{:S(2)}) collective-permute-start(bf16[3,200,256]{2,1,0:T(8,128)(2,1)} %get-tuple-element.54), channel_id=1, source_target_pairs={{0,1},{1,0},{2,3},{3,2},{4,5},{5,4},{6,7},{7,6},{8,9},{9,8},{10,11... | collective-permute-start | bytes 921608 | tf_op jit(solution)/shard_map/ppermute | solution.py:463
  21.5 10.5 %collective-permute-start.3 = (bf16[3,200,256]{2,1,0:T(8,128)(2,1)}, bf16[3,200,256]{2,1,0:T(8,128)(2,1)S(1)}, u32[]{:S(2)}, u32[]{:S(2)}) collective-permute-start(bf16[3,200,256]{2,1,0:T(8,128)(2,1)} %get-tuple-element.55), channel_id=1, source_target_pairs={{1,15},{3,13},{5,11},{7,9},{9,7},{11,5},{13,3},{15,1},{17,31},{19,... | collective-permute-start | bytes 921608 | tf_op jit(solution)/shard_map/ppermute | solution.py:460
  26.0 5.9 %copy-start.6 = (bf16[3,200,256]{2,1,0:T(8,128)(2,1)}, bf16[3,200,256]{2,1,0:T(8,128)(2,1)S(1)}, u32[]{:S(2)}) copy-start(bf16[3,200,256]{2,1,0:T(8,128)(2,1)S(1)} %collective-permute-done.2.lat_ref) | copy-start | bytes 921604
  67.1 2.0 %collective-permute-start.4 = (bf16[1600,128]{1,0:T(8,128)(2,1)}, bf16[1600,128]{1,0:T(8,128)(2,1)S(1)}, u32[]{:S(2)}, u32[]{:S(2)}) collective-permute-start(bf16[1600,128]{1,0:T(8,128)(2,1)} %get-tuple-element.58), channel_id=1, source_target_pairs={{0,1},{1,0},{2,3},{3,2},{4,5},{5,4},{6,7},{7,6},{8,9},{9,8},{10,11... | collective-permute-start | bytes 1228808 | tf_op jit(solution)/shard_map/ppermute | solution.py:484
  67.2 12.5 %collective-permute-start.7 = (bf16[8,6400]{1,0:T(8,128)(2,1)}, bf16[8,6400]{1,0:T(8,128)(2,1)S(1)}, u32[]{:S(2)}, u32[]{:S(2)}) collective-permute-start(bf16[8,6400]{1,0:T(8,128)(2,1)} %get-tuple-element.68), channel_id=1, source_target_pairs={{2,0},{4,2},{6,4},{8,6},{10,8},{12,10},{14,12},{0,14},{3,1},{5,3},... | collective-permute-start | bytes 307208 | tf_op jit(solution)/shard_map/ppermute | solution.py:443
  67.3 12.3 %collective-permute-start.8 = (bf16[8,6400]{1,0:T(8,128)(2,1)}, bf16[8,6400]{1,0:T(8,128)(2,1)S(1)}, u32[]{:S(2)}, u32[]{:S(2)}) collective-permute-start(bf16[8,6400]{1,0:T(8,128)(2,1)} %get-tuple-element.69), channel_id=1, source_target_pairs={{0,2},{2,4},{4,6},{6,8},{8,10},{10,12},{12,14},{14,0},{1,3},{3,5},... | collective-permute-start | bytes 307208 | tf_op jit(solution)/shard_map/ppermute | solution.py:444
  70.4 9.1 %collective-permute-start.5 = (bf16[800,128]{1,0:T(8,128)(2,1)S(1)}, bf16[800,128]{1,0:T(8,128)(2,1)S(1)}, u32[]{:S(2)}, u32[]{:S(2)}) collective-permute-start(bf16[800,128]{1,0:T(8,128)(2,1)S(1)} %select_convert_fusion), channel_id=1, source_target_pairs={{0,2},{2,0},{4,6},{6,4},{8,10},{10,8},{12,14},{14,12},{1,3},{3,1},... | collective-permute-start | bytes 614408 | tf_op jit(solution)/shard_map/ppermute | solution.py:484
  79.5 10.7 %collective-permute-start.6 = (bf16[400,128]{1,0:T(8,128)(2,1)S(1)}, bf16[400,128]{1,0:T(8,128)(2,1)S(1)}, u32[]{:S(2)}, u32[]{:S(2)}) collective-permute-start(bf16[400,128]{1,0:T(8,128)(2,1)S(1)} %select_convert_fusion.1), channel_id=1, source_target_pairs={{0,4},{2,6},{4,0},{6,2},{8,12},{10,14},{12,8},{14,10},{1,5},{3,7},... | collective-permute-start | bytes 307208 | tf_op jit(solution)/shard_map/ppermute | solution.py:484
  84.7 17.9 %collective-permute-start.12 = (bf16[3,200,256]{2,1,0:T(8,128)(2,1)}, bf16[3,200,256]{2,1,0:T(8,128)(2,1)S(1)}, u32[]{:S(2)}, u32[]{:S(2)}) collective-permute-start(bf16[3,200,256]{2,1,0:T(8,128)(2,1)} %get-tuple-element.83), channel_id=1, source_target_pairs={{0,1},{1,0},{2,3},{3,2},{4,5},{5,4},{6,7},{7,6},{8,9},{9,8},{10,11... | collective-permute-start | bytes 921608 | tf_op jit(solution)/shard_map/ppermute | solution.py:463
  85.9 16.8 %collective-permute-start.13 = (bf16[3,200,256]{2,1,0:T(8,128)(2,1)}, bf16[3,200,256]{2,1,0:T(8,128)(2,1)S(1)}, u32[]{:S(2)}, u32[]{:S(2)}) collective-permute-start(bf16[3,200,256]{2,1,0:T(8,128)(2,1)} %get-tuple-element.84), channel_id=1, source_target_pairs={{1,15},{3,13},{5,11},{7,9},{9,7},{11,5},{13,3},{15,1},{17,31},{19,... | collective-permute-start | bytes 921608 | tf_op jit(solution)/shard_map/ppermute | solution.py:460
  90.3 10.1 %copy-start.4 = (f32[120,64]{1,0:T(8,128)S(1)}, f32[120,64]{1,0:T(8,128)}, u32[]{:S(2)}) copy-start(f32[120,64]{1,0:T(8,128)} %shard_map.138) | copy-start | bytes 92164
  90.3 10.1 %slice-start = ((f32[120,64]{1,0:T(8,128)}), f32[100,64]{1,0:T(8,128)S(1)}, s32[]{:S(2)}) async-start(f32[120,64]{1,0:T(8,128)} %shard_map.138), calls=%async_computation | async-start | bytes 106496 | tf_op jit(solution)/shard_map/slice | solution.py:600
  90.3 10.1 %collective-permute-start.9 = (bf16[200,128]{1,0:T(8,128)(2,1)S(1)}, bf16[200,128]{1,0:T(8,128)(2,1)S(1)}, u32[]{:S(2)}, u32[]{:S(2)}) collective-permute-start(bf16[200,128]{1,0:T(8,128)(2,1)S(1)} %select_convert_fusion.2), channel_id=1, source_target_pairs={{0,8},{2,10},{4,12},{6,14},{8,0},{10,2},{12,4},{14,6},{1,9},{3,11}... | collective-permute-start | bytes 153608 | tf_op jit(solution)/shard_map/ppermute | solution.py:484
  101.3 1.3 %collective-permute-start.10 = (f32[104,128]{1,0:T(8,128)S(1)}, f32[104,128]{1,0:T(8,128)S(1)}, u32[]{:S(2)}, u32[]{:S(2)}) collective-permute-start(f32[104,128]{1,0:T(8,128)S(1)} %select_maximum_fusion), channel_id=1, source_target_pairs={{0,1},{1,0},{2,3},{3,2},{4,5},{5,4},{6,7},{7,6},{8,9},{9,8},{10,11... | collective-permute-start | bytes 159752 | tf_op jit(solution)/shard_map/ppermute | solution.py:484
  102.6 6.7 %collective-permute-start.11 = (bf16[304,128]{1,0:T(8,128)(2,1)S(1)}, bf16[304,128]{1,0:T(8,128)(2,1)S(1)}, u32[]{:S(2)}, u32[]{:S(2)}) collective-permute-start(bf16[304,128]{1,0:T(8,128)(2,1)S(1)} %pad_maximum_fusion.6), channel_id=1, source_target_pairs={{0,8},{2,10},{4,12},{6,14},{8,0},{10,2},{12,4},{14,6},{1,9},{3,11}... | collective-permute-start | bytes 233480 | tf_op jit(solution)/shard_map/ppermute | solution.py:484
  109.4 7.5 %collective-permute-start.14 = (bf16[504,128]{1,0:T(8,128)(2,1)S(1)}, bf16[504,128]{1,0:T(8,128)(2,1)S(1)}, u32[]{:S(2)}, u32[]{:S(2)}) collective-permute-start(bf16[504,128]{1,0:T(8,128)(2,1)S(1)} %pad_maximum_fusion.3), channel_id=1, source_target_pairs={{0,4},{2,6},{4,0},{6,2},{8,12},{10,14},{12,8},{14,10},{1,5},{3,7},... | collective-permute-start | bytes 387080 | tf_op jit(solution)/shard_map/ppermute | solution.py:484
  116.9 6.5 %collective-permute-start.15 = (bf16[904,128]{1,0:T(8,128)(2,1)S(1)}, bf16[904,128]{1,0:T(8,128)(2,1)S(1)}, u32[]{:S(2)}, u32[]{:S(2)}) collective-permute-start(bf16[904,128]{1,0:T(8,128)(2,1)S(1)} %pad_maximum_fusion.1), channel_id=1, source_target_pairs={{0,2},{2,0},{4,6},{6,4},{8,10},{10,8},{12,14},{14,12},{1,3},{3,1},... | collective-permute-start | bytes 694280 | tf_op jit(solution)/shard_map/ppermute | solution.py:484
  123.6 3.3 %collective-permute-start.16 = (bf16[1600,128]{1,0:T(8,128)(2,1)S(1)}, bf16[1600,128]{1,0:T(8,128)(2,1)S(1)}, u32[]{:S(2)}, u32[]{:S(2)}) collective-permute-start(bf16[1600,128]{1,0:T(8,128)(2,1)S(1)} %pad_maximum_fusion), channel_id=1, source_target_pairs={{0,1},{1,0},{2,3},{3,2},{4,5},{5,4},{6,7},{7,6},{8,9},{9,8},{10,11... | collective-permute-start | bytes 1228808 | tf_op jit(solution)/shard_map/ppermute | solution.py:484
  (6 other events, 4.1 us)

commit v4 on v3

--- a/solution.py
+++ b/solution.py
@@ -1,5 +1,3 @@
-import functools
-
 import jax
 import jax.numpy as jnp
 from jax import lax
@@ -14,6 +12,7 @@
 HALO = 8
 VMEM_LIMIT = 58 << 20
 CHUNKS = 5
+MAIN = 1
 WIDE = 8
 SMALL = 64
 PITCH = 40
@@ -205,8 +204,8 @@
         rh[pl.ds(t * channels, channels), :] = jnp.zeros((channels, lanes), F32)
 
 
-def channel_stack(c, first, x_ref, h_ref, rb, rh):
-    at = pl.ds(first + c, HALO, stride=rb.shape[0] // HALO)
+def channel_stack(c, x_ref, h_ref, rb, rh):
+    at = pl.ds(c, HALO, stride=rb.shape[0] // HALO)
     own = jnp.concatenate([x_ref[c].astype(F32), rb[at, :]], axis=0)
     edge = jnp.concatenate([h_ref[c].astype(F32), rh[at, :]], axis=0)
     return shift_stack(own, edge)
@@ -277,16 +276,16 @@
 
     @pl.when(step == 0)
     def _():
-        stage_halo(north_ref[0], lat_ref, fold_ref, rb, rh)
         rows_s[...] = tap_rows(taps_ref[...], rows)
 
-    @pl.when(step < CHUNKS)
+    @pl.when(step < MAIN)
     def _():
         first = step * chunk
+        stage_halo(north_ref[0], lat_ref, fold_ref, rb, rh)
 
         def conv_step(k, carry):
             c = first + k
-            stack = channel_stack(k, first, x_ref, h_ref, rb, rh)
+            stack = channel_stack(k, x_ref, h_ref, rb, rh)
             high, low = split(tap_matrix(rows_s[pl.ds(c, 1), :], rows))
             both = dot(jnp.concatenate([high, low], axis=0), stack, 1, 0)
             conv[pl.ds(c, rows, stride=channels), :] = both[:rows] + both[rows:]
@@ -298,16 +297,16 @@
 
         lax.fori_loop(0, chunk, conv_step, 0, unroll=20)
 
-    @pl.when(step == CHUNKS)
+    @pl.when(step == MAIN)
     def _():
         cell_work(
             north_ref, wet_ref, we_ref, wr_ref, wrt_ref, keep_ref, send_ref, sums_ref,
             conv, cots, gs, gr, ms, act_s, hg_s, exp_ref, red_ref, gain_s, scale_s, rows,
         )
 
-    @pl.when(step > CHUNKS)
+    @pl.when(step > MAIN)
     def _():
-        first = (step - CHUNKS - 1) * chunk
+        first = (step - MAIN - 1) * chunk
 
         def out_step(k, carry):
             at = pl.multiple_of((first + k) * PITCH, 8)
@@ -357,7 +356,7 @@
         normed = (normalized * gain).astype(BF16)
         branch = group(cots, i)
         mixed_grad = (scale * branch).astype(BF16)
-        part = 160
+        part = hiddens
         for f in range(0, hiddens, part):
             hidden = dot(wet_ref[f : f + part, :], normed, 1, 0)
             act_grad = dot(wr_ref[f : f + part, :], mixed_grad, 1, 0)
@@ -392,16 +391,12 @@
         ref[hiddens:, :] = cat([value[:, lanes:], blank]).astype(ref.dtype)
 
 
-def tap_kernel(start, north_ref, x_ref, h_ref, lat_ref, fold_ref, back_ref, sums_ref, small_ref, rb, rh, rows_s):
+def tap_kernel(north_ref, x_ref, h_ref, lat_ref, fold_ref, back_ref, sums_ref, small_ref, rb, rh, rows_s):
     chunk, rows, lanes = x_ref.shape
-    first = (pl.program_id(0) + start) * chunk
-
-    @pl.when(pl.program_id(0) == 0)
-    def _():
-        stage_halo(north_ref[0], lat_ref, fold_ref, rb, rh)
+    stage_halo(north_ref[0], lat_ref, fold_ref, rb, rh)
 
     def step(k, carry):
-        stack = channel_stack(k, first, x_ref, h_ref, rb, rh)
+        stack = channel_stack(k, x_ref, h_ref, rb, rh)
         rows_s[pl.ds(k, 1), :] = tap_sums(dot(back_ref[k], stack, 1, 1), rows)
         return carry
 
@@ -419,19 +414,15 @@
     small_ref[...] = taps
 
 
-def adjoint_kernel(start, north_ref, g_ref, h_ref, lat_ref, fold_ref, taps_ref, cot_ref, *refs):
+def adjoint_kernel(north_ref, g_ref, h_ref, lat_ref, fold_ref, taps_ref, cot_ref, *refs):
     out_ref, rb, rh, rows_s = refs[-4:]
     chunk, rows, lanes = g_ref.shape
-    first = (pl.program_id(0) + start) * chunk
-
-    @pl.when(pl.program_id(0) == 0)
-    def _():
-        stage_halo(north_ref[0], lat_ref, fold_ref, rb, rh)
-        rows_s[...] = tap_rows(taps_ref[...], rows, north_ref[0])
+    stage_halo(north_ref[0], lat_ref, fold_ref, rb, rh)
+    rows_s[...] = tap_rows(taps_ref[...], rows, north_ref[0])
 
     def step(k, carry):
-        stack = channel_stack(k, first, g_ref, h_ref, rb, rh)
-        matrix = tap_matrix(rows_s[pl.ds(first + k, 1), :], rows).astype(BF16)
+        stack = channel_stack(k, g_ref, h_ref, rb, rh)
+        matrix = tap_matrix(rows_s[pl.ds(k, 1), :], rows).astype(BF16)
         out_ref[k] = (cot_ref[k].astype(F32) + dot(matrix, stack, 1, 0)).astype(BF16)
         return carry
 
@@ -502,7 +493,7 @@
     north = is_north.astype(jnp.int32).reshape(1)
     edge = shape((HALO, channels * rows), BF16)
     field = shape(ocean_state.shape, BF16)
-    rowbuf = pltpu.VMEM((HALO * channels, lanes), F32)
+    rowbuf = pltpu.VMEM((HALO * (channels // CHUNKS), lanes), F32)
     cellbuf = pltpu.VMEM((channels * rows, lanes), F32)
     pitchbuf = pltpu.VMEM((channels * PITCH, lanes), F32)
     tapbuf = pltpu.VMEM((channels, width), F32)
@@ -519,22 +510,27 @@
     chunk = channels // CHUNKS
     whole = vmem()
 
-    def block(index):
-        return pl.BlockSpec((chunk, rows, lanes), lambda i: (index(i), 0, 0))
+    big = channels // MAIN
+
+    def block(index, size=chunk):
+        return pl.BlockSpec((size, rows, lanes), lambda i: (index(i), 0, 0))
 
     def into(i):
-        return jnp.minimum(i, CHUNKS - 1)
+        return jnp.minimum(i, MAIN - 1)
 
     def back_out(i):
-        return jnp.maximum(i - CHUNKS - 1, 0)
+        return jnp.maximum(i - MAIN - 1, 0)
 
     def both_ways(i):
-        return jnp.where(i <= CHUNKS, into(i), back_out(i))
-
-    edge_block = pl.BlockSpec((HALO, chunk * rows), lambda i: (0, back_out(i)))
+        return jnp.where(i <= MAIN, into(i), back_out(i))
+
+    def halo_block(index, size=chunk):
+        return pl.BlockSpec((REACH, size, 2 * lanes), lambda i: (0, index(i), 0))
+
+    edge_block = pl.BlockSpec((HALO, big * rows), lambda i: (0, back_out(i)))
     block_out, conv_grad, back_grad, g_low, g_high, keep, send, sums = grid_call(
         main_kernel,
-        2 * CHUNKS + 1,
+        2 * MAIN + 1,
         (
             field,
             field,
@@ -545,9 +541,10 @@
             shape((2 * hiddens, lanes), BF16),
             shape((2, channels, lanes), F32),
         ),
-        [smem()] * 3 + [block(both_ways), block(into)] + [whole] * 3 + [block(into)] + [whole] * 5,
-        [block(back_out)] * 3 + [edge_block] * 2 + [whole] * 3,
-        [cellbuf] * 2 + [pitchbuf] * 3 + [rowbuf] * 2 + [hidbuf] * 2 + [gradbuf] * 2 + [tapbuf] + [lanebuf] * 2,
+        [smem()] * 3 + [block(both_ways, big), block(into, big)] + [halo_block(into, big)] * 2
+        + [whole, block(into, big)] + [whole] * 5,
+        [block(back_out, big)] * 3 + [edge_block] * 2 + [whole] * 3,
+        [cellbuf] * 2 + [pitchbuf] * 3 + [pltpu.VMEM((HALO * big, lanes), F32)] * 2 + [hidbuf] * 2 + [gradbuf] * 2 + [tapbuf] + [lanebuf] * 2,
         cost(40),
     )(
         north, norm_gain, layer_scale, ocean_state, halo, lat_rows, fold_rows, kernel, cotangent, land_mask,
@@ -555,28 +552,29 @@
     )
 
     def adjoint_part(start, count, grad, lane_halo, previous):
-        here = block(lambda i: i + start)
+        here, rows_in = block(lambda i: i + start), halo_block(lambda i: i + start)
         extra = () if previous is None else (previous,)
         return grid_call(
-            functools.partial(adjoint_kernel, start),
+            adjoint_kernel,
             count,
             field,
-            [smem(), here, here] + [whole] * 3 + [here]
+            [smem(), here, here, rows_in, rows_in]
+            + [pl.BlockSpec((chunk, KS * KS), lambda i: (i + start, 0)), here]
             + [pl.BlockSpec(memory_space=pl.ANY)] * len(extra),
             here,
-            [rowbuf] * 2 + [tapbuf],
+            [rowbuf] * 2 + [pltpu.VMEM((chunk, width), F32)],
             cost(2 * count),
             {7: 0} if extra else None,
         )(north, grad, lane_halo, g_lat, g_fold, kernel, cotangent, *extra)
 
     g_east, g_west = lon_edges(g_low, g_high)
     def taps_part(start, count, back):
-        here = block(lambda i: i + start)
+        here, rows_in = block(lambda i: i + start), halo_block(lambda i: i + start)
         return grid_call(
-            functools.partial(tap_kernel, start),
+            tap_kernel,
             count,
             shape((count * chunk, SMALL), F32),
-            [smem(), here, here] + [whole] * 2
+            [smem(), here, here, rows_in, rows_in]
             + [here, pl.BlockSpec((2, chunk, lanes), lambda i: (0, i + start, 0))],
             pl.BlockSpec((chunk, SMALL), lambda i: (i, 0)),
             [rowbuf] * 2 + [pltpu.VMEM((chunk, width), F32)],

time: 130 us -> 128 us (0.985)
  Pallas kernels: 74.6 us -> 72.1 us
    pallas_call x6, Pallas kernels: 64.2 us -> 61.7 us  [the longest x1 33.3 us: on_device(): grid_call(main_kernel, 2 * MAIN + 1, (field, field, field, edge, edge, sh...]
  transfers between devices with their start and end apart: 17 -> 17, of which waited for: 7 -> 9; matrix products, arithmetic and copies ran while one was open for 5% -> 5% of each run, Pallas kernels for 26% -> 25%
where the time goes in v4:
time: 128 us
  Pallas kernels  72.1 us (56%)
  starting transfers between devices  22.9 us (18%)
  waiting for transfers between devices  18.2 us (14%)
  local copies, waits for them, and re-layouts  9.83 us (8%)
  other arithmetic  3.62 us (3%)
    pallas_call x1, Pallas kernels, on_device(): grid_call(main_kernel, 2 * MAIN + 1, (field, field, field, edge, edge, sh...  33.3 us
    pallas_call x2, Pallas kernels, taps_part(): grid_call(tap_kernel, count, shape((count * chunk, SMALL), F32), [smem(),...  15.2 us
    pallas_call x3, Pallas kernels, adjoint_part(): grid_call(adjoint_kernel, count, field, [smem(), here, here, rows_in, row...  13.2 us
    unnamed x30, local copies, waits for them, and re-layouts  9.69 us
    pallas_call x2, Pallas kernels, halo_rows(): call(unpack_kernel, (shape(field.shape, BF16), msg, msg), scratch=[pltpu....  7.74 us
    ppermute x9, starting transfers between devices, partner(): lax.ppermute(value, axis, [(i, i ^ 1 << b) for i in range(lax.axis_size(a...  6.99 us
    ppermute x2, starting transfers between devices, halo_rows(): lax.ppermute(fold_msg, ('lon', 'lat'), [(i * m + m - 1, (n - 1 - i) * m +...  6.23 us
    ppermute x2, waiting for transfers between devices, halo_rows(): lax.ppermute(fold_msg, ('lon', 'lat'), [(i * m + m - 1, (n - 1 - i) * m +...  5.94 us
  transfers between devices with their start and end apart: 17, of which 9 were waited for; matrix products, arithmetic and copies ran while one was open for 5% of the time, Pallas kernels for 25%

profile of v4, /device:TPU:1, one launch (start us, length us, event | category | flops | bytes accessed | tf_op | source)
XLA Modules:
  0.0 127.7 jit_solution(3684559311662553610)
XLA Ops:
  0.6 2.7 %shard_map.135 = (bf16[8,6400]{1,0:T(8,128)(2,1)}, bf16[8,6400]{1,0:T(8,128)(2,1)}) custom-call(bf16[6400,128]{1,0:T(8,128)(2,1)} %bitcast.8), custom_call_target="tpu_custom_call" | custom-call | flops 2000000000 | bytes 6000000 | tf_op jit(solution)/shard_map/pallas_call | solution.py:504
  3.3 5.1 %collective-permute-start = (bf16[8,6400]{1,0:T(8,128)(2,1)}, bf16[8,6400]{1,0:T(8,128)(2,1)S(1)}, u32[]{:S(2)}, u32[]{:S(2)}) collective-permute-start(bf16[8,6400]{1,0:T(8,128)(2,1)} %get-tuple-element.51), channel_id=1, source_target_pairs={{2,0},{4,2},{6,4},{8,6},{10,8},{12,10},{14,12},{0,14},{3,1},{5,3},... | collective-permute-start | bytes 307208 | tf_op jit(solution)/shard_map/ppermute | solution.py:434
  8.4 2.0 %collective-permute-done.east_ref = bf16[8,6400]{1,0:T(8,128)(2,1)S(1)} collective-permute-done((bf16[8,6400]{1,0:T(8,128)(2,1)}, bf16[8,6400]{1,0:T(8,128)(2,1)S(1)}, u32[]{:S(2)}, u32[]{:S(2)}) %collective-permute-start) | collective-permute-done | bytes 102432 | tf_op jit(solution)/shard_map/ppermute | solution.py:434
  10.4 4.4 %collective-permute-done.1.west_ref = bf16[8,6400]{1,0:T(8,128)(2,1)S(1)} collective-permute-done((bf16[8,6400]{1,0:T(8,128)(2,1)}, bf16[8,6400]{1,0:T(8,128)(2,1)S(1)}, u32[]{:S(2)}, u32[]{:S(2)}) %collective-permute-start.1) | collective-permute-done | bytes 102432 | tf_op jit(solution)/shard_map/ppermute | solution.py:435
  15.5 3.9 %shard_map.136 = (bf16[200,32,128]{2,1,0:T(8,128)(2,1)}, bf16[3,200,256]{2,1,0:T(8,128)(2,1)}, bf16[3,200,256]{2,1,0:T(8,128)(2,1)}) custom-call(s32[1]{0:T(128)} %bitcast.north_ref, bf16[200,32,128]{2,1,0:T(8,128)(2,1)} %x_ref.7, bf16[8,6400]{1,0:T(8,128)(2,1)} %copy-done.10, bf16[8,6400]{1,0:T(8,128)(2,1)} %copy-done.11), custom_call_target="tpu_custom_call" | custom-call | flops 3000000000 | bytes 9000000 | tf_op jit(solution)/shard_map/pallas_call | solution.py:443
  19.4 2.1 %collective-permute-start.2 = (bf16[3,200,256]{2,1,0:T(8,128)(2,1)}, bf16[3,200,256]{2,1,0:T(8,128)(2,1)S(1)}, u32[]{:S(2)}, u32[]{:S(2)}) collective-permute-start(bf16[3,200,256]{2,1,0:T(8,128)(2,1)} %get-tuple-element.54), channel_id=1, source_target_pairs={{0,1},{1,0},{2,3},{3,2},{4,5},{5,4},{6,7},{7,6},{8,9},{9,8},{10,11... | collective-permute-start | bytes 921608 | tf_op jit(solution)/shard_map/ppermute | solution.py:454
  21.5 1.9 %collective-permute-start.3 = (bf16[3,200,256]{2,1,0:T(8,128)(2,1)}, bf16[3,200,256]{2,1,0:T(8,128)(2,1)S(1)}, u32[]{:S(2)}, u32[]{:S(2)}) collective-permute-start(bf16[3,200,256]{2,1,0:T(8,128)(2,1)} %get-tuple-element.55), channel_id=1, source_target_pairs={{1,15},{3,13},{5,11},{7,9},{9,7},{11,5},{13,3},{15,1},{17,31},{19,... | collective-permute-start | bytes 921608 | tf_op jit(solution)/shard_map/ppermute | solution.py:451
  26.0 5.9 %collective-permute-done.3.fold_ref = bf16[3,200,256]{2,1,0:T(8,128)(2,1)S(1)} collective-permute-done((bf16[3,200,256]{2,1,0:T(8,128)(2,1)}, bf16[3,200,256]{2,1,0:T(8,128)(2,1)S(1)}, u32[]{:S(2)}, u32[]{:S(2)}) %collective-permute-start.3) | collective-permute-done | bytes 307232 | tf_op jit(solution)/shard_map/ppermute | solution.py:451
  32.7 33.3 %shard_map.137 = (bf16[200,32,128]{2,1,0:T(8,128)(2,1)}, bf16[200,32,128]{2,1,0:T(8,128)(2,1)}, bf16[200,32,128]{2,1,0:T(8,128)(2,1)}, bf16[8,6400]{1,0:T(8,128)...) custom-call(s32[1]{0:T(128)} %bitcast.north_ref, ...), custom_call_target="tpu_custom_call" | custom-call | flops 40000000000 | bytes 120000000 | tf_op jit(solution)/shard_map/pallas_call | solution.py:531
  66.3 1.4 %collective-permute-start.8 = (bf16[8,6400]{1,0:T(8,128)(2,1)}, bf16[8,6400]{1,0:T(8,128)(2,1)S(1)}, u32[]{:S(2)}, u32[]{:S(2)}) collective-permute-start(bf16[8,6400]{1,0:T(8,128)(2,1)} %get-tuple-element.69), channel_id=1, source_target_pairs={{0,2},{2,4},{4,6},{6,8},{8,10},{10,12},{12,14},{14,0},{1,3},{3,5},... | collective-permute-start | bytes 307208 | tf_op jit(solution)/shard_map/ppermute | solution.py:435
  68.0 1.2 convert_add_fusion
  69.4 8.8 %shard_map.138 = f32[120,64]{1,0:T(8,128)} custom-call(s32[1]{0:T(128)} %bitcast.north_ref, bf16[200,32,128]{2,1,0:T(8,128)(2,1)} %x_ref.7, bf16[200,32,128]{2,1,0:T(8,128)(2,1)} %get-tuple-element.53.h_ref, bf16[3,200,256]{2,1,0:T(8,128)(2,1)} %copy-done.6, bf16[3,200,256]{2,1,0:T(8,128)(2,1)} %copy-done.7, ...), custom_call_target="tpu_custom_call" | custom-call | flops 8999999488 | bytes 27000000 | tf_op jit(solution)/shard_map/pallas_call | solution.py:573
  79.8 3.8 %shard_map.139 = (bf16[200,32,128]{2,1,0:T(8,128)(2,1)}, bf16[3,200,256]{2,1,0:T(8,128)(2,1)}, bf16[3,200,256]{2,1,0:T(8,128)(2,1)}) custom-call(s32[1]{0:T(128)} %bitcast.north_ref, bf16[200,32,128]{2,1,0:T(8,128)(2,1)} %get-tuple-element.91.x_ref.g_ref, bf16[8,6400]{1,0:T(8,128)(2,1)} %copy-done.8, bf16[8,6400]{1,0:T(8,128)(2,1)} %copy-done.9), custom_call_target="tpu_custom_call" | custom-call | flops 3000000000 | bytes 9000000 | tf_op jit(solution)/shard_map/pallas_call | solution.py:443
  84.6 4.3 %collective-permute-start.13 = (bf16[3,200,256]{2,1,0:T(8,128)(2,1)}, bf16[3,200,256]{2,1,0:T(8,128)(2,1)S(1)}, u32[]{:S(2)}, u32[]{:S(2)}) collective-permute-start(bf16[3,200,256]{2,1,0:T(8,128)(2,1)} %get-tuple-element.84), channel_id=1, source_target_pairs={{1,15},{3,13},{5,11},{7,9},{9,7},{11,5},{13,3},{15,1},{17,31},{19,... | collective-permute-start | bytes 921608 | tf_op jit(solution)/shard_map/ppermute | solution.py:451
  89.0 1.6 %collective-permute-start.9 = (bf16[200,128]{1,0:T(8,128)(2,1)S(1)}, bf16[200,128]{1,0:T(8,128)(2,1)S(1)}, u32[]{:S(2)}, u32[]{:S(2)}) collective-permute-start(bf16[200,128]{1,0:T(8,128)(2,1)S(1)} %select_convert_fusion.2), channel_id=1, source_target_pairs={{0,8},{2,10},{4,12},{6,14},{8,0},{10,2},{12,4},{14,6},{1,9},{3,11}... | collective-permute-start | bytes 153608 | tf_op jit(solution)/shard_map/ppermute | solution.py:475
  90.6 6.4 %shard_map.140 = f32[80,64]{1,0:T(8,128)} custom-call(s32[1]{0:T(128)} %bitcast.north_ref, bf16[200,32,128]{2,1,0:T(8,128)(2,1)} %x_ref.7, bf16[200,32,128]{2,1,0:T(8,128)(2,1)} %get-tuple-element.53.h_ref, bf16[3,200,256]{2,1,0:T(8,128)(2,1)} %copy-done.6, bf16[3,200,256]{2,1,0:T(8,128)(2,1)} %copy-done.7, ...), custom_call_target="tpu_custom_call" | custom-call | flops 6000000000 | bytes 18000000 | tf_op jit(solution)/shard_map/pallas_call | solution.py:573
  97.1 2.0 %collective-permute-done.9 = bf16[200,128]{1,0:T(8,128)(2,1)S(1)} collective-permute-done((bf16[200,128]{1,0:T(8,128)(2,1)S(1)}, bf16[200,128]{1,0:T(8,128)(2,1)S(1)}, u32[]{:S(2)}, u32[]{:S(2)}) %collective-permute-start.9) | collective-permute-done | bytes 51232 | tf_op jit(solution)/shard_map/ppermute | solution.py:475
  102.8 4.9 %shard_map.141.refs_0_ = bf16[200,32,128]{2,1,0:T(8,128)(2,1)} custom-call(s32[1]{0:T(128)} %bitcast.north_ref, bf16[200,32,128]{2,1,0:T(8,128)(2,1)} %get-tuple-element.91.x_ref.g_ref, bf16[200,32,128]{2,1,0:T(8,128)(2,1)} %get-tuple-element.82.h_ref, bf16[3,200,256]{2,1,0:T(8,128)(2,1)} %copy-done.2, bf16[3,200,256]{2,1,0:T(8,128)(2,1)} %copy-done.3, ...), custom_call_target="tpu_custom_call" | custom-call | flops 4000000000 | bytes 12000000 | tf_op jit(solution)/shard_map/pallas_call | solution.py:557
  107.9 2.2 %collective-permute-start.14 = (bf16[504,128]{1,0:T(8,128)(2,1)S(1)}, bf16[504,128]{1,0:T(8,128)(2,1)S(1)}, u32[]{:S(2)}, u32[]{:S(2)}) collective-permute-start(bf16[504,128]{1,0:T(8,128)(2,1)S(1)} %pad_maximum_fusion.3), channel_id=1, source_target_pairs={{0,4},{2,6},{4,0},{6,2},{8,12},{10,14},{12,8},{14,10},{1,5},{3,7},... | collective-permute-start | bytes 387080 | tf_op jit(solution)/shard_map/ppermute | solution.py:475
  110.1 4.9 %shard_map.142.refs_0_ = bf16[200,32,128]{2,1,0:T(8,128)(2,1)} custom-call(s32[1]{0:T(128)} %bitcast.north_ref, bf16[200,32,128]{2,1,0:T(8,128)(2,1)} %get-tuple-element.91.x_ref.g_ref, bf16[200,32,128]{2,1,0:T(8,128)(2,1)} %get-tuple-element.82.h_ref, bf16[3,200,256]{2,1,0:T(8,128)(2,1)} %copy-done.2, ...), custom_call_target="tpu_custom_call", output_to_operand_aliasing={{}: (7, {})} | custom-call | flops 4000000000 | bytes 12000000 | tf_op jit(solution)/shard_map/pallas_call | solution.py:557
  115.0 1.2 collective-permute-start.15
  116.3 3.4 %shard_map.143 = bf16[200,32,128]{2,1,0:T(8,128)(2,1)} custom-call(s32[1]{0:T(128)} %bitcast.north_ref, bf16[200,32,128]{2,1,0:T(8,128)(2,1)} %get-tuple-element.91.x_ref.g_ref, bf16[200,32,128]{2,1,0:T(8,128)(2,1)} %get-tuple-element.82.h_ref, bf16[3,200,256]{2,1,0:T(8,128)(2,1)} %copy-done.2, ...), custom_call_target="tpu_custom_call", output_to_operand_aliasing={{}: (7, {})} | custom-call | flops 2000000000 | bytes 6000000 | tf_op jit(solution)/shard_map/pallas_call | solution.py:557
  119.7 1.9 %collective-permute-done.15 = bf16[904,128]{1,0:T(8,128)(2,1)S(1)} collective-permute-done((bf16[904,128]{1,0:T(8,128)(2,1)S(1)}, bf16[904,128]{1,0:T(8,128)(2,1)S(1)}, u32[]{:S(2)}, u32[]{:S(2)}) %collective-permute-start.15) | collective-permute-done | bytes 231456 | tf_op jit(solution)/shard_map/ppermute | solution.py:475
  121.7 1.7 %collective-permute-start.16 = (bf16[1600,128]{1,0:T(8,128)(2,1)S(1)}, bf16[1600,128]{1,0:T(8,128)(2,1)S(1)}, u32[]{:S(2)}, u32[]{:S(2)}) collective-permute-start(bf16[1600,128]{1,0:T(8,128)(2,1)S(1)} %pad_maximum_fusion), channel_id=1, source_target_pairs={{0,1},{1,0},{2,3},{3,2},{4,5},{5,4},{6,7},{7,6},{8,9},{9,8},{10,11... | collective-permute-start | bytes 1228808 | tf_op jit(solution)/shard_map/ppermute | solution.py:475
  (80 shorter events, 15.7 us)
Async XLA Ops:
  3.3 7.1 %collective-permute-start = (bf16[8,6400]{1,0:T(8,128)(2,1)}, bf16[8,6400]{1,0:T(8,128)(2,1)S(1)}, u32[]{:S(2)}, u32[]{:S(2)}) collective-permute-start(bf16[8,6400]{1,0:T(8,128)(2,1)} %get-tuple-element.51), channel_id=1, source_target_pairs={{2,0},{4,2},{6,4},{8,6},{10,8},{12,10},{14,12},{0,14},{3,1},{5,3},... | collective-permute-start | bytes 307208 | tf_op jit(solution)/shard_map/ppermute | solution.py:434
  8.4 6.4 %collective-permute-start.1 = (bf16[8,6400]{1,0:T(8,128)(2,1)}, bf16[8,6400]{1,0:T(8,128)(2,1)S(1)}, u32[]{:S(2)}, u32[]{:S(2)}) collective-permute-start(bf16[8,6400]{1,0:T(8,128)(2,1)} %get-tuple-element.52), channel_id=1, source_target_pairs={{0,2},{2,4},{4,6},{6,8},{8,10},{10,12},{12,14},{14,0},{1,3},{3,5},... | collective-permute-start | bytes 307208 | tf_op jit(solution)/shard_map/ppermute | solution.py:435
  10.4 4.4 %copy-start.10 = (bf16[8,6400]{1,0:T(8,128)(2,1)}, bf16[8,6400]{1,0:T(8,128)(2,1)S(1)}, u32[]{:S(2)}) copy-start(bf16[8,6400]{1,0:T(8,128)(2,1)S(1)} %collective-permute-done.east_ref) | copy-start | bytes 307204
  15.5 7.9 %copy-start.5 = (f32[200,49]{0,1:T(8,128)S(1)}, f32[200,49]{0,1:T(8,128)}, u32[]{:S(2)}) copy-start(f32[200,49]{0,1:T(8,128)} %param.10) | copy-start | bytes 117604
  15.5 8.7 %copy-start = (bf16[200,800]{1,0:T(8,128)(2,1)S(1)}, bf16[200,800]{1,0:T(8,128)(2,1)}, u32[]{:S(2)}) copy-start(bf16[200,800]{1,0:T(8,128)(2,1)} %we_ref.1) | copy-start | bytes 960004
  15.5 9.6 %copy-start.1 = (bf16[800,200]{0,1:T(8,128)(2,1)S(1)}, bf16[800,200]{0,1:T(8,128)(2,1)}, u32[]{:S(2)}) copy-start(bf16[800,200]{0,1:T(8,128)(2,1)} %param.13) | copy-start | bytes 960004
  19.4 6.7 %collective-permute-start.2 = (bf16[3,200,256]{2,1,0:T(8,128)(2,1)}, bf16[3,200,256]{2,1,0:T(8,128)(2,1)S(1)}, u32[]{:S(2)}, u32[]{:S(2)}) collective-permute-start(bf16[3,200,256]{2,1,0:T(8,128)(2,1)} %get-tuple-element.54), channel_id=1, source_target_pairs={{0,1},{1,0},{2,3},{3,2},{4,5},{5,4},{6,7},{7,6},{8,9},{9,8},{10,11... | collective-permute-start | bytes 921608 | tf_op jit(solution)/shard_map/ppermute | solution.py:454
  21.5 10.5 %collective-permute-start.3 = (bf16[3,200,256]{2,1,0:T(8,128)(2,1)}, bf16[3,200,256]{2,1,0:T(8,128)(2,1)S(1)}, u32[]{:S(2)}, u32[]{:S(2)}) collective-permute-start(bf16[3,200,256]{2,1,0:T(8,128)(2,1)} %get-tuple-element.55), channel_id=1, source_target_pairs={{1,15},{3,13},{5,11},{7,9},{9,7},{11,5},{13,3},{15,1},{17,31},{19,... | collective-permute-start | bytes 921608 | tf_op jit(solution)/shard_map/ppermute | solution.py:451
  26.0 5.9 %copy-start.6 = (bf16[3,200,256]{2,1,0:T(8,128)(2,1)}, bf16[3,200,256]{2,1,0:T(8,128)(2,1)S(1)}, u32[]{:S(2)}) copy-start(bf16[3,200,256]{2,1,0:T(8,128)(2,1)S(1)} %collective-permute-done.2.lat_ref) | copy-start | bytes 921604
  66.0 2.0 %collective-permute-start.4 = (bf16[1600,128]{1,0:T(8,128)(2,1)}, bf16[1600,128]{1,0:T(8,128)(2,1)S(1)}, u32[]{:S(2)}, u32[]{:S(2)}) collective-permute-start(bf16[1600,128]{1,0:T(8,128)(2,1)} %get-tuple-element.58), channel_id=1, source_target_pairs={{0,1},{1,0},{2,3},{3,2},{4,5},{5,4},{6,7},{7,6},{8,9},{9,8},{10,11... | collective-permute-start | bytes 1228808 | tf_op jit(solution)/shard_map/ppermute | solution.py:475
  66.1 12.4 %collective-permute-start.7 = (bf16[8,6400]{1,0:T(8,128)(2,1)}, bf16[8,6400]{1,0:T(8,128)(2,1)S(1)}, u32[]{:S(2)}, u32[]{:S(2)}) collective-permute-start(bf16[8,6400]{1,0:T(8,128)(2,1)} %get-tuple-element.68), channel_id=1, source_target_pairs={{2,0},{4,2},{6,4},{8,6},{10,8},{12,10},{14,12},{0,14},{3,1},{5,3},... | collective-permute-start | bytes 307208 | tf_op jit(solution)/shard_map/ppermute | solution.py:434
  66.3 12.3 %collective-permute-start.8 = (bf16[8,6400]{1,0:T(8,128)(2,1)}, bf16[8,6400]{1,0:T(8,128)(2,1)S(1)}, u32[]{:S(2)}, u32[]{:S(2)}) collective-permute-start(bf16[8,6400]{1,0:T(8,128)(2,1)} %get-tuple-element.69), channel_id=1, source_target_pairs={{0,2},{2,4},{4,6},{6,8},{8,10},{10,12},{12,14},{14,0},{1,3},{3,5},... | collective-permute-start | bytes 307208 | tf_op jit(solution)/shard_map/ppermute | solution.py:435
  69.3 9.1 %collective-permute-start.5 = (bf16[800,128]{1,0:T(8,128)(2,1)S(1)}, bf16[800,128]{1,0:T(8,128)(2,1)S(1)}, u32[]{:S(2)}, u32[]{:S(2)}) collective-permute-start(bf16[800,128]{1,0:T(8,128)(2,1)S(1)} %select_convert_fusion), channel_id=1, source_target_pairs={{0,2},{2,0},{4,6},{6,4},{8,10},{10,8},{12,14},{14,12},{1,3},{3,1},... | collective-permute-start | bytes 614408 | tf_op jit(solution)/shard_map/ppermute | solution.py:475
  78.5 10.5 %collective-permute-start.6 = (bf16[400,128]{1,0:T(8,128)(2,1)S(1)}, bf16[400,128]{1,0:T(8,128)(2,1)S(1)}, u32[]{:S(2)}, u32[]{:S(2)}) collective-permute-start(bf16[400,128]{1,0:T(8,128)(2,1)S(1)} %select_convert_fusion.1), channel_id=1, source_target_pairs={{0,4},{2,6},{4,0},{6,2},{8,12},{10,14},{12,8},{14,10},{1,5},{3,7},... | collective-permute-start | bytes 307208 | tf_op jit(solution)/shard_map/ppermute | solution.py:475
  83.7 17.7 %collective-permute-start.12 = (bf16[3,200,256]{2,1,0:T(8,128)(2,1)}, bf16[3,200,256]{2,1,0:T(8,128)(2,1)S(1)}, u32[]{:S(2)}, u32[]{:S(2)}) collective-permute-start(bf16[3,200,256]{2,1,0:T(8,128)(2,1)} %get-tuple-element.83), channel_id=1, source_target_pairs={{0,1},{1,0},{2,3},{3,2},{4,5},{5,4},{6,7},{7,6},{8,9},{9,8},{10,11... | collective-permute-start | bytes 921608 | tf_op jit(solution)/shard_map/ppermute | solution.py:454
  84.6 16.8 %collective-permute-start.13 = (bf16[3,200,256]{2,1,0:T(8,128)(2,1)}, bf16[3,200,256]{2,1,0:T(8,128)(2,1)S(1)}, u32[]{:S(2)}, u32[]{:S(2)}) collective-permute-start(bf16[3,200,256]{2,1,0:T(8,128)(2,1)} %get-tuple-element.84), channel_id=1, source_target_pairs={{1,15},{3,13},{5,11},{7,9},{9,7},{11,5},{13,3},{15,1},{17,31},{19,... | collective-permute-start | bytes 921608 | tf_op jit(solution)/shard_map/ppermute | solution.py:451
  89.0 10.1 %copy-start.4 = (f32[120,64]{1,0:T(8,128)S(1)}, f32[120,64]{1,0:T(8,128)}, u32[]{:S(2)}) copy-start(f32[120,64]{1,0:T(8,128)} %shard_map.138) | copy-start | bytes 92164
  89.0 10.1 %slice-start = ((f32[120,64]{1,0:T(8,128)}), f32[100,64]{1,0:T(8,128)S(1)}, s32[]{:S(2)}) async-start(f32[120,64]{1,0:T(8,128)} %shard_map.138), calls=%async_computation | async-start | bytes 106496 | tf_op jit(solution)/shard_map/slice | solution.py:598
  89.0 10.1 %collective-permute-start.9 = (bf16[200,128]{1,0:T(8,128)(2,1)S(1)}, bf16[200,128]{1,0:T(8,128)(2,1)S(1)}, u32[]{:S(2)}, u32[]{:S(2)}) collective-permute-start(bf16[200,128]{1,0:T(8,128)(2,1)S(1)} %select_convert_fusion.2), channel_id=1, source_target_pairs={{0,8},{2,10},{4,12},{6,14},{8,0},{10,2},{12,4},{14,6},{1,9},{3,11}... | collective-permute-start | bytes 153608 | tf_op jit(solution)/shard_map/ppermute | solution.py:475
  100.0 1.3 %collective-permute-start.10 = (f32[104,128]{1,0:T(8,128)S(1)}, f32[104,128]{1,0:T(8,128)S(1)}, u32[]{:S(2)}, u32[]{:S(2)}) collective-permute-start(f32[104,128]{1,0:T(8,128)S(1)} %select_maximum_fusion), channel_id=1, source_target_pairs={{0,1},{1,0},{2,3},{3,2},{4,5},{5,4},{6,7},{7,6},{8,9},{9,8},{10,11... | collective-permute-start | bytes 159752 | tf_op jit(solution)/shard_map/ppermute | solution.py:475
  101.3 6.5 %collective-permute-start.11 = (bf16[304,128]{1,0:T(8,128)(2,1)S(1)}, bf16[304,128]{1,0:T(8,128)(2,1)S(1)}, u32[]{:S(2)}, u32[]{:S(2)}) collective-permute-start(bf16[304,128]{1,0:T(8,128)(2,1)S(1)} %pad_maximum_fusion.6), channel_id=1, source_target_pairs={{0,8},{2,10},{4,12},{6,14},{8,0},{10,2},{12,4},{14,6},{1,9},{3,11}... | collective-permute-start | bytes 233480 | tf_op jit(solution)/shard_map/ppermute | solution.py:475
  107.9 7.0 %collective-permute-start.14 = (bf16[504,128]{1,0:T(8,128)(2,1)S(1)}, bf16[504,128]{1,0:T(8,128)(2,1)S(1)}, u32[]{:S(2)}, u32[]{:S(2)}) collective-permute-start(bf16[504,128]{1,0:T(8,128)(2,1)S(1)} %pad_maximum_fusion.3), channel_id=1, source_target_pairs={{0,4},{2,6},{4,0},{6,2},{8,12},{10,14},{12,8},{14,10},{1,5},{3,7},... | collective-permute-start | bytes 387080 | tf_op jit(solution)/shard_map/ppermute | solution.py:475
  115.0 6.5 %collective-permute-start.15 = (bf16[904,128]{1,0:T(8,128)(2,1)S(1)}, bf16[904,128]{1,0:T(8,128)(2,1)S(1)}, u32[]{:S(2)}, u32[]{:S(2)}) collective-permute-start(bf16[904,128]{1,0:T(8,128)(2,1)S(1)} %pad_maximum_fusion.1), channel_id=1, source_target_pairs={{0,2},{2,0},{4,6},{6,4},{8,10},{10,8},{12,14},{14,12},{1,3},{3,1},... | collective-permute-start | bytes 694280 | tf_op jit(solution)/shard_map/ppermute | solution.py:475
  121.7 3.3 %collective-permute-start.16 = (bf16[1600,128]{1,0:T(8,128)(2,1)S(1)}, bf16[1600,128]{1,0:T(8,128)(2,1)S(1)}, u32[]{:S(2)}, u32[]{:S(2)}) collective-permute-start(bf16[1600,128]{1,0:T(8,128)(2,1)S(1)} %pad_maximum_fusion), channel_id=1, source_target_pairs={{0,1},{1,0},{2,3},{3,2},{4,5},{5,4},{6,7},{7,6},{8,9},{9,8},{10,11... | collective-permute-start | bytes 1228808 | tf_op jit(solution)/shard_map/ppermute | solution.py:475
  (6 other events, 4.1 us)
